TPU v7x, 128 devices: a whole 4x4x4 slice. The times are simulated.
128 devices in a mesh: shot: 32 (over z, y, core), tm: 4 (over x).
Axes of the slice: x: 4, y: 4, z: 4, core: 2. Of those that a mesh axis runs over, the one named last changes fastest.
Arguments:
- signals: bfloat16 [256, 128, 2048], P('tm', 'shot'), may hold values from -0.59765625 to 0.59765625
- aperture: int32 [128, 128, 128], P('shot'), may hold values from 0 to 2047
- counts: int32 [128, 128], P('shot'), may hold values from 97 to 128, as said below
Outputs:
- prediction: float32 [256, 128, 128], P('tm', None, 'shot')
Inputs may be any that keep to these rules, and one draw needn't show every extreme that they name: Slots j >= counts[r, s] of aperture[r, s] are padding and do not enter the prediction. `counts`: in every draw some output trace uses all 128 slots.
All inputs are finite; a program needn't handle non-finite values.
Results may differ from a plain program's by a relative error of at most 0.0003.
Values may be sent and summed in bfloat16 or wider, within the bound.
No kernel may reach another device: no remote copies, remote signals or barrier semaphores. Data moves between devices by JAX's collectives and lax.ppermute only.
A program may use at most 128 MiB of HBM per device.

v0:
```python
import functools
import itertools

import jax
import jax.numpy as jnp
import numpy as np
from jax import lax
from jax.experimental import pallas as pl
from jax.experimental.pallas import tpu as pltpu
from jax.sharding import Mesh
from jax.sharding import PartitionSpec as P

AXES = ("z", "y", "c", "x")
SIZES = (4, 4, 2, 4)
LANES = 128
NT_DIMS = (((1,), (1,)), ((), ()))

ROUNDS = (
    (((0, 1), (0, 1), (0, 0)), ((0, 3), (0, 3), (0, 0)), ((1, 0), (1, 0), (0, 0))),
    (((3, 0), (3, 0), (0, 0)), ((1, 1), (0, 1), (1, 0)), ((1, 3), (0, 3), (1, 0)), ((2, 0), (1, 0), (1, 0))),
    (((0, 2), (0, 1), (0, 1)), ((3, 3), (0, 3), (3, 0)), ((2, 1), (1, 0), (1, 1)), ((3, 1), (3, 0), (0, 1))),
    (((2, 2), (0, 1), (2, 1)), ((1, 2), (1, 0), (0, 2)), ((2, 3), (0, 3), (2, 0)), ((3, 2), (3, 0), (0, 2))),
)
S_OFFSETS = ((0, 0),) + tuple(hop[0] for hops in ROUNDS for hop in hops)
R_OFFSETS = ((0, 0), (0, 1), (0, 3), (1, 0), (1, 1), (1, 3), (0, 2), (1, 2))


def from_offset(value, dz=0, dy=0, dc=0, dx=0):
    pairs = []
    for place in itertools.product(*(range(n) for n in SIZES)):
        source = tuple((p + d) % n for p, d, n in zip(place, (dz, dy, dc, dx), SIZES))
        pairs.append((int(np.ravel_multi_index(source, SIZES)), int(np.ravel_multi_index(place, SIZES))))
    return lax.ppermute(value, AXES, pairs)


def row_tables():
    list_rows, made_rows = [], []
    for z, y, c, x in itertools.product(*(range(n) for n in SIZES)):
        r_slot = [other * 4 + (x + dx) % 4 for other, dx in R_OFFSETS]
        s_slot = [(z + dz) % 4 * 4 + (y + dy) % 4 for dz, dy in S_OFFSETS]
        list_rows.append([r * 16 + s for r in r_slot for s in s_slot])
        made_rows.append(
            [
                r_slot.index((core ^ c) * 4 + r) * 16 + s_slot.index(s)
                for core in range(2)
                for r in range(4)
                for s in range(16)
            ]
        )
    return np.asarray(list_rows, np.int32), np.asarray(made_rows, np.int32)


def count_kernel(list_ref, out_ref):
    stations = list_ref[0]
    high = stations >> 7
    low = stations & (LANES - 1)
    chunk = lax.broadcasted_iota(jnp.int32, (16, LANES), 0)
    lane = lax.broadcasted_iota(jnp.int32, (LANES, LANES), 0)
    for s in range(stations.shape[0]):
        is_high = (high[s : s + 1, :] == chunk).astype(jnp.float32).astype(jnp.bfloat16)
        is_low = (low[s : s + 1, :] == lane).astype(jnp.float32).astype(jnp.bfloat16)
        out_ref[0, s] = lax.dot_general(is_high, is_low, NT_DIMS, preferred_element_type=jnp.float32)


def station_counts(lists):
    count_r, count_s, _ = lists.shape
    return pl.pallas_call(
        count_kernel,
        grid=(count_r,),
        in_specs=[pl.BlockSpec((1, count_s, LANES), lambda i: (i, 0, 0))],
        out_specs=pl.BlockSpec((1, count_s, 16, LANES), lambda i: (i, 0, 0, 0)),
        out_shape=jax.ShapeDtypeStruct((count_r, count_s, 16, LANES), jnp.float32),
        cost_estimate=pl.CostEstimate(flops=10**9, bytes_accessed=2**20, transcendentals=0),
        name="station_counts",
    )(lists)


def antidiagonals(outer):
    tau = lax.broadcasted_iota(jnp.int32, (LANES, LANES), 0)
    lane = lax.broadcasted_iota(jnp.int32, (LANES, LANES), 1)
    keep = lane >= tau
    near = pltpu.roll(outer[:LANES, :LANES], 0, 1, stride=1, stride_axis=0)
    far = outer[:LANES, LANES:] + outer[LANES:, :LANES]
    far = pltpu.roll(far, 0, 1, stride=1, stride_axis=0)
    first = jnp.sum(jnp.where(keep, near, 0.0), axis=0, keepdims=True)
    second = jnp.sum(jnp.where(keep, far, near), axis=0, keepdims=True)
    return first, second


def pair_kernel(r_parts, count_s, first_r, first_s, flag_ref, times_ref, *refs):
    count_arrays = 1 + max(array for array, _ in r_parts)
    r_refs = refs[:count_arrays]
    s_refs = refs[count_arrays : count_arrays + count_s]
    out_ref, scaled, outer, r_buf, sems = refs[count_arrays + count_s :]
    length, stations = s_refs[0].shape
    chunks = stations // LANES
    r = pl.program_id(0)
    slot = lax.rem(r, 2)

    def fetch(part):
        array, row = r_parts[part]
        source = r_refs[array] if row is None else r_refs[array].at[row]
        return pltpu.make_async_copy(source, r_buf.at[part % 2], sems.at[part % 2])

    @pl.when(r == 0)
    def _():
        fetch(0).start()

    for part in range(1, len(r_parts)):

        @pl.when(r == part - 1)
        def _():
            fetch(part).start()

    for s in range(count_s):
        for c in range(chunks):
            cols = slice(c * LANES, (c + 1) * LANES)
            times = jnp.broadcast_to(times_ref[0, s, c : c + 1, :], (16, LANES)).astype(jnp.bfloat16)
            times = jnp.concatenate([times] * (length // 16), axis=0)
            scaled[s * length : (s + 1) * length, cols] = s_refs[s][:, cols] * times
    pltpu.make_async_copy(r_buf.at[slot], r_buf.at[slot], sems.at[slot]).wait()
    outer[...] = lax.dot_general(scaled[...], r_buf[slot], NT_DIMS, preferred_element_type=jnp.float32)
    for s in range(count_s):
        rows = slice(s * length, (s + 1) * length)
        flag = flag_ref[first_r + r, first_s + s]

        @pl.when(flag != 0)
        def _():
            def one(pair, carry):
                @pl.when((flag >> pair) & 1 != 0)
                def _():
                    parts = []
                    for half in range(2):
                        cols = pl.ds(pl.multiple_of(pair * 2 * LANES + half * LANES, LANES), LANES)
                        times = jnp.broadcast_to(times_ref[0, s, pl.ds(pair * 2 + half, 1), :], (length, LANES))
                        whole = s_refs[s][:, cols].astype(jnp.float32) * times
                        parts.append((whole - scaled[rows, cols].astype(jnp.float32)).astype(jnp.bfloat16))
                    both = pl.ds(pl.multiple_of(pair * 2 * LANES, 2 * LANES), 2 * LANES)
                    outer[rows, :] += lax.dot_general(
                        jnp.concatenate(parts, axis=1),
                        r_buf[slot, :, both],
                        NT_DIMS,
                        preferred_element_type=jnp.float32,
                    )

                return carry

            lax.fori_loop(0, chunks // 2, one, 0)

        first, second = antidiagonals(outer[rows, :])
        out_ref[0, s, 0:1, :] = first
        out_ref[0, s, 1:2, :] = second


def predict(flags, times, r_arrays, s_shots, first_r, first_s):
    r_parts = []
    for number, array in enumerate(r_arrays):
        r_parts += [(number, row) for row in range(array.shape[0])] if array.ndim == 3 else [(number, None)]
    count_r, count_s = len(r_parts), len(s_shots)
    length, stations = s_shots[0].shape
    grid_spec = pltpu.PrefetchScalarGridSpec(
        num_scalar_prefetch=1,
        grid=(count_r,),
        in_specs=[
            pl.BlockSpec((1, count_s, 16, LANES), lambda i, f: (first_r + i, first_s // count_s, 0, 0)),
        ]
        + [pl.BlockSpec(memory_space=pl.ANY)] * len(r_arrays)
        + [pl.BlockSpec((length, stations), lambda i, f: (0, 0), pipeline_mode=pl.Buffered(1))] * count_s,
        out_specs=pl.BlockSpec((1, count_s, 2, LANES), lambda i, f: (i, 0, 0, 0)),
        scratch_shapes=[
            pltpu.VMEM((count_s * length, stations), jnp.bfloat16),
            pltpu.VMEM((count_s * length, length), jnp.float32),
            pltpu.VMEM((2, length, stations), jnp.bfloat16),
            pltpu.SemaphoreType.DMA((2,)),
        ],
    )
    return pl.pallas_call(
        functools.partial(pair_kernel, tuple(r_parts), count_s, first_r, first_s),
        grid_spec=grid_spec,
        out_shape=jax.ShapeDtypeStruct((count_r, count_s, 2, LANES), jnp.float32),
        compiler_params=pltpu.CompilerParams(vmem_limit_bytes=32 << 20),
        cost_estimate=pl.CostEstimate(
            flops=count_r * count_s * 2 * length * length * stations * 2,
            bytes_accessed=(count_r + count_s) * length * stations * 2,
            transcendentals=0,
        ),
        name="pairs",
    )(flags, times, *r_arrays, *s_shots)


def body(signals, aperture, counts):
    length_win, group, stations = signals.shape
    shots = aperture.shape[1]
    slots = aperture.shape[2]
    z, y, c, x = (lax.axis_index(name) for name in AXES)

    live = jnp.arange(slots, dtype=jnp.int32) < counts[:, :, None]
    lists = jnp.where(live, aperture, -1).reshape(group, 16, 2, 4, slots)
    lists = lax.dynamic_index_in_dim(lists, x, 3, keepdims=False)
    mine = lax.dynamic_index_in_dim(lists, c, 2, keepdims=False)
    theirs = from_offset(lax.dynamic_index_in_dim(lists, 1 - c, 2, keepdims=False), dc=1)

    native = jnp.transpose(signals, (1, 0, 2))
    windows = [lax.dynamic_index_in_dim(native, x, 0, keepdims=False)]
    for dx in (1, 2, 3):
        windows.append(from_offset(lax.dynamic_index_in_dim(native, (x - dx) % 4, 0, keepdims=False), dx=dx))
    windows = jnp.stack(windows + windows)
    own = lax.dynamic_slice_in_dim(windows, (4 - x) % 4, 4, 0).reshape(4 * length_win, stations)
    own, mine, theirs = lax.optimization_barrier((own, mine, theirs))

    held = {(0, 0): own}

    def travel(number):
        for offset, (dz, dy), forwarded in ROUNDS[number]:
            held[offset] = from_offset(held[forwarded], dz=dz, dy=dy)

    def meet(number, *others):
        names = [hop[0] for hop in ROUNDS[number]]
        values = lax.optimization_barrier([held[name] for name in names] + list(others))
        held.update(zip(names, values))
        return values[len(names) :]

    travel(0)
    right, left = meet(0, from_offset(own, dx=1), from_offset(own, dx=3))

    lists = jnp.stack([mine, theirs]).reshape(2 * group * 16, slots)
    list_rows, made_rows = row_tables()
    device = ((z * 4 + y) * 2 + c) * 4 + x
    rows = lax.dynamic_index_in_dim(jnp.asarray(list_rows), device, 0, keepdims=False)
    lists = jnp.take(lists, rows, axis=0).reshape(len(R_OFFSETS), 16, slots)
    times = station_counts(lists)
    whole = times.astype(jnp.int32).reshape(len(R_OFFSETS), 16, 8, 2 * LANES)
    odd = jnp.max((whole & (whole - 1) != 0).astype(jnp.int32), axis=3)
    flags = jnp.sum(odd << jnp.arange(8, dtype=jnp.int32), axis=2)

    def some(first_s, count=4):
        return [held[offset] for offset in S_OFFSETS[first_s : first_s + count]]

    near = jnp.stack([own, right, left])
    near_other = from_offset(near, dc=1)
    travel(1)
    right, near_other = lax.optimization_barrier((right, near_other))
    away = from_offset(right, dx=1)
    (near_other,) = meet(1, near_other)
    blocks = [predict(flags, times, [near, near_other], some(0), 0, 0)]
    travel(2)
    blocks.append(predict(flags, times, [near, near_other], some(4), 0, 4))
    (away,) = meet(2, away)
    away_other = from_offset(away, dc=1)
    travel(3)
    ends = [predict(flags, times, [away, away_other], some(first_s), 6, first_s) for first_s in (0, 4)]
    for first_s in (8, 12):
        both = predict(flags, times, [near, near_other, away, away_other], some(first_s), 0, first_s)
        blocks.append(both)
    head = jnp.concatenate([jnp.concatenate(blocks[:2], axis=1), jnp.concatenate(ends, axis=1)], axis=0)
    made = jnp.concatenate([head] + blocks[2:], axis=1).reshape(len(R_OFFSETS) * 16, 4 * length_win)

    rows = lax.dynamic_index_in_dim(jnp.asarray(made_rows), device, 0, keepdims=False)
    made = jnp.take(made, rows, axis=0).reshape(2, group, 16, 4, length_win)
    made = jnp.transpose(made, (0, 3, 4, 1, 2)).reshape(8, length_win, group, 16)
    made = lax.all_to_all(made, ("c", "x"), 0, 0, tiled=True)
    made = made.reshape(2, 4, length_win, group, 16)
    return jnp.transpose(made, (2, 4, 0, 1, 3)).reshape(length_win, shots, group)


def solution(mesh):
    fine = Mesh(np.asarray(mesh.devices).reshape(SIZES), AXES)
    shot = ("z", "y", "c")
    in_specs = (P("x", shot, None), P(shot, None, None), P(shot, None))
    return jax.shard_map(body, mesh=fine, in_specs=in_specs, out_specs=P("x", None, shot), check_vma=False)
```

profile of v0, /device:TPU:1, one launch (start us, length us, event | category | flops | bytes accessed | tf_op | source)
XLA Modules:
  0.0 221.1 jit_solution(2566105088318900016)
XLA Ops:
  0.0 5.0 %constant_dynamic-slice_fusion.3 = (bf16[64,1,2048]{2,1,0:T(2,128)(2,1)S(1)}, bf16[64,1,2048]{2,1,0:T(2,128)(2,1)S(1)}, bf16[64,1,2048]{2,1,0:T(2,128)(2,1)S(1)}, bf16[64,1,2048]{2,1,0:T(2,128)(2,1)S(1)}) fusion(bf16[64,4,2048]{2,1,0:T(4,128)(2,1)} %param.5, s32[]{:T(128)S(6)} %select_n.111, s32[]{:T(128)S(6)} %select_n.109, s32[]{:T(128)S(6)} %select_n.107, ...), kind=kLoop, calls=%fused_computation.38 | loop fusion | bytes 2097168 | tf_op jit(solution)/shard_map/dynamic-slice.3
  5.1 3.4 %collective-permute-start = (bf16[64,2048]{1,0:T(8,128)(2,1)S(1)}, bf16[64,2048]{1,0:T(8,128)(2,1)S(1)}, u32[]{:S(2)}, u32[]{:S(2)}) collective-permute-start(bf16[64,2048]{1,0:T(8,128)(2,1)S(1)} %bitcast.77), channel_id=1, source_target_pairs={{1,0},{2,1},{3,2},{0,3},{5,4},{6,5},{7,6},{4,7},{9,8},{10,9},{11,1... | collective-permute-start | bytes 786440 | tf_op jit(solution)/shard_map/ppermute | solution.py:33
  12.1 2.6 %collective-permute-done = bf16[64,2048]{1,0:T(8,128)(2,1)S(1)} collective-permute-done((bf16[64,2048]{1,0:T(8,128)(2,1)S(1)}, bf16[64,2048]{1,0:T(8,128)(2,1)S(1)}, u32[]{:S(2)}, u32[]{:S(2)}) %collective-permute-start) | collective-permute-done | bytes 262176 | tf_op jit(solution)/shard_map/ppermute | solution.py:33
  17.2 6.9 %collective-permute-done.2 = bf16[64,2048]{1,0:T(8,128)(2,1)S(1)} collective-permute-done((bf16[64,2048]{1,0:T(8,128)(2,1)S(1)}, bf16[64,2048]{1,0:T(8,128)(2,1)S(1)}, u32[]{:S(2)}, u32[]{:S(2)}) %collective-permute-start.2) | collective-permute-done | bytes 262176 | tf_op jit(solution)/shard_map/ppermute | solution.py:33
  24.5 2.8 %collective-permute-start.4 = (bf16[256,2048]{1,0:T(8,128)(2,1)S(1)}, bf16[256,2048]{1,0:T(8,128)(2,1)S(1)}, u32[]{:S(2)}, u32[]{:S(2)}) collective-permute-start(bf16[256,2048]{1,0:T(8,128)(2,1)S(1)} %bitcast.59), channel_id=1, source_target_pairs={{8,0},{9,1},{10,2},{11,3},{12,4},{13,5},{14,6},{15,7},{16,8},{17,9... | collective-permute-start | bytes 3145736 | tf_op jit(solution)/shard_map/ppermute | solution.py:33
  27.3 3.8 %collective-permute-start.6 = (bf16[256,2048]{1,0:T(8,128)(2,1)S(1)}, bf16[256,2048]{1,0:T(8,128)(2,1)}, u32[]{:S(2)}, u32[]{:S(2)}) collective-permute-start(bf16[256,2048]{1,0:T(8,128)(2,1)S(1)} %bitcast.61), channel_id=1, source_target_pairs={{32,0},{33,1},{34,2},{35,3},{36,4},{37,5},{38,6},{39,7},{40,8},{41... | collective-permute-start | bytes 3145736 | tf_op jit(solution)/shard_map/ppermute | solution.py:33
  32.5 16.8 %collective-permute-done.4.refs_3_ = bf16[256,2048]{1,0:T(8,128)(2,1)S(1)} collective-permute-done((bf16[256,2048]{1,0:T(8,128)(2,1)S(1)}, bf16[256,2048]{1,0:T(8,128)(2,1)S(1)}, u32[]{:S(2)}, u32[]{:S(2)}) %collective-permute-start.4) | collective-permute-done | bytes 1048608 | tf_op jit(solution)/shard_map/ppermute | solution.py:33
  49.3 3.1 %collective-permute-done.5.refs_4_ = bf16[256,2048]{1,0:T(8,128)(2,1)S(1)} collective-permute-done((bf16[256,2048]{1,0:T(8,128)(2,1)S(1)}, bf16[256,2048]{1,0:T(8,128)(2,1)S(1)}, u32[]{:S(2)}, u32[]{:S(2)}) %collective-permute-start.5) | collective-permute-done | bytes 1048608 | tf_op jit(solution)/shard_map/ppermute | solution.py:33
  57.3 2.6 %collective-permute-start.13 = (bf16[3,256,2048]{2,1,0:T(8,128)(2,1)}, bf16[3,256,2048]{2,1,0:T(8,128)(2,1)}, u32[]{:S(2)}, u32[]{:S(2)}) collective-permute-start(bf16[3,256,2048]{2,1,0:T(8,128)(2,1)} %pad_maximum_fusion.refs_0_), channel_id=1, source_target_pairs={{4,0},{5,1},{6,2},{7,3},{0,4},{1,5},{2,6},{3,7},{12,8},{13,9},{14,... | collective-permute-start | bytes 9437192 | tf_op jit(solution)/shard_map/ppermute | solution.py:33
  61.6 2.7 %collective-permute-start.10 = (bf16[256,2048]{1,0:T(8,128)(2,1)}, bf16[256,2048]{1,0:T(8,128)(2,1)}, u32[]{:S(2)}, u32[]{:S(2)}) collective-permute-start(bf16[256,2048]{1,0:T(8,128)(2,1)} %collective-permute-done.6.refs_5_), channel_id=1, source_target_pairs={{8,0},{9,1},{10,2},{11,3},{12,4},{13,5},{14,6},{15,7},{16,8},{17,9... | collective-permute-start | bytes 3145736 | tf_op jit(solution)/shard_map/ppermute | solution.py:33
  64.3 2.6 %collective-permute-start.12 = (bf16[256,2048]{1,0:T(8,128)(2,1)}, bf16[256,2048]{1,0:T(8,128)(2,1)}, u32[]{:S(2)}, u32[]{:S(2)}) collective-permute-start(bf16[256,2048]{1,0:T(8,128)(2,1)} %collective-permute-done.6.refs_5_), channel_id=1, source_target_pairs={{32,0},{33,1},{34,2},{35,3},{36,4},{37,5},{38,6},{39,7},{40,8},{41... | collective-permute-start | bytes 3145736 | tf_op jit(solution)/shard_map/ppermute | solution.py:33
  68.3 5.7 %station_counts.1.times_ref = f32[8,16,16,128]{3,2,1,0:T(8,128)} custom-call(s32[8,16,128]{2,1,0:T(8,128)} %broadcast_select_fusion.list_ref), custom_call_target="tpu_custom_call" | custom-call | flops 1000000000 | bytes 1048576 | tf_op jit(solution)/shard_map/station_counts/pallas_call | solution.py:67
  74.0 3.5 %convert_reduce_fusion = s32[8,16,16]{2,1,0:T(8,128)S(1)} fusion(f32[8,16,16,128]{3,2,1,0:T(8,128)} %station_counts.1.times_ref), kind=kLoop, calls=%fused_computation.5 | loop fusion | flops 1570816 | bytes 1056768 | tf_op jit(solution)/shard_map/reduce_max | solution.py:233
  77.7 2.7 %collective-permute-start.14 = (bf16[256,2048]{1,0:T(8,128)(2,1)S(1)}, bf16[256,2048]{1,0:T(8,128)(2,1)S(1)}, u32[]{:S(2)}, u32[]{:S(2)}) collective-permute-start(bf16[256,2048]{1,0:T(8,128)(2,1)S(1)} %collective-permute-done.4.refs_3_), channel_id=1, source_target_pairs={{8,0},{9,1},{10,2},{11,3},{12,4},{13,5},{14,6},{15,7},{16,8},{17,9... | collective-permute-start | bytes 3145736 | tf_op jit(solution)/shard_map/ppermute | solution.py:33
  80.4 7.2 %collective-permute-done.9.refs_2_ = bf16[256,2048]{1,0:T(8,128)(2,1)} collective-permute-done((bf16[256,2048]{1,0:T(8,128)(2,1)S(1)}, bf16[256,2048]{1,0:T(8,128)(2,1)}, u32[]{:S(2)}, u32[]{:S(2)}) %collective-permute-start.9) | collective-permute-done | bytes 1048608 | tf_op jit(solution)/shard_map/ppermute | solution.py:33
  87.6 2.6 %collective-permute-done.11.refs_4_ = bf16[256,2048]{1,0:T(8,128)(2,1)} collective-permute-done((bf16[256,2048]{1,0:T(8,128)(2,1)}, bf16[256,2048]{1,0:T(8,128)(2,1)}, u32[]{:S(2)}, u32[]{:S(2)}) %collective-permute-start.11) | collective-permute-done | bytes 1048608 | tf_op jit(solution)/shard_map/ppermute | solution.py:33
  95.0 19.0 %pairs.6 = f32[6,4,2,128]{3,2,1,0:T(2,128)S(1)} custom-call(s32[8,16]{1,0:T(8,128)S(1)} %shift-left_reduce_fusion.flag_ref, f32[8,16,16,128]{3,2,1,0:T(8,128)S(1)} %copy-done, bf16[3,256,2048]{2,1,0:T(8,128)(2,1)} %pad_maximum_fusion.refs_0_, bf16[3,256,2048]{2,1,0:T(8,128)(2,1)} %collective-permute-done.13.refs_1_, bf16[256,2048]{1,0:T(8,128)(2,1)S(1)} %bitcast.66, ...), custom_call_target="tpu_custom_call" | custom-call | flops 12884901888 | bytes 10485760 | tf_op jit(solution)/shard_map/pairs/pallas_call | solution.py:177
  115.7 2.6 %collective-permute-start.19 = (bf16[256,2048]{1,0:T(8,128)(2,1)S(1)}, bf16[256,2048]{1,0:T(8,128)(2,1)S(1)}, u32[]{:S(2)}, u32[]{:S(2)}) collective-permute-start(bf16[256,2048]{1,0:T(8,128)(2,1)S(1)} %collective-permute-done.18.refs_0_.refs_2_), channel_id=1, source_target_pairs={{4,0},{5,1},{6,2},{7,3},{0,4},{1,5},{2,6},{3,7},{12,8},{13,9},{14,... | collective-permute-start | bytes 3145736 | tf_op jit(solution)/shard_map/ppermute | solution.py:33
  118.4 21.6 %pairs.7 = f32[6,4,2,128]{3,2,1,0:T(2,128)S(1)} custom-call(s32[8,16]{1,0:T(8,128)S(1)} %shift-left_reduce_fusion.flag_ref, f32[8,16,16,128]{3,2,1,0:T(8,128)S(1)} %copy-done.1, bf16[3,256,2048]{2,1,0:T(8,128)(2,1)} %pad_maximum_fusion.refs_0_, bf16[3,256,2048]{2,1,0:T(8,128)(2,1)} %collective-permute-done.13.refs_1_, ...), custom_call_target="tpu_custom_call" | custom-call | flops 12884901888 | bytes 10485760 | tf_op jit(solution)/shard_map/pairs/pallas_call | solution.py:177
  144.7 7.8 %pairs.8 = f32[2,4,2,128]{3,2,1,0:T(2,128)S(1)} custom-call(s32[8,16]{1,0:T(8,128)S(1)} %shift-left_reduce_fusion.flag_ref, f32[8,16,16,128]{3,2,1,0:T(8,128)S(1)} %copy-done.1, bf16[256,2048]{1,0:T(8,128)(2,1)S(1)} %collective-permute-done.18.refs_0_.refs_2_, bf16[256,2048]{1,0:T(8,128)(2,1)S(1)} %collective-permute-done.19.refs_1_.refs_3_, ...), custom_call_target="tpu_custom_call" | custom-call | flops 4294967296 | bytes 6291456 | tf_op jit(solution)/shard_map/pairs/pallas_call | solution.py:177
  152.5 9.1 %pairs.9 = f32[2,4,2,128]{3,2,1,0:T(2,128)S(1)} custom-call(s32[8,16]{1,0:T(8,128)S(1)} %shift-left_reduce_fusion.flag_ref, f32[8,16,16,128]{3,2,1,0:T(8,128)S(1)} %copy-done.1, bf16[256,2048]{1,0:T(8,128)(2,1)S(1)} %collective-permute-done.18.refs_0_.refs_2_, bf16[256,2048]{1,0:T(8,128)(2,1)S(1)} %collective-permute-done.19.refs_1_.refs_3_, ...), custom_call_target="tpu_custom_call" | custom-call | flops 4294967296 | bytes 6291456 | tf_op jit(solution)/shard_map/pairs/pallas_call | solution.py:177
  161.6 22.4 %pairs.10 = f32[8,4,2,128]{3,2,1,0:T(2,128)S(1)} custom-call(s32[8,16]{1,0:T(8,128)S(1)} %shift-left_reduce_fusion.flag_ref, f32[8,16,16,128]{3,2,1,0:T(8,128)S(1)} %copy-done.1, bf16[3,256,2048]{2,1,0:T(8,128)(2,1)} %pad_maximum_fusion.refs_0_, bf16[3,256,2048]{2,1,0:T(8,128)(2,1)} %collective-permute-done.13.refs_1_, ...), custom_call_target="tpu_custom_call" | custom-call | flops 17179869184 | bytes 12582912 | tf_op jit(solution)/shard_map/pairs/pallas_call | solution.py:177
  184.0 22.4 %pairs.11 = f32[8,4,2,128]{3,2,1,0:T(2,128)S(1)} custom-call(s32[8,16]{1,0:T(8,128)S(1)} %shift-left_reduce_fusion.flag_ref, f32[8,16,16,128]{3,2,1,0:T(8,128)S(1)} %copy-done.1, bf16[3,256,2048]{2,1,0:T(8,128)(2,1)} %pad_maximum_fusion.refs_0_, bf16[3,256,2048]{2,1,0:T(8,128)(2,1)} %collective-permute-done.13.refs_1_, ...), custom_call_target="tpu_custom_call" | custom-call | flops 17179869184 | bytes 12582912 | tf_op jit(solution)/shard_map/pairs/pallas_call | solution.py:177
  207.8 10.8 %all_to_all.5 = f32[8,1,4096]{2,1,0:T(1,128)S(1)} all-to-all(f32[8,1,4096]{2,1,0:T(1,128)S(1)} %reshape.152), channel_id=1, replica_groups=mesh['z'=4,'y'=4,'c'=2,'x'=4] {'c','x'}, dimensions={0} | all-to-all | bytes 262144 | tf_op jit(solution)/shard_map/all_to_all | solution.py:261
  (90 shorter events, 30.8 us)
Async XLA Ops:
  5.1 9.6 %collective-permute-start = (bf16[64,2048]{1,0:T(8,128)(2,1)S(1)}, bf16[64,2048]{1,0:T(8,128)(2,1)S(1)}, u32[]{:S(2)}, u32[]{:S(2)}) collective-permute-start(bf16[64,2048]{1,0:T(8,128)(2,1)S(1)} %bitcast.77), channel_id=1, source_target_pairs={{1,0},{2,1},{3,2},{0,3},{5,4},{6,5},{7,6},{4,7},{9,8},{10,9},{11,1... | collective-permute-start | bytes 786440 | tf_op jit(solution)/shard_map/ppermute | solution.py:33
  8.7 8.5 %collective-permute-start.1 = (bf16[64,2048]{1,0:T(8,128)(2,1)S(1)}, bf16[64,2048]{1,0:T(8,128)(2,1)S(1)}, u32[]{:S(2)}, u32[]{:S(2)}) collective-permute-start(bf16[64,2048]{1,0:T(8,128)(2,1)S(1)} %bitcast.78), channel_id=1, source_target_pairs={{2,0},{3,1},{0,2},{1,3},{6,4},{7,5},{4,6},{5,7},{10,8},{11,9},{8,1... | collective-permute-start | bytes 786440 | tf_op jit(solution)/shard_map/ppermute | solution.py:33
  9.4 14.7 %collective-permute-start.2 = (bf16[64,2048]{1,0:T(8,128)(2,1)S(1)}, bf16[64,2048]{1,0:T(8,128)(2,1)S(1)}, u32[]{:S(2)}, u32[]{:S(2)}) collective-permute-start(bf16[64,2048]{1,0:T(8,128)(2,1)S(1)} %bitcast.79), channel_id=1, source_target_pairs={{3,0},{0,1},{1,2},{2,3},{7,4},{4,5},{5,6},{6,7},{11,8},{8,9},{9,10... | collective-permute-start | bytes 786440 | tf_op jit(solution)/shard_map/ppermute | solution.py:33
  10.3 14.2 %collective-permute-start.3 = (s32[4,16,128]{2,1,0:T(8,128)S(1)}, s32[4,16,128]{2,1,0:T(8,128)S(1)}, u32[]{:S(2)}, u32[]{:S(2)}) collective-permute-start(s32[4,16,128]{2,1,0:T(8,128)S(1)} %bitcast.83), channel_id=1, source_target_pairs={{4,0},{5,1},{6,2},{7,3},{0,4},{1,5},{2,6},{3,7},{12,8},{13,9},{14,... | collective-permute-start | bytes 98312 | tf_op jit(solution)/shard_map/ppermute | solution.py:33
  24.5 24.8 %collective-permute-start.4 = (bf16[256,2048]{1,0:T(8,128)(2,1)S(1)}, bf16[256,2048]{1,0:T(8,128)(2,1)S(1)}, u32[]{:S(2)}, u32[]{:S(2)}) collective-permute-start(bf16[256,2048]{1,0:T(8,128)(2,1)S(1)} %bitcast.59), channel_id=1, source_target_pairs={{8,0},{9,1},{10,2},{11,3},{12,4},{13,5},{14,6},{15,7},{16,8},{17,9... | collective-permute-start | bytes 3145736 | tf_op jit(solution)/shard_map/ppermute | solution.py:33
  27.3 25.1 %collective-permute-start.5 = (bf16[256,2048]{1,0:T(8,128)(2,1)S(1)}, bf16[256,2048]{1,0:T(8,128)(2,1)S(1)}, u32[]{:S(2)}, u32[]{:S(2)}) collective-permute-start(bf16[256,2048]{1,0:T(8,128)(2,1)S(1)} %bitcast.60), channel_id=1, source_target_pairs={{24,0},{25,1},{26,2},{27,3},{28,4},{29,5},{30,6},{31,7},{0,8},{1,9... | collective-permute-start | bytes 3145736 | tf_op jit(solution)/shard_map/ppermute | solution.py:33
  27.3 25.5 %collective-permute-start.6 = (bf16[256,2048]{1,0:T(8,128)(2,1)S(1)}, bf16[256,2048]{1,0:T(8,128)(2,1)}, u32[]{:S(2)}, u32[]{:S(2)}) collective-permute-start(bf16[256,2048]{1,0:T(8,128)(2,1)S(1)} %bitcast.61), channel_id=1, source_target_pairs={{32,0},{33,1},{34,2},{35,3},{36,4},{37,5},{38,6},{39,7},{40,8},{41... | collective-permute-start | bytes 3145736 | tf_op jit(solution)/shard_map/ppermute | solution.py:33
  31.1 23.6 %collective-permute-start.7 = (bf16[256,2048]{1,0:T(8,128)(2,1)S(1)}, bf16[256,2048]{1,0:T(8,128)(2,1)S(1)}, u32[]{:S(2)}, u32[]{:S(2)}) collective-permute-start(bf16[256,2048]{1,0:T(8,128)(2,1)S(1)} %bitcast.62), channel_id=1, source_target_pairs={{1,0},{2,1},{3,2},{0,3},{5,4},{6,5},{7,6},{4,7},{9,8},{10,9},{11,1... | collective-permute-start | bytes 3145736 | tf_op jit(solution)/shard_map/ppermute | solution.py:33
  31.1 24.2 %collective-permute-start.8 = (bf16[256,2048]{1,0:T(8,128)(2,1)S(1)}, bf16[256,2048]{1,0:T(8,128)(2,1)S(1)}, u32[]{:S(2)}, u32[]{:S(2)}) collective-permute-start(bf16[256,2048]{1,0:T(8,128)(2,1)S(1)} %bitcast.63), channel_id=1, source_target_pairs={{3,0},{0,1},{1,2},{2,3},{7,4},{4,5},{5,6},{6,7},{11,8},{8,9},{9,10... | collective-permute-start | bytes 3145736 | tf_op jit(solution)/shard_map/ppermute | solution.py:33
  57.3 20.4 %collective-permute-start.13 = (bf16[3,256,2048]{2,1,0:T(8,128)(2,1)}, bf16[3,256,2048]{2,1,0:T(8,128)(2,1)}, u32[]{:S(2)}, u32[]{:S(2)}) collective-permute-start(bf16[3,256,2048]{2,1,0:T(8,128)(2,1)} %pad_maximum_fusion.refs_0_), channel_id=1, source_target_pairs={{4,0},{5,1},{6,2},{7,3},{0,4},{1,5},{2,6},{3,7},{12,8},{13,9},{14,... | collective-permute-start | bytes 9437192 | tf_op jit(solution)/shard_map/ppermute | solution.py:33
  61.5 26.2 %collective-permute-start.9 = (bf16[256,2048]{1,0:T(8,128)(2,1)S(1)}, bf16[256,2048]{1,0:T(8,128)(2,1)}, u32[]{:S(2)}, u32[]{:S(2)}) collective-permute-start(bf16[256,2048]{1,0:T(8,128)(2,1)S(1)} %bitcast.65), channel_id=1, source_target_pairs={{96,0},{97,1},{98,2},{99,3},{100,4},{101,5},{102,6},{103,7},{104,8... | collective-permute-start | bytes 3145736 | tf_op jit(solution)/shard_map/ppermute | solution.py:33
  61.6 26.1 %collective-permute-start.10 = (bf16[256,2048]{1,0:T(8,128)(2,1)}, bf16[256,2048]{1,0:T(8,128)(2,1)}, u32[]{:S(2)}, u32[]{:S(2)}) collective-permute-start(bf16[256,2048]{1,0:T(8,128)(2,1)} %collective-permute-done.6.refs_5_), channel_id=1, source_target_pairs={{8,0},{9,1},{10,2},{11,3},{12,4},{13,5},{14,6},{15,7},{16,8},{17,9... | collective-permute-start | bytes 3145736 | tf_op jit(solution)/shard_map/ppermute | solution.py:33
  64.3 26.0 %collective-permute-start.11 = (bf16[256,2048]{1,0:T(8,128)(2,1)}, bf16[256,2048]{1,0:T(8,128)(2,1)}, u32[]{:S(2)}, u32[]{:S(2)}) collective-permute-start(bf16[256,2048]{1,0:T(8,128)(2,1)} %collective-permute-done.6.refs_5_), channel_id=1, source_target_pairs={{24,0},{25,1},{26,2},{27,3},{28,4},{29,5},{30,6},{31,7},{0,8},{1,9... | collective-permute-start | bytes 3145736 | tf_op jit(solution)/shard_map/ppermute | solution.py:33
  64.3 26.0 %collective-permute-start.12 = (bf16[256,2048]{1,0:T(8,128)(2,1)}, bf16[256,2048]{1,0:T(8,128)(2,1)}, u32[]{:S(2)}, u32[]{:S(2)}) collective-permute-start(bf16[256,2048]{1,0:T(8,128)(2,1)} %collective-permute-done.6.refs_5_), channel_id=1, source_target_pairs={{32,0},{33,1},{34,2},{35,3},{36,4},{37,5},{38,6},{39,7},{40,8},{41... | collective-permute-start | bytes 3145736 | tf_op jit(solution)/shard_map/ppermute | solution.py:33
  77.7 36.4 %collective-permute-start.14 = (bf16[256,2048]{1,0:T(8,128)(2,1)S(1)}, bf16[256,2048]{1,0:T(8,128)(2,1)S(1)}, u32[]{:S(2)}, u32[]{:S(2)}) collective-permute-start(bf16[256,2048]{1,0:T(8,128)(2,1)S(1)} %collective-permute-done.4.refs_3_), channel_id=1, source_target_pairs={{8,0},{9,1},{10,2},{11,3},{12,4},{13,5},{14,6},{15,7},{16,8},{17,9... | collective-permute-start | bytes 3145736 | tf_op jit(solution)/shard_map/ppermute | solution.py:33
  87.6 27.4 %collective-permute-start.17 = (bf16[256,2048]{1,0:T(8,128)(2,1)S(1)}, bf16[256,2048]{1,0:T(8,128)(2,1)S(1)}, u32[]{:S(2)}, u32[]{:S(2)}) collective-permute-start(bf16[256,2048]{1,0:T(8,128)(2,1)S(1)} %collective-permute-done.4.refs_3_), channel_id=1, source_target_pairs={{96,0},{97,1},{98,2},{99,3},{100,4},{101,5},{102,6},{103,7},{104,8... | collective-permute-start | bytes 3145736 | tf_op jit(solution)/shard_map/ppermute | solution.py:33
  90.3 24.9 %collective-permute-start.15 = (bf16[256,2048]{1,0:T(8,128)(2,1)}, bf16[256,2048]{1,0:T(8,128)(2,1)S(1)}, u32[]{:S(2)}, u32[]{:S(2)}) collective-permute-start(bf16[256,2048]{1,0:T(8,128)(2,1)} %collective-permute-done.9.refs_2_), channel_id=1, source_target_pairs={{24,0},{25,1},{26,2},{27,3},{28,4},{29,5},{30,6},{31,7},{0,8},{1,9... | collective-permute-start | bytes 3145736 | tf_op jit(solution)/shard_map/ppermute | solution.py:33
  90.3 24.9 %collective-permute-start.16 = (bf16[256,2048]{1,0:T(8,128)(2,1)}, bf16[256,2048]{1,0:T(8,128)(2,1)S(1)}, u32[]{:S(2)}, u32[]{:S(2)}) collective-permute-start(bf16[256,2048]{1,0:T(8,128)(2,1)} %collective-permute-done.10.refs_3_), channel_id=1, source_target_pairs={{32,0},{33,1},{34,2},{35,3},{36,4},{37,5},{38,6},{39,7},{40,8},{41... | collective-permute-start | bytes 3145736 | tf_op jit(solution)/shard_map/ppermute | solution.py:33
  92.6 23.1 %collective-permute-start.18 = (bf16[256,2048]{1,0:T(8,128)(2,1)}, bf16[256,2048]{1,0:T(8,128)(2,1)S(1)}, u32[]{:S(2)}, u32[]{:S(2)}) collective-permute-start(bf16[256,2048]{1,0:T(8,128)(2,1)} %copy-done.5), channel_id=1, source_target_pairs={{1,0},{2,1},{3,2},{0,3},{5,4},{6,5},{7,6},{4,7},{9,8},{10,9},{11,1... | collective-permute-start | bytes 3145736 | tf_op jit(solution)/shard_map/ppermute | solution.py:33
  114.1 69.9 %collective-permute-start.22 = (bf16[256,2048]{1,0:T(8,128)(2,1)}, bf16[256,2048]{1,0:T(8,128)(2,1)S(1)}, u32[]{:S(2)}, u32[]{:S(2)}) collective-permute-start(bf16[256,2048]{1,0:T(8,128)(2,1)} %collective-permute-done.12.refs_5_), channel_id=1, source_target_pairs={{24,0},{25,1},{26,2},{27,3},{28,4},{29,5},{30,6},{31,7},{0,8},{1,9... | collective-permute-start | bytes 3145736 | tf_op jit(solution)/shard_map/ppermute | solution.py:33
  115.7 29.0 %collective-permute-start.19 = (bf16[256,2048]{1,0:T(8,128)(2,1)S(1)}, bf16[256,2048]{1,0:T(8,128)(2,1)S(1)}, u32[]{:S(2)}, u32[]{:S(2)}) collective-permute-start(bf16[256,2048]{1,0:T(8,128)(2,1)S(1)} %collective-permute-done.18.refs_0_.refs_2_), channel_id=1, source_target_pairs={{4,0},{5,1},{6,2},{7,3},{0,4},{1,5},{2,6},{3,7},{12,8},{13,9},{14,... | collective-permute-start | bytes 3145736 | tf_op jit(solution)/shard_map/ppermute | solution.py:33
  140.0 44.0 %collective-permute-start.21 = (bf16[256,2048]{1,0:T(8,128)(2,1)S(1)}, bf16[256,2048]{1,0:T(8,128)(2,1)S(1)}, u32[]{:S(2)}, u32[]{:S(2)}) collective-permute-start(bf16[256,2048]{1,0:T(8,128)(2,1)S(1)} %collective-permute-done.14.refs_4_), channel_id=1, source_target_pairs={{32,0},{33,1},{34,2},{35,3},{36,4},{37,5},{38,6},{39,7},{40,8},{41... | collective-permute-start | bytes 3145736 | tf_op jit(solution)/shard_map/ppermute | solution.py:33
  142.4 41.7 %collective-permute-start.23 = (bf16[256,2048]{1,0:T(8,128)(2,1)S(1)}, bf16[256,2048]{1,0:T(8,128)(2,1)S(1)}, u32[]{:S(2)}, u32[]{:S(2)}) collective-permute-start(bf16[256,2048]{1,0:T(8,128)(2,1)S(1)} %collective-permute-done.14.refs_4_), channel_id=1, source_target_pairs={{96,0},{97,1},{98,2},{99,3},{100,4},{101,5},{102,6},{103,7},{104,8... | collective-permute-start | bytes 3145736 | tf_op jit(solution)/shard_map/ppermute | solution.py:33
  142.4 41.7 %collective-permute-start.20 = (bf16[256,2048]{1,0:T(8,128)(2,1)S(1)}, bf16[256,2048]{1,0:T(8,128)(2,1)S(1)}, u32[]{:S(2)}, u32[]{:S(2)}) collective-permute-start(bf16[256,2048]{1,0:T(8,128)(2,1)S(1)} %collective-permute-done.16.refs_6_), channel_id=1, source_target_pairs={{8,0},{9,1},{10,2},{11,3},{12,4},{13,5},{14,6},{15,7},{16,8},{17,9... | collective-permute-start | bytes 3145736 | tf_op jit(solution)/shard_map/ppermute | solution.py:33
  (8 other events, 95.1 us)
where the time goes:
time: 221 us
  Pallas kernels  108 us (49%)
  waiting for transfers between devices  45.2 us (20%)
  starting transfers between devices  35.6 us (16%)
  local copies, waits for them, and re-layouts  12.8 us (6%)
  blocking collectives  10.8 us (5%)
  other arithmetic  8.26 us (4%)
    pallas_call x6, Pallas kernels, predict(): pl.pallas_call(functools.partial(pair_kernel, tuple(r_parts), count_s, fi...  102 us
    ppermute x24, waiting for transfers between devices, from_offset(): return lax.ppermute(value, AXES, pairs)  45.2 us
    ppermute x24, starting transfers between devices, from_offset(): return lax.ppermute(value, AXES, pairs)  35.6 us
    all_to_all x1, blocking collectives, body(): made = lax.all_to_all(made, ('c', 'x'), 0, 0, tiled=True)  10.8 us
    pallas_call x1, Pallas kernels, station_counts(): pl.pallas_call(count_kernel, grid=(count_r,), in_specs=[pl.BlockSpec((1,...  5.71 us
    another operation x1, local copies, waits for them, and re-layouts  4.96 us
  transfers between devices with their start and end apart: 24, of which 12 were waited for; matrix products, arithmetic and copies ran while one was open for 3% of the time, Pallas kernels for 39%

commit v1 on v0

v1 whole, which is shorter than its diff:
```python
import functools
import itertools

import jax
import jax.numpy as jnp
import numpy as np
from jax import lax
from jax.experimental import pallas as pl
from jax.experimental.pallas import tpu as pltpu
from jax.sharding import Mesh
from jax.sharding import PartitionSpec as P

AXES = ("z", "y", "c", "x")
SIZES = (4, 4, 2, 4)
LANES = 128
NT_DIMS = (((1,), (1,)), ((), ()))

ROUNDS = (
    (((0, 1), (0, 1), (0, 0)), ((0, 3), (0, 3), (0, 0)), ((1, 0), (1, 0), (0, 0)), ((3, 0), (3, 0), (0, 0))),
    (((1, 1), (0, 1), (1, 0)), ((3, 3), (0, 3), (3, 0)), ((1, 3), (1, 0), (0, 3)), ((3, 1), (3, 0), (0, 1))),
    (((0, 2), (0, 1), (0, 1)), ((3, 2), (0, 3), (3, 3)), ((2, 0), (1, 0), (1, 0)), ((2, 1), (3, 0), (3, 1))),
    (((2, 2), (0, 1), (2, 1)), ((1, 2), (0, 3), (1, 3)), ((2, 3), (3, 0), (3, 3))),
)
S_OFFSETS = ((0, 0),) + tuple(hop[0] for hops in ROUNDS for hop in hops)


def from_offset(value, dz=0, dy=0, dc=0, dx=0):
    pairs = []
    for place in itertools.product(*(range(n) for n in SIZES)):
        source = tuple((p + d) % n for p, d, n in zip(place, (dz, dy, dc, dx), SIZES))
        pairs.append((int(np.ravel_multi_index(source, SIZES)), int(np.ravel_multi_index(place, SIZES))))
    return lax.ppermute(value, AXES, pairs)


def row_tables():
    list_rows, made_rows = [], []
    for z, y, c, x in itertools.product(*(range(n) for n in SIZES)):
        s_slot = [(z + dz) % 4 * 4 + (y + dy) % 4 for dz, dy in S_OFFSETS]
        cores = (0, 1) if c == 0 else (1, 0)
        list_rows.append([(core * 4 + r) * 16 + s for core in cores for r in range(4) for s in s_slot])
        made_rows.append([r * 16 + s_slot.index(s) for r in range(8) for s in range(16)])
    return np.asarray(list_rows, np.int32), np.asarray(made_rows, np.int32)


def count_kernel(list_ref, out_ref):
    stations = list_ref[0]
    high = stations >> 7
    low = stations & (LANES - 1)
    chunk = lax.broadcasted_iota(jnp.int32, (16, LANES), 0)
    lane = lax.broadcasted_iota(jnp.int32, (LANES, LANES), 0)
    for s in range(stations.shape[0]):
        is_high = (high[s : s + 1, :] == chunk).astype(jnp.float32).astype(jnp.bfloat16)
        is_low = (low[s : s + 1, :] == lane).astype(jnp.float32).astype(jnp.bfloat16)
        out_ref[0, s] = lax.dot_general(is_high, is_low, NT_DIMS, preferred_element_type=jnp.float32)


def station_counts(lists):
    count_r, count_s, _ = lists.shape
    return pl.pallas_call(
        count_kernel,
        grid=(count_r,),
        in_specs=[pl.BlockSpec((1, count_s, LANES), lambda i: (i, 0, 0))],
        out_specs=pl.BlockSpec((1, count_s, 16, LANES), lambda i: (i, 0, 0, 0)),
        out_shape=jax.ShapeDtypeStruct((count_r, count_s, 16, LANES), jnp.float32),
        cost_estimate=pl.CostEstimate(flops=10**9, bytes_accessed=2**20, transcendentals=0),
        name="station_counts",
    )(lists)


def antidiagonals(outer):
    tau = lax.broadcasted_iota(jnp.int32, (LANES, LANES), 0)
    lane = lax.broadcasted_iota(jnp.int32, (LANES, LANES), 1)
    keep = lane >= tau
    near = pltpu.roll(outer[:LANES, :LANES], 0, 1, stride=1, stride_axis=0)
    far = outer[:LANES, LANES:] + outer[LANES:, :LANES]
    far = pltpu.roll(far, 0, 1, stride=1, stride_axis=0)
    first = jnp.sum(jnp.where(keep, near, 0.0), axis=0, keepdims=True)
    second = jnp.sum(jnp.where(keep, far, near), axis=0, keepdims=True)
    return first, second


def pair_kernel(first_s, count_s, flag_ref, times_ref, r_ref, *refs):
    s_refs = refs[:count_s]
    out_ref, scaled, outer, rest, r_buf, sems = refs[count_s:]
    length, stations = s_refs[0].shape
    _, windows, group, window_len, _ = r_ref.shape
    chunks = stations // LANES
    r = pl.program_id(0)
    slot = lax.rem(r, 2)

    def fetches(number, to):
        for w in range(windows):
            yield pltpu.make_async_copy(
                r_ref.at[number // group, w, lax.rem(number, group)],
                r_buf.at[to, pl.ds(w * window_len, window_len)],
                sems.at[to, w],
            )

    @pl.when(r == 0)
    def _():
        for fetch in fetches(r, 0):
            fetch.start()

    @pl.when(r + 1 < pl.num_programs(0))
    def _():
        for fetch in fetches(r + 1, 1 - slot):
            fetch.start()

    for fetch in fetches(r, slot):
        fetch.wait()

    for s in range(count_s):
        for c in range(chunks):
            cols = slice(c * LANES, (c + 1) * LANES)
            times = jnp.broadcast_to(times_ref[0, first_s + s, c : c + 1, :], (16, LANES)).astype(jnp.bfloat16)
            times = jnp.concatenate([times] * (length // 16), axis=0)
            scaled[s * length : (s + 1) * length, cols] = s_refs[s][:, cols] * times
    outer[...] = lax.dot_general(scaled[...], r_buf[slot], NT_DIMS, preferred_element_type=jnp.float32)
    for s in range(count_s):
        first, second = antidiagonals(outer[s * length : (s + 1) * length, :])
        out_ref[0, s, 0:1, :] = first
        out_ref[0, s, 1:2, :] = second

    for s in range(count_s):
        rows = slice(s * length, (s + 1) * length)
        flag = flag_ref[r, first_s + s]

        @pl.when(flag != 0)
        def _():
            rest[...] = jnp.zeros_like(rest)

            def one(pair, carry):
                @pl.when((flag >> pair) & 1 != 0)
                def _():
                    parts = []
                    for half in range(2):
                        cols = pl.ds(pl.multiple_of((pair * 2 + half) * LANES, LANES), LANES)
                        times = times_ref[0, first_s + s, pl.ds(pair * 2 + half, 1), :]
                        whole = s_refs[s][:, cols].astype(jnp.float32) * jnp.broadcast_to(times, (length, LANES))
                        parts.append((whole - scaled[rows, cols].astype(jnp.float32)).astype(jnp.bfloat16))
                    both = pl.ds(pl.multiple_of(pair * 2 * LANES, 2 * LANES), 2 * LANES)
                    rest[...] += lax.dot_general(
                        jnp.concatenate(parts, axis=1),
                        r_buf[slot, :, both],
                        NT_DIMS,
                        preferred_element_type=jnp.float32,
                    )

                return carry

            lax.fori_loop(0, chunks // 2, one, 0)
            first, second = antidiagonals(rest[...])
            out_ref[0, s, 0:1, :] += first
            out_ref[0, s, 1:2, :] += second


def predict(flags, times, r_shots, s_shots, first_s):
    count_r, count_s = flags.shape[0], len(s_shots)
    length, stations = s_shots[0].shape
    grid_spec = pltpu.PrefetchScalarGridSpec(
        num_scalar_prefetch=1,
        grid=(count_r,),
        in_specs=[
            pl.BlockSpec((1,) + times.shape[1:], lambda i, f: (i, 0, 0, 0)),
            pl.BlockSpec(memory_space=pl.ANY),
        ]
        + [pl.BlockSpec((length, stations), lambda i, f: (0, 0), pipeline_mode=pl.Buffered(1))] * count_s,
        out_specs=pl.BlockSpec((1, count_s, 2, LANES), lambda i, f: (i, 0, 0, 0)),
        scratch_shapes=[
            pltpu.VMEM((count_s * length, stations), jnp.bfloat16),
            pltpu.VMEM((count_s * length, length), jnp.float32),
            pltpu.VMEM((length, length), jnp.float32),
            pltpu.VMEM((2, length, stations), jnp.bfloat16),
            pltpu.SemaphoreType.DMA((2, 4)),
        ],
    )
    return pl.pallas_call(
        functools.partial(pair_kernel, first_s, count_s),
        grid_spec=grid_spec,
        out_shape=jax.ShapeDtypeStruct((count_r, count_s, 2, LANES), jnp.float32),
        compiler_params=pltpu.CompilerParams(vmem_limit_bytes=20 << 20),
        cost_estimate=pl.CostEstimate(flops=2 * 10**9, bytes_accessed=2**20, transcendentals=0),
        name="pairs",
    )(flags, times, r_shots, *s_shots)


def body(signals, aperture, counts):
    length_win, group, stations = signals.shape
    shots = aperture.shape[1]
    slots = aperture.shape[2]
    z, y, c, x = (lax.axis_index(name) for name in AXES)

    live = jnp.arange(slots, dtype=jnp.int32) < counts[:, :, None]
    lists = jnp.where(live, aperture, -1).reshape(group, 16, 2, 4, slots)
    lists = lax.dynamic_index_in_dim(lists, x, 3, keepdims=False)
    mine = lax.dynamic_index_in_dim(lists, c, 2, keepdims=False)
    theirs = from_offset(lax.dynamic_index_in_dim(lists, 1 - c, 2, keepdims=False), dc=1)

    native = lax.optimization_barrier(jnp.transpose(signals, (1, 0, 2)))
    windows = [lax.dynamic_index_in_dim(native, x, 0, keepdims=False)]
    for dx in (1, 2, 3):
        windows.append(from_offset(lax.dynamic_index_in_dim(native, (x - dx) % 4, 0, keepdims=False), dx=dx))
    windows = jnp.stack(windows + windows)
    own = lax.dynamic_slice_in_dim(windows, (4 - x) % 4, 4, 0).reshape(4 * length_win, stations)
    r_shots = lax.all_gather(native, ("c", "x"), axis=0).reshape(2, 4, group, length_win, stations)
    own, mine, theirs = lax.optimization_barrier((own, mine, theirs))

    held = {(0, 0): own}
    blocks = []

    def travel(number):
        for offset, (dz, dy), forwarded in ROUNDS[number]:
            held[offset] = from_offset(held[forwarded], dz=dz, dy=dy)

    def meet(number, others):
        names = [hop[0] for hop in ROUNDS[number]]
        values = lax.optimization_barrier([held[name] for name in names] + list(others))
        held.update(zip(names, values))
        return values[len(names) :]

    def made_of(first_s, count_s):
        s_shots = [held[offset] for offset in S_OFFSETS[first_s : first_s + count_s]]
        return predict(flags, times, r_shots, s_shots, first_s)

    travel(0)
    lists = jnp.stack([mine, theirs]).reshape(2 * group * 16, slots)
    list_rows, made_rows = row_tables()
    device = ((z * 4 + y) * 2 + c) * 4 + x
    rows = lax.dynamic_index_in_dim(jnp.asarray(list_rows), device, 0, keepdims=False)
    lists = lists.at[rows].get(mode="promise_in_bounds").reshape(2 * group, 16, slots)
    times = station_counts(lists)
    whole = times.astype(jnp.int32).reshape(2 * group, 16, 8, 2 * LANES)
    odd = jnp.max((whole & (whole - 1) != 0).astype(jnp.int32), axis=3)
    flags = jnp.sum(odd << jnp.arange(8, dtype=jnp.int32), axis=2)
    flags, times = meet(0, (flags, times))

    travel(1)
    blocks += meet(1, [made_of(0, 5)])
    travel(2)
    blocks += meet(2, [made_of(5, 4)])
    travel(3)
    blocks += meet(3, [made_of(9, 4)])
    blocks.append(made_of(13, 3))
    made = jnp.concatenate(blocks, axis=1).reshape(2 * group * 16, 4 * length_win)

    rows = lax.dynamic_index_in_dim(jnp.asarray(made_rows), device, 0, keepdims=False)
    made = made.at[rows].get(mode="promise_in_bounds").reshape(2, group, 16, 4, length_win)
    made = jnp.transpose(made, (0, 3, 4, 1, 2)).reshape(8, length_win, group, 16)
    made = lax.all_to_all(made, ("c", "x"), 0, 0, tiled=True)
    made = made.reshape(2, 4, length_win, group, 16)
    return jnp.transpose(made, (2, 4, 0, 1, 3)).reshape(length_win, shots, group)


def solution(mesh):
    fine = Mesh(np.asarray(mesh.devices).reshape(SIZES), AXES)
    shot = ("z", "y", "c")
    in_specs = (P("x", shot, None), P(shot, None, None), P(shot, None))
    return jax.shard_map(body, mesh=fine, in_specs=in_specs, out_specs=P("x", None, shot), check_vma=False)
```

time: 221 us -> 179 us (0.81)
  Pallas kernels: 108 us -> 66.3 us
  between operations: 0.35 us -> 13.7 us
  starting transfers between devices: 35.6 us -> 25.4 us
  waiting for transfers between devices: 45.2 us -> 39.4 us
  blocking collectives: 10.8 us -> 13.8 us
  other arithmetic: 8.26 us -> 5.44 us
    pallas_call x6 -> x4, Pallas kernels: 102 us -> 60.6 us  [predict(): pl.pallas_call(functools.partial(pair_kernel, first_s, count_s), grid_spe...]
    ppermute x24 -> x19, starting transfers between devices: 35.6 us -> 25.4 us  [from_offset(): return lax.ppermute(value, AXES, pairs)]
    ppermute x24 -> x19, waiting for transfers between devices: 45.2 us -> 39.4 us  [from_offset(): return lax.ppermute(value, AXES, pairs)]
    unnamed x29 -> x22, local copies, waits for them, and re-layouts: 3.63 us -> 8.85 us
    another operation x1 -> x0, local copies, waits for them, and re-layouts: 4.96 us -> none
    all_to_all x1, blocking collectives: 10.8 us -> 13.8 us  [body(): made = lax.all_to_all(made, ('c', 'x'), 0, 0, tiled=True)]
  transfers between devices with their start and end apart: 24 -> 20, of which waited for: 12 -> 10; matrix products, arithmetic and copies ran while one was open for 3% -> 5% of each run, Pallas kernels for 39% -> 31%
where the time goes in v1:
time: 179 us
  Pallas kernels  66.3 us (37%)
  waiting for transfers between devices  39.4 us (22%)
  starting transfers between devices  25.4 us (14%)
  local copies, waits for them, and re-layouts  14.8 us (8%)
  blocking collectives  13.8 us (8%)
  between operations  13.7 us (8%)
  other arithmetic  5.44 us (3%)
    pallas_call x4, Pallas kernels, predict(): pl.pallas_call(functools.partial(pair_kernel, first_s, count_s), grid_spe...  60.6 us
    ppermute x19, waiting for transfers between devices, from_offset(): return lax.ppermute(value, AXES, pairs)  39.4 us
    ppermute x19, starting transfers between devices, from_offset(): return lax.ppermute(value, AXES, pairs)  25.4 us
    all_to_all x1, blocking collectives, body(): made = lax.all_to_all(made, ('c', 'x'), 0, 0, tiled=True)  13.8 us
    unnamed x22, local copies, waits for them, and re-layouts  8.85 us
    pallas_call x1, Pallas kernels, station_counts(): pl.pallas_call(count_kernel, grid=(count_r,), in_specs=[pl.BlockSpec((1,...  5.64 us
  transfers between devices with their start and end apart: 20, of which 10 were waited for; matrix products, arithmetic and copies ran while one was open for 5% of the time, Pallas kernels for 31%

profile of v1, /device:TPU:1, one launch (start us, length us, event | category | flops | bytes accessed | tf_op | source)
XLA Modules:
  0.0 178.9 jit_solution(12879411335847583454)
XLA Ops:
  6.5 2.9 %copy.20 = bf16[64,4,2048]{2,0,1:T(8,128)(2,1)} copy(bf16[64,4,2048]{2,1,0:T(4,128)(2,1)} %param.5) | data formatting | bytes 2097152 | tf_op args[0]
  9.5 2.1 %dynamic-slice_bitcast_fusion = (bf16[64,2048]{1,0:T(8,128)(2,1)S(1)}, bf16[8,64,2048]{2,1,0:T(8,128)(2,1)S(1)}, bf16[64,2048]{1,0:T(8,128)(2,1)}, bf16[64,2048]{1,0:T(8,128)(2,1)}) fusion(bf16[4,64,2048]{2,1,0:T(8,128)(2,1)} %bitcast.69, s32[]{:T(128)S(6)} %select_n.85, s32[]{:T(128)S(6)} %select_n.79, s32[]{:T(128)S(6)} %select_n.83, s32[]{:T(128)S(6)} %select_n.81), kind=kLoop, calls=%fused_computation.13 | loop fusion | bytes 2097168 | tf_op jit(solution)/shard_map/jit(dynamic_index_in_dim)/squeeze | solution.py:202
  11.6 3.3 %collective-permute-start = (bf16[64,2048]{1,0:T(8,128)(2,1)}, bf16[64,2048]{1,0:T(8,128)(2,1)S(1)}, u32[]{:S(2)}, u32[]{:S(2)}) collective-permute-start(bf16[64,2048]{1,0:T(8,128)(2,1)} %get-tuple-element.54), channel_id=1, source_target_pairs={{1,0},{2,1},{3,2},{0,3},{5,4},{6,5},{7,6},{4,7},{9,8},{10,9},{11,1... | collective-permute-start | bytes 786440 | tf_op jit(solution)/shard_map/ppermute | solution.py:32
  17.8 3.6 %collective-permute-done = bf16[64,2048]{1,0:T(8,128)(2,1)S(1)} collective-permute-done((bf16[64,2048]{1,0:T(8,128)(2,1)}, bf16[64,2048]{1,0:T(8,128)(2,1)S(1)}, u32[]{:S(2)}, u32[]{:S(2)}) %collective-permute-start) | collective-permute-done | bytes 262176 | tf_op jit(solution)/shard_map/ppermute | solution.py:32
  21.4 2.1 %collective-permute-done.1 = bf16[64,2048]{1,0:T(8,128)(2,1)S(1)} collective-permute-done((bf16[64,2048]{1,0:T(8,128)(2,1)}, bf16[64,2048]{1,0:T(8,128)(2,1)S(1)}, u32[]{:S(2)}, u32[]{:S(2)}) %collective-permute-start.1) | collective-permute-done | bytes 262176 | tf_op jit(solution)/shard_map/ppermute | solution.py:32
  23.5 10.1 %collective-permute-done.2 = bf16[64,2048]{1,0:T(8,128)(2,1)S(1)} collective-permute-done((bf16[64,2048]{1,0:T(8,128)(2,1)S(1)}, bf16[64,2048]{1,0:T(8,128)(2,1)S(1)}, u32[]{:S(2)}, u32[]{:S(2)}) %collective-permute-start.2) | collective-permute-done | bytes 262176 | tf_op jit(solution)/shard_map/ppermute | solution.py:32
  34.9 3.1 %collective-permute-start.4 = (bf16[256,2048]{1,0:T(8,128)(2,1)S(1)}, bf16[256,2048]{1,0:T(8,128)(2,1)S(1)}, u32[]{:S(2)}, u32[]{:S(2)}) collective-permute-start(bf16[256,2048]{1,0:T(8,128)(2,1)S(1)} %bitcast.63), channel_id=1, source_target_pairs={{8,0},{9,1},{10,2},{11,3},{12,4},{13,5},{14,6},{15,7},{16,8},{17,9... | collective-permute-start | bytes 3145736 | tf_op jit(solution)/shard_map/ppermute | solution.py:32
  38.0 4.6 %collective-permute-start.6 = (bf16[256,2048]{1,0:T(8,128)(2,1)S(1)}, bf16[256,2048]{1,0:T(8,128)(2,1)}, u32[]{:S(2)}, u32[]{:S(2)}) collective-permute-start(bf16[256,2048]{1,0:T(8,128)(2,1)S(1)} %bitcast.65), channel_id=1, source_target_pairs={{32,0},{33,1},{34,2},{35,3},{36,4},{37,5},{38,6},{39,7},{40,8},{41... | collective-permute-start | bytes 3145736 | tf_op jit(solution)/shard_map/ppermute | solution.py:32
  44.5 5.6 %station_counts.1.times_ref = f32[8,16,16,128]{3,2,1,0:T(8,128)} custom-call(s32[8,16,128]{2,1,0:T(8,128)} %bitcast.79), custom_call_target="tpu_custom_call" | custom-call | flops 1000000000 | bytes 1048576 | tf_op jit(solution)/shard_map/station_counts/pallas_call | solution.py:59
  50.1 3.5 %convert_reduce_fusion = s32[8,16,16]{2,1,0:T(8,128)S(1)} fusion(f32[8,16,16,128]{3,2,1,0:T(8,128)} %station_counts.1.times_ref), kind=kLoop, calls=%fused_computation.5 | loop fusion | flops 1570816 | bytes 1056768 | tf_op jit(solution)/shard_map/reduce_max | solution.py:233
  53.8 6.1 %collective-permute-done.4.refs_1_ = bf16[256,2048]{1,0:T(8,128)(2,1)S(1)} collective-permute-done((bf16[256,2048]{1,0:T(8,128)(2,1)S(1)}, bf16[256,2048]{1,0:T(8,128)(2,1)S(1)}, u32[]{:S(2)}, u32[]{:S(2)}) %collective-permute-start.4) | collective-permute-done | bytes 1048608 | tf_op jit(solution)/shard_map/ppermute | solution.py:32
  59.9 3.2 %collective-permute-done.5.refs_2_ = bf16[256,2048]{1,0:T(8,128)(2,1)} collective-permute-done((bf16[256,2048]{1,0:T(8,128)(2,1)S(1)}, bf16[256,2048]{1,0:T(8,128)(2,1)}, u32[]{:S(2)}, u32[]{:S(2)}) %collective-permute-start.5) | collective-permute-done | bytes 1048608 | tf_op jit(solution)/shard_map/ppermute | solution.py:32
  64.1 3.2 %collective-permute-done.7.refs_4_ = bf16[256,2048]{1,0:T(8,128)(2,1)} collective-permute-done((bf16[256,2048]{1,0:T(8,128)(2,1)S(1)}, bf16[256,2048]{1,0:T(8,128)(2,1)}, u32[]{:S(2)}, u32[]{:S(2)}) %collective-permute-start.7) | collective-permute-done | bytes 1048608 | tf_op jit(solution)/shard_map/ppermute | solution.py:32
  68.8 2.4 %collective-permute-start.8 = (bf16[256,2048]{1,0:T(8,128)(2,1)}, bf16[256,2048]{1,0:T(8,128)(2,1)}, u32[]{:S(2)}, u32[]{:S(2)}) collective-permute-start(bf16[256,2048]{1,0:T(8,128)(2,1)} %collective-permute-done.6.refs_3_), channel_id=1, source_target_pairs={{8,0},{9,1},{10,2},{11,3},{12,4},{13,5},{14,6},{15,7},{16,8},{17,9... | collective-permute-start | bytes 3145736 | tf_op jit(solution)/shard_map/ppermute | solution.py:32
  71.2 2.7 %collective-permute-start.12 = (bf16[256,2048]{1,0:T(8,128)(2,1)}, bf16[256,2048]{1,0:T(8,128)(2,1)}, u32[]{:S(2)}, u32[]{:S(2)}) collective-permute-start(bf16[256,2048]{1,0:T(8,128)(2,1)} %copy-done.2), channel_id=1, source_target_pairs={{8,0},{9,1},{10,2},{11,3},{12,4},{13,5},{14,6},{15,7},{16,8},{17,9... | collective-permute-start | bytes 3145736 | tf_op jit(solution)/shard_map/ppermute | solution.py:32
  73.9 3.4 %copy-done = bf16[32,64,2048]{2,1,0:T(8,128)(2,1)S(1)} copy-done((bf16[32,64,2048]{2,1,0:T(8,128)(2,1)S(1)}, bf16[32,64,2048]{2,1,0:T(8,128)(2,1)}, u32[]{:S(2)}) %copy-start) | copy-done | bytes 8388632
  78.5 19.7 %pairs.4 = f32[8,5,2,128]{3,2,1,0:T(2,128)S(1)} custom-call(s32[8,16]{1,0:T(8,128)S(1)} %shift-left_reduce_fusion.flag_ref, f32[8,16,16,128]{3,2,1,0:T(8,128)S(1)} %copy-done.1, bf16[2,4,4,64,2048]{4,3,2,1,0:T(8,128)(2,1)S(1)} %bitcast.59, bf16[256,2048]{1,0:T(8,128)(2,1)S(1)} %bitcast.67, bf16[256,2048]{1,0:T(8,128)(2,1)S(1)} %copy-done.3, ...), custom_call_target="tpu_custom_call" | custom-call | flops 2000000000 | bytes 1048576 | tf_op jit(solution)/shard_map/pairs/pallas_call | solution.py:177
  100.1 15.2 %pairs.5 = f32[8,4,2,128]{3,2,1,0:T(2,128)S(1)} custom-call(s32[8,16]{1,0:T(8,128)S(1)} %shift-left_reduce_fusion.flag_ref, f32[8,16,16,128]{3,2,1,0:T(8,128)S(1)} %copy-done.1, bf16[2,4,4,64,2048]{4,3,2,1,0:T(8,128)(2,1)S(1)} %bitcast.60, bf16[256,2048]{1,0:T(8,128)(2,1)} %collective-permute-done.8.refs_0_, ...), custom_call_target="tpu_custom_call" | custom-call | flops 2000000000 | bytes 1048576 | tf_op jit(solution)/shard_map/pairs/pallas_call | solution.py:177
  116.4 4.6 %collective-permute-done.14.refs_2_ = bf16[256,2048]{1,0:T(8,128)(2,1)S(1)} collective-permute-done((bf16[256,2048]{1,0:T(8,128)(2,1)}, bf16[256,2048]{1,0:T(8,128)(2,1)S(1)}, u32[]{:S(2)}, u32[]{:S(2)}) %collective-permute-start.14) | collective-permute-done | bytes 1048608 | tf_op jit(solution)/shard_map/ppermute | solution.py:32
  121.0 2.3 %collective-permute-start.16 = (bf16[256,2048]{1,0:T(8,128)(2,1)S(1)}, bf16[256,2048]{1,0:T(8,128)(2,1)S(1)}, u32[]{:S(2)}, u32[]{:S(2)}) collective-permute-start(bf16[256,2048]{1,0:T(8,128)(2,1)S(1)} %collective-permute-done.15.refs_3_), channel_id=1, source_target_pairs={{8,0},{9,1},{10,2},{11,3},{12,4},{13,5},{14,6},{15,7},{16,8},{17,9... | collective-permute-start | bytes 3145736 | tf_op jit(solution)/shard_map/ppermute | solution.py:32
  123.2 14.6 %pairs.6 = f32[8,4,2,128]{3,2,1,0:T(2,128)S(1)} custom-call(s32[8,16]{1,0:T(8,128)S(1)} %shift-left_reduce_fusion.flag_ref, f32[8,16,16,128]{3,2,1,0:T(8,128)S(1)} %copy-done.1, bf16[2,4,4,64,2048]{4,3,2,1,0:T(8,128)(2,1)S(1)} %bitcast.61, bf16[256,2048]{1,0:T(8,128)(2,1)} %collective-permute-done.12.refs_0_, ...), custom_call_target="tpu_custom_call" | custom-call | flops 2000000000 | bytes 1048576 | tf_op jit(solution)/shard_map/pairs/pallas_call | solution.py:177
  137.8 5.4 %collective-permute-done.17.refs_1_ = bf16[256,2048]{1,0:T(8,128)(2,1)S(1)} collective-permute-done((bf16[256,2048]{1,0:T(8,128)(2,1)S(1)}, bf16[256,2048]{1,0:T(8,128)(2,1)S(1)}, u32[]{:S(2)}, u32[]{:S(2)}) %collective-permute-start.17) | collective-permute-done | bytes 1048608 | tf_op jit(solution)/shard_map/ppermute | solution.py:32
  143.4 11.1 %pairs.7 = f32[8,3,2,128]{3,2,1,0:T(2,128)S(1)} custom-call(s32[8,16]{1,0:T(8,128)S(1)} %shift-left_reduce_fusion.flag_ref, f32[8,16,16,128]{3,2,1,0:T(8,128)S(1)} %copy-done.1, bf16[2,4,4,64,2048]{4,3,2,1,0:T(8,128)(2,1)S(1)} %bitcast.62, bf16[256,2048]{1,0:T(8,128)(2,1)S(1)} %collective-permute-done.16.refs_0_, ...), custom_call_target="tpu_custom_call" | custom-call | flops 2000000000 | bytes 1048576 | tf_op jit(solution)/shard_map/pairs/pallas_call | solution.py:177
  155.7 13.8 %all_to_all.5 = f32[8,1,4096]{2,1,0:T(1,128)S(1)} all-to-all(f32[8,1,4096]{2,1,0:T(1,128)S(1)} %reshape.121), channel_id=1, replica_groups=mesh['z'=4,'y'=4,'c'=2,'x'=4] {'c','x'}, dimensions={0} | all-to-all | bytes 262144 | tf_op jit(solution)/shard_map/all_to_all | solution.py:249
  (67 shorter events, 16.7 us)
Async XLA Ops:
  6.5 67.3 %all-gather.3.cloned.1.call-start = ((), (), s32[]{:S(2)}) async-start(), calls=%async_computation.1 | async-start | bytes 9437184 | tf_op jit(solution)/shard_map/all_gather | solution.py:205
  9.4 6.6 %copy-start.4 = (s32[4,128,128]{2,1,0:T(8,128)S(1)}, s32[4,128,128]{2,1,0:T(8,128)}, u32[]{:S(2)}) copy-start(s32[4,128,128]{2,1,0:T(8,128)} %param.6) | copy-start | bytes 786436
  9.4 6.6 %copy-start.5 = (s32[4,128]{1,0:T(4,128)S(1)}, s32[4,128]{1,0:T(4,128)}, u32[]{:S(2)}) copy-start(s32[4,128]{1,0:T(4,128)} %param.7) | copy-start | bytes 6148
  11.6 9.8 %collective-permute-start = (bf16[64,2048]{1,0:T(8,128)(2,1)}, bf16[64,2048]{1,0:T(8,128)(2,1)S(1)}, u32[]{:S(2)}, u32[]{:S(2)}) collective-permute-start(bf16[64,2048]{1,0:T(8,128)(2,1)} %get-tuple-element.54), channel_id=1, source_target_pairs={{1,0},{2,1},{3,2},{0,3},{5,4},{6,5},{7,6},{4,7},{9,8},{10,9},{11,1... | collective-permute-start | bytes 786440 | tf_op jit(solution)/shard_map/ppermute | solution.py:32
  14.9 8.6 %collective-permute-start.1 = (bf16[64,2048]{1,0:T(8,128)(2,1)}, bf16[64,2048]{1,0:T(8,128)(2,1)S(1)}, u32[]{:S(2)}, u32[]{:S(2)}) collective-permute-start(bf16[64,2048]{1,0:T(8,128)(2,1)} %get-tuple-element.53), channel_id=1, source_target_pairs={{2,0},{3,1},{0,2},{1,3},{6,4},{7,5},{4,6},{5,7},{10,8},{11,9},{8,1... | collective-permute-start | bytes 786440 | tf_op jit(solution)/shard_map/ppermute | solution.py:32
  15.4 18.2 %collective-permute-start.2 = (bf16[64,2048]{1,0:T(8,128)(2,1)S(1)}, bf16[64,2048]{1,0:T(8,128)(2,1)S(1)}, u32[]{:S(2)}, u32[]{:S(2)}) collective-permute-start(bf16[64,2048]{1,0:T(8,128)(2,1)S(1)} %get-tuple-element.51), channel_id=1, source_target_pairs={{3,0},{0,1},{1,2},{2,3},{7,4},{4,5},{5,6},{6,7},{11,8},{8,9},{9,10... | collective-permute-start | bytes 786440 | tf_op jit(solution)/shard_map/ppermute | solution.py:32
  16.2 18.6 %collective-permute-start.3 = (s32[4,16,128]{2,1,0:T(8,128)S(1)}, s32[4,16,128]{2,1,0:T(8,128)S(1)}, u32[]{:S(2)}, u32[]{:S(2)}) collective-permute-start(s32[4,16,128]{2,1,0:T(8,128)S(1)} %bitcast.81), channel_id=1, source_target_pairs={{4,0},{5,1},{6,2},{7,3},{0,4},{1,5},{2,6},{3,7},{12,8},{13,9},{14,... | collective-permute-start | bytes 98312 | tf_op jit(solution)/shard_map/ppermute | solution.py:32
  34.9 25.0 %collective-permute-start.4 = (bf16[256,2048]{1,0:T(8,128)(2,1)S(1)}, bf16[256,2048]{1,0:T(8,128)(2,1)S(1)}, u32[]{:S(2)}, u32[]{:S(2)}) collective-permute-start(bf16[256,2048]{1,0:T(8,128)(2,1)S(1)} %bitcast.63), channel_id=1, source_target_pairs={{8,0},{9,1},{10,2},{11,3},{12,4},{13,5},{14,6},{15,7},{16,8},{17,9... | collective-permute-start | bytes 3145736 | tf_op jit(solution)/shard_map/ppermute | solution.py:32
  37.9 25.1 %collective-permute-start.5 = (bf16[256,2048]{1,0:T(8,128)(2,1)S(1)}, bf16[256,2048]{1,0:T(8,128)(2,1)}, u32[]{:S(2)}, u32[]{:S(2)}) collective-permute-start(bf16[256,2048]{1,0:T(8,128)(2,1)S(1)} %bitcast.64), channel_id=1, source_target_pairs={{24,0},{25,1},{26,2},{27,3},{28,4},{29,5},{30,6},{31,7},{0,8},{1,9... | collective-permute-start | bytes 3145736 | tf_op jit(solution)/shard_map/ppermute | solution.py:32
  38.0 26.2 %collective-permute-start.6 = (bf16[256,2048]{1,0:T(8,128)(2,1)S(1)}, bf16[256,2048]{1,0:T(8,128)(2,1)}, u32[]{:S(2)}, u32[]{:S(2)}) collective-permute-start(bf16[256,2048]{1,0:T(8,128)(2,1)S(1)} %bitcast.65), channel_id=1, source_target_pairs={{32,0},{33,1},{34,2},{35,3},{36,4},{37,5},{38,6},{39,7},{40,8},{41... | collective-permute-start | bytes 3145736 | tf_op jit(solution)/shard_map/ppermute | solution.py:32
  42.5 24.8 %collective-permute-start.7 = (bf16[256,2048]{1,0:T(8,128)(2,1)S(1)}, bf16[256,2048]{1,0:T(8,128)(2,1)}, u32[]{:S(2)}, u32[]{:S(2)}) collective-permute-start(bf16[256,2048]{1,0:T(8,128)(2,1)S(1)} %bitcast.66), channel_id=1, source_target_pairs={{96,0},{97,1},{98,2},{99,3},{100,4},{101,5},{102,6},{103,7},{104,8... | collective-permute-start | bytes 3145736 | tf_op jit(solution)/shard_map/ppermute | solution.py:32
  50.1 23.7 %copy-start.1 = (f32[8,16,16,128]{3,2,1,0:T(8,128)S(1)}, f32[8,16,16,128]{3,2,1,0:T(8,128)}, u32[]{:S(2)}) copy-start(f32[8,16,16,128]{3,2,1,0:T(8,128)} %station_counts.1.times_ref) | copy-start | bytes 3145732
  59.9 4.2 %copy-start.2 = (bf16[256,2048]{1,0:T(8,128)(2,1)}, bf16[256,2048]{1,0:T(8,128)(2,1)S(1)}, u32[]{:S(2)}) copy-start(bf16[256,2048]{1,0:T(8,128)(2,1)S(1)} %collective-permute-done.4.refs_1_) | copy-start | bytes 3145732
  67.3 30.9 %collective-permute-start.10 = (bf16[256,2048]{1,0:T(8,128)(2,1)}, bf16[256,2048]{1,0:T(8,128)(2,1)S(1)}, u32[]{:S(2)}, u32[]{:S(2)}) collective-permute-start(bf16[256,2048]{1,0:T(8,128)(2,1)} %collective-permute-done.5.refs_2_), channel_id=1, source_target_pairs={{32,0},{33,1},{34,2},{35,3},{36,4},{37,5},{38,6},{39,7},{40,8},{41... | collective-permute-start | bytes 3145736 | tf_op jit(solution)/shard_map/ppermute | solution.py:32
  67.7 30.8 %collective-permute-start.11 = (bf16[256,2048]{1,0:T(8,128)(2,1)}, bf16[256,2048]{1,0:T(8,128)(2,1)}, u32[]{:S(2)}, u32[]{:S(2)}) collective-permute-start(bf16[256,2048]{1,0:T(8,128)(2,1)} %copy-done.2), channel_id=1, source_target_pairs={{96,0},{97,1},{98,2},{99,3},{100,4},{101,5},{102,6},{103,7},{104,8... | collective-permute-start | bytes 3145736 | tf_op jit(solution)/shard_map/ppermute | solution.py:32
  68.8 29.7 %collective-permute-start.8 = (bf16[256,2048]{1,0:T(8,128)(2,1)}, bf16[256,2048]{1,0:T(8,128)(2,1)}, u32[]{:S(2)}, u32[]{:S(2)}) collective-permute-start(bf16[256,2048]{1,0:T(8,128)(2,1)} %collective-permute-done.6.refs_3_), channel_id=1, source_target_pairs={{8,0},{9,1},{10,2},{11,3},{12,4},{13,5},{14,6},{15,7},{16,8},{17,9... | collective-permute-start | bytes 3145736 | tf_op jit(solution)/shard_map/ppermute | solution.py:32
  71.2 27.3 %collective-permute-start.9 = (bf16[256,2048]{1,0:T(8,128)(2,1)}, bf16[256,2048]{1,0:T(8,128)(2,1)}, u32[]{:S(2)}, u32[]{:S(2)}) collective-permute-start(bf16[256,2048]{1,0:T(8,128)(2,1)} %collective-permute-done.7.refs_4_), channel_id=1, source_target_pairs={{24,0},{25,1},{26,2},{27,3},{28,4},{29,5},{30,6},{31,7},{0,8},{1,9... | collective-permute-start | bytes 3145736 | tf_op jit(solution)/shard_map/ppermute | solution.py:32
  71.2 44.1 %collective-permute-start.12 = (bf16[256,2048]{1,0:T(8,128)(2,1)}, bf16[256,2048]{1,0:T(8,128)(2,1)}, u32[]{:S(2)}, u32[]{:S(2)}) collective-permute-start(bf16[256,2048]{1,0:T(8,128)(2,1)} %copy-done.2), channel_id=1, source_target_pairs={{8,0},{9,1},{10,2},{11,3},{12,4},{13,5},{14,6},{15,7},{16,8},{17,9... | collective-permute-start | bytes 3145736 | tf_op jit(solution)/shard_map/ppermute | solution.py:32
  98.2 22.7 %collective-permute-start.14 = (bf16[256,2048]{1,0:T(8,128)(2,1)}, bf16[256,2048]{1,0:T(8,128)(2,1)S(1)}, u32[]{:S(2)}, u32[]{:S(2)}) collective-permute-start(bf16[256,2048]{1,0:T(8,128)(2,1)} %collective-permute-done.6.refs_3_), channel_id=1, source_target_pairs={{32,0},{33,1},{34,2},{35,3},{36,4},{37,5},{38,6},{39,7},{40,8},{41... | collective-permute-start | bytes 3145736 | tf_op jit(solution)/shard_map/ppermute | solution.py:32
  98.5 22.4 %collective-permute-start.13 = (bf16[256,2048]{1,0:T(8,128)(2,1)}, bf16[256,2048]{1,0:T(8,128)(2,1)S(1)}, u32[]{:S(2)}, u32[]{:S(2)}) collective-permute-start(bf16[256,2048]{1,0:T(8,128)(2,1)} %collective-permute-done.9.refs_1_), channel_id=1, source_target_pairs={{24,0},{25,1},{26,2},{27,3},{28,4},{29,5},{30,6},{31,7},{0,8},{1,9... | collective-permute-start | bytes 3145736 | tf_op jit(solution)/shard_map/ppermute | solution.py:32
  98.6 22.4 %collective-permute-start.15 = (bf16[256,2048]{1,0:T(8,128)(2,1)}, bf16[256,2048]{1,0:T(8,128)(2,1)S(1)}, u32[]{:S(2)}, u32[]{:S(2)}) collective-permute-start(bf16[256,2048]{1,0:T(8,128)(2,1)} %collective-permute-done.11.refs_3_), channel_id=1, source_target_pairs={{96,0},{97,1},{98,2},{99,3},{100,4},{101,5},{102,6},{103,7},{104,8... | collective-permute-start | bytes 3145736 | tf_op jit(solution)/shard_map/ppermute | solution.py:32
  100.1 43.2 %collective-permute-start.17 = (bf16[256,2048]{1,0:T(8,128)(2,1)S(1)}, bf16[256,2048]{1,0:T(8,128)(2,1)S(1)}, u32[]{:S(2)}, u32[]{:S(2)}) collective-permute-start(bf16[256,2048]{1,0:T(8,128)(2,1)S(1)} %collective-permute-done.10.refs_2_), channel_id=1, source_target_pairs={{24,0},{25,1},{26,2},{27,3},{28,4},{29,5},{30,6},{31,7},{0,8},{1,9... | collective-permute-start | bytes 3145736 | tf_op jit(solution)/shard_map/ppermute | solution.py:32
  115.3 28.1 %collective-permute-start.18 = (bf16[256,2048]{1,0:T(8,128)(2,1)}, bf16[256,2048]{1,0:T(8,128)(2,1)S(1)}, u32[]{:S(2)}, u32[]{:S(2)}) collective-permute-start(bf16[256,2048]{1,0:T(8,128)(2,1)} %collective-permute-done.9.refs_1_), channel_id=1, source_target_pairs={{96,0},{97,1},{98,2},{99,3},{100,4},{101,5},{102,6},{103,7},{104,8... | collective-permute-start | bytes 3145736 | tf_op jit(solution)/shard_map/ppermute | solution.py:32
  121.0 22.4 %collective-permute-start.16 = (bf16[256,2048]{1,0:T(8,128)(2,1)S(1)}, bf16[256,2048]{1,0:T(8,128)(2,1)S(1)}, u32[]{:S(2)}, u32[]{:S(2)}) collective-permute-start(bf16[256,2048]{1,0:T(8,128)(2,1)S(1)} %collective-permute-done.15.refs_3_), channel_id=1, source_target_pairs={{8,0},{9,1},{10,2},{11,3},{12,4},{13,5},{14,6},{15,7},{16,8},{17,9... | collective-permute-start | bytes 3145736 | tf_op jit(solution)/shard_map/ppermute | solution.py:32
  (2 other events, 4.6 us)
Sparse Core Ops, SparseCore 0:
  9.5 56.6 all-gather.2

commit v2 on v1

--- a/solution.py
+++ b/solution.py
@@ -16,12 +16,24 @@
 NT_DIMS = (((1,), (1,)), ((), ()))
 
 ROUNDS = (
-    (((0, 1), (0, 1), (0, 0)), ((0, 3), (0, 3), (0, 0)), ((1, 0), (1, 0), (0, 0)), ((3, 0), (3, 0), (0, 0))),
-    (((1, 1), (0, 1), (1, 0)), ((3, 3), (0, 3), (3, 0)), ((1, 3), (1, 0), (0, 3)), ((3, 1), (3, 0), (0, 1))),
-    (((0, 2), (0, 1), (0, 1)), ((3, 2), (0, 3), (3, 3)), ((2, 0), (1, 0), (1, 0)), ((2, 1), (3, 0), (3, 1))),
-    (((2, 2), (0, 1), (2, 1)), ((1, 2), (0, 3), (1, 3)), ((2, 3), (3, 0), (3, 3))),
+    (
+        (((0, 1), (0, 1), (0, 0)), ((0, 3), (0, 3), (0, 0))),
+        (((1, 0), (1, 0), (0, 0)), ((3, 0), (3, 0), (0, 0))),
+    ),
+    (
+        (((1, 3), (1, 0), (0, 3)), ((3, 1), (3, 0), (0, 1))),
+        (((1, 1), (0, 1), (1, 0)), ((3, 3), (0, 3), (3, 0))),
+    ),
+    (
+        (((3, 2), (0, 1), (3, 1)), ((1, 2), (0, 3), (1, 3))),
+        (((2, 1), (1, 0), (1, 1)), ((2, 3), (3, 0), (3, 3))),
+    ),
+    (
+        (((0, 2), (1, 0), (3, 2)),),
+        (((2, 2), (0, 1), (2, 1)), ((2, 0), (0, 3), (2, 1))),
+    ),
 )
-S_OFFSETS = ((0, 0),) + tuple(hop[0] for hops in ROUNDS for hop in hops)
+S_OFFSETS = ((0, 0),) + tuple(hop[0] for parts in ROUNDS for part in parts for hop in part)
 
 
 def from_offset(value, dz=0, dy=0, dc=0, dx=0):
@@ -83,31 +95,22 @@
     s_refs = refs[:count_s]
     out_ref, scaled, outer, rest, r_buf, sems = refs[count_s:]
     length, stations = s_refs[0].shape
-    _, windows, group, window_len, _ = r_ref.shape
     chunks = stations // LANES
     r = pl.program_id(0)
     slot = lax.rem(r, 2)
 
-    def fetches(number, to):
-        for w in range(windows):
-            yield pltpu.make_async_copy(
-                r_ref.at[number // group, w, lax.rem(number, group)],
-                r_buf.at[to, pl.ds(w * window_len, window_len)],
-                sems.at[to, w],
-            )
+    def fetch(number, to):
+        return pltpu.make_async_copy(r_ref.at[number], r_buf.at[to], sems.at[to])
 
     @pl.when(r == 0)
     def _():
-        for fetch in fetches(r, 0):
-            fetch.start()
+        fetch(r, 0).start()
 
     @pl.when(r + 1 < pl.num_programs(0))
     def _():
-        for fetch in fetches(r + 1, 1 - slot):
-            fetch.start()
-
-    for fetch in fetches(r, slot):
-        fetch.wait()
+        fetch(r + 1, 1 - slot).start()
+
+    fetch(r, slot).wait()
 
     for s in range(count_s):
         for c in range(chunks):
@@ -162,7 +165,7 @@
         grid=(count_r,),
         in_specs=[
             pl.BlockSpec((1,) + times.shape[1:], lambda i, f: (i, 0, 0, 0)),
-            pl.BlockSpec(memory_space=pl.ANY),
+            pl.BlockSpec(memory_space=pltpu.HBM),
         ]
         + [pl.BlockSpec((length, stations), lambda i, f: (0, 0), pipeline_mode=pl.Buffered(1))] * count_s,
         out_specs=pl.BlockSpec((1, count_s, 2, LANES), lambda i, f: (i, 0, 0, 0)),
@@ -171,14 +174,14 @@
             pltpu.VMEM((count_s * length, length), jnp.float32),
             pltpu.VMEM((length, length), jnp.float32),
             pltpu.VMEM((2, length, stations), jnp.bfloat16),
-            pltpu.SemaphoreType.DMA((2, 4)),
+            pltpu.SemaphoreType.DMA((2,)),
         ],
     )
     return pl.pallas_call(
         functools.partial(pair_kernel, first_s, count_s),
         grid_spec=grid_spec,
         out_shape=jax.ShapeDtypeStruct((count_r, count_s, 2, LANES), jnp.float32),
-        compiler_params=pltpu.CompilerParams(vmem_limit_bytes=20 << 20),
+        compiler_params=pltpu.CompilerParams(vmem_limit_bytes=46 << 20),
         cost_estimate=pl.CostEstimate(flops=2 * 10**9, bytes_accessed=2**20, transcendentals=0),
         name="pairs",
     )(flags, times, r_shots, *s_shots)
@@ -202,18 +205,18 @@
         windows.append(from_offset(lax.dynamic_index_in_dim(native, (x - dx) % 4, 0, keepdims=False), dx=dx))
     windows = jnp.stack(windows + windows)
     own = lax.dynamic_slice_in_dim(windows, (4 - x) % 4, 4, 0).reshape(4 * length_win, stations)
-    r_shots = lax.all_gather(native, ("c", "x"), axis=0).reshape(2, 4, group, length_win, stations)
     own, mine, theirs = lax.optimization_barrier((own, mine, theirs))
+    r_shots = lax.all_gather(own, ("c", "x"), axis=0)
 
     held = {(0, 0): own}
     blocks = []
 
-    def travel(number):
-        for offset, (dz, dy), forwarded in ROUNDS[number]:
+    def travel(number, part):
+        for offset, (dz, dy), forwarded in ROUNDS[number][part]:
             held[offset] = from_offset(held[forwarded], dz=dz, dy=dy)
 
-    def meet(number, others):
-        names = [hop[0] for hop in ROUNDS[number]]
+    def meet(number, part, *others):
+        names = [hop[0] for hop in ROUNDS[number][part]]
         values = lax.optimization_barrier([held[name] for name in names] + list(others))
         held.update(zip(names, values))
         return values[len(names) :]
@@ -222,7 +225,8 @@
         s_shots = [held[offset] for offset in S_OFFSETS[first_s : first_s + count_s]]
         return predict(flags, times, r_shots, s_shots, first_s)
 
-    travel(0)
+    travel(0, 0)
+    travel(0, 1)
     lists = jnp.stack([mine, theirs]).reshape(2 * group * 16, slots)
     list_rows, made_rows = row_tables()
     device = ((z * 4 + y) * 2 + c) * 4 + x
@@ -232,15 +236,23 @@
     whole = times.astype(jnp.int32).reshape(2 * group, 16, 8, 2 * LANES)
     odd = jnp.max((whole & (whole - 1) != 0).astype(jnp.int32), axis=3)
     flags = jnp.sum(odd << jnp.arange(8, dtype=jnp.int32), axis=2)
-    flags, times = meet(0, (flags, times))
-
-    travel(1)
-    blocks += meet(1, [made_of(0, 5)])
-    travel(2)
-    blocks += meet(2, [made_of(5, 4)])
-    travel(3)
-    blocks += meet(3, [made_of(9, 4)])
-    blocks.append(made_of(13, 3))
+    flags, times = meet(0, 0, flags, times)
+    made = None
+    first_s = 0
+    for number in range(1, 4):
+        travel(number, 0)
+        if made is None:
+            meet(number - 1, 1)
+        else:
+            made = meet(number - 1, 1, made)[0]
+            blocks.append(made)
+        travel(number, 1)
+        count_s = 5 if number == 1 else 4
+        made = made_of(first_s, count_s)
+        first_s += count_s
+        made = meet(number, 0, made)[0]
+    blocks.append(meet(3, 1, made)[0])
+    blocks.append(made_of(first_s, 3))
     made = jnp.concatenate(blocks, axis=1).reshape(2 * group * 16, 4 * length_win)
 
     rows = lax.dynamic_index_in_dim(jnp.asarray(made_rows), device, 0, keepdims=False)

time: 179 us -> 197 us (1.10)
  waiting for transfers between devices: 39.4 us -> 52.3 us
  starting transfers between devices: 25.4 us -> 30.8 us
    all_gather x1, waiting for transfers between devices: 0.01 us -> 16.9 us  [body(): r_shots = lax.all_gather(own, ('c', 'x'), axis=0)]
    ppermute x19, starting transfers between devices: 25.4 us -> 30.8 us  [from_offset(): return lax.ppermute(value, AXES, pairs)]
    ppermute x19, waiting for transfers between devices: 39.4 us -> 35.4 us  [from_offset(): return lax.ppermute(value, AXES, pairs)]
    dynamic_slice x1, local copies, waits for them, and re-layouts: 0.11 us -> 2.39 us  [body(): lax.dynamic_slice_in_dim(windows, (4 - x) % 4, 4, 0)]
  transfers between devices with their start and end apart: 20 -> 20, of which waited for: 10 -> 12; matrix products, arithmetic and copies ran while one was open for 5% -> 7% of each run, Pallas kernels for 31% -> 28%
where the time goes in v2:
time: 197 us
  Pallas kernels  66.3 us (34%)
  waiting for transfers between devices  52.3 us (27%)
  starting transfers between devices  30.8 us (16%)
  local copies, waits for them, and re-layouts  16.4 us (8%)
  between operations  13.6 us (7%)
  blocking collectives  12.5 us (6%)
  other arithmetic  5.44 us (3%)
    pallas_call x4, Pallas kernels, predict(): pl.pallas_call(functools.partial(pair_kernel, first_s, count_s), grid_spe...  60.5 us
    ppermute x19, waiting for transfers between devices, from_offset(): return lax.ppermute(value, AXES, pairs)  35.4 us
    ppermute x19, starting transfers between devices, from_offset(): return lax.ppermute(value, AXES, pairs)  30.8 us
    all_gather x1, waiting for transfers between devices, body(): r_shots = lax.all_gather(own, ('c', 'x'), axis=0)  16.9 us
    all_to_all x1, blocking collectives, body(): made = lax.all_to_all(made, ('c', 'x'), 0, 0, tiled=True)  12.5 us
    unnamed x22, local copies, waits for them, and re-layouts  8.68 us
    pallas_call x1, Pallas kernels, station_counts(): pl.pallas_call(count_kernel, grid=(count_r,), in_specs=[pl.BlockSpec((1,...  5.8 us
  transfers between devices with their start and end apart: 20, of which 12 were waited for; matrix products, arithmetic and copies ran while one was open for 7% of the time, Pallas kernels for 28%

profile of v2, /device:TPU:1, one launch (start us, length us, event | category | flops | bytes accessed | tf_op | source)
XLA Modules:
  0.0 197.3 jit_solution(6829630467383535699)
XLA Ops:
  9.2 3.3 %collective-permute-start = (bf16[64,2048]{1,0:T(8,128)(2,1)S(1)}, bf16[64,2048]{1,0:T(8,128)(2,1)S(1)}, u32[]{:S(2)}, u32[]{:S(2)}) collective-permute-start(bf16[64,2048]{1,0:T(8,128)(2,1)S(1)} %get-tuple-element.60), channel_id=1, source_target_pairs={{1,0},{2,1},{3,2},{0,3},{5,4},{6,5},{7,6},{4,7},{9,8},{10,9},{11,1... | collective-permute-start | bytes 786440 | tf_op jit(solution)/shard_map/ppermute | solution.py:44
  15.5 3.2 %collective-permute-done = bf16[64,2048]{1,0:T(8,128)(2,1)S(1)} collective-permute-done((bf16[64,2048]{1,0:T(8,128)(2,1)S(1)}, bf16[64,2048]{1,0:T(8,128)(2,1)S(1)}, u32[]{:S(2)}, u32[]{:S(2)}) %collective-permute-start) | collective-permute-done | bytes 262176 | tf_op jit(solution)/shard_map/ppermute | solution.py:44
  21.6 6.2 %collective-permute-done.2 = bf16[64,2048]{1,0:T(8,128)(2,1)S(1)} collective-permute-done((bf16[64,2048]{1,0:T(8,128)(2,1)S(1)}, bf16[64,2048]{1,0:T(8,128)(2,1)S(1)}, u32[]{:S(2)}, u32[]{:S(2)}) %collective-permute-start.2) | collective-permute-done | bytes 262176 | tf_op jit(solution)/shard_map/ppermute | solution.py:44
  31.5 2.4 %constant_dynamic-slice_fusion.4 = bf16[4,64,2048]{2,1,0:T(8,128)(2,1)} fusion(bf16[8,64,2048]{2,1,0:T(8,128)(2,1)} %bitcast_dynamic-update-slice_fusion.1, s32[]{:T(128)S(6)} %select_n.87), kind=kLoop, calls=%fused_computation.32 | loop fusion | bytes 2097156 | tf_op jit(solution)/shard_map/dynamic_slice | solution.py:207
  33.9 2.8 %collective-permute-start.8 = (bf16[256,2048]{1,0:T(8,128)(2,1)}, bf16[256,2048]{1,0:T(8,128)(2,1)S(1)}, u32[]{:S(2)}, u32[]{:S(2)}) collective-permute-start(bf16[256,2048]{1,0:T(8,128)(2,1)} %bitcast.60), channel_id=1, source_target_pairs={{8,0},{9,1},{10,2},{11,3},{12,4},{13,5},{14,6},{15,7},{16,8},{17,9... | collective-permute-start | bytes 3145736 | tf_op jit(solution)/shard_map/ppermute | solution.py:44
  36.7 3.8 %collective-permute-start.4 = (bf16[256,2048]{1,0:T(8,128)(2,1)}, bf16[256,2048]{1,0:T(8,128)(2,1)}, u32[]{:S(2)}, u32[]{:S(2)}) collective-permute-start(bf16[256,2048]{1,0:T(8,128)(2,1)} %bitcast.62), channel_id=1, source_target_pairs={{32,0},{33,1},{34,2},{35,3},{36,4},{37,5},{38,6},{39,7},{40,8},{41... | collective-permute-start | bytes 3145736 | tf_op jit(solution)/shard_map/ppermute | solution.py:44
  42.5 5.8 %station_counts.1.times_ref = f32[8,16,16,128]{3,2,1,0:T(8,128)} custom-call(s32[8,16,128]{2,1,0:T(8,128)} %bitcast.79), custom_call_target="tpu_custom_call" | custom-call | flops 1000000000 | bytes 1048576 | tf_op jit(solution)/shard_map/station_counts/pallas_call | solution.py:71
  48.3 3.5 %convert_reduce_fusion = s32[8,16,16]{2,1,0:T(8,128)S(1)} fusion(f32[8,16,16,128]{3,2,1,0:T(8,128)} %station_counts.1.times_ref), kind=kLoop, calls=%fused_computation.5 | loop fusion | flops 1570816 | bytes 1056768 | tf_op jit(solution)/shard_map/reduce_max | solution.py:237
  52.0 7.1 %collective-permute-done.8.refs_1_ = bf16[256,2048]{1,0:T(8,128)(2,1)S(1)} collective-permute-done((bf16[256,2048]{1,0:T(8,128)(2,1)}, bf16[256,2048]{1,0:T(8,128)(2,1)S(1)}, u32[]{:S(2)}, u32[]{:S(2)}) %collective-permute-start.8) | collective-permute-done | bytes 1048608 | tf_op jit(solution)/shard_map/ppermute | solution.py:44
  60.1 2.1 %collective-permute-done.9.refs_2_ = bf16[256,2048]{1,0:T(8,128)(2,1)} collective-permute-done((bf16[256,2048]{1,0:T(8,128)(2,1)}, bf16[256,2048]{1,0:T(8,128)(2,1)}, u32[]{:S(2)}, u32[]{:S(2)}) %collective-permute-start.9) | collective-permute-done | bytes 1048608 | tf_op jit(solution)/shard_map/ppermute | solution.py:44
  62.2 3.8 %collective-permute-start.10 = (bf16[256,2048]{1,0:T(8,128)(2,1)}, bf16[256,2048]{1,0:T(8,128)(2,1)S(1)}, u32[]{:S(2)}, u32[]{:S(2)}) collective-permute-start(bf16[256,2048]{1,0:T(8,128)(2,1)} %collective-permute-done.9.refs_2_), channel_id=1, source_target_pairs={{32,0},{33,1},{34,2},{35,3},{36,4},{37,5},{38,6},{39,7},{40,8},{41... | collective-permute-start | bytes 3145736 | tf_op jit(solution)/shard_map/ppermute | solution.py:44
  65.9 2.1 %collective-permute-start.6 = (bf16[256,2048]{1,0:T(8,128)(2,1)}, bf16[256,2048]{1,0:T(8,128)(2,1)}, u32[]{:S(2)}, u32[]{:S(2)}) collective-permute-start(bf16[256,2048]{1,0:T(8,128)(2,1)} %collective-permute-done.4.refs_3_), channel_id=1, source_target_pairs={{8,0},{9,1},{10,2},{11,3},{12,4},{13,5},{14,6},{15,7},{16,8},{17,9... | collective-permute-start | bytes 3145736 | tf_op jit(solution)/shard_map/ppermute | solution.py:44
  68.0 16.9 %all-gather.3.cloned.1.call-done = bf16[2048,2048]{1,0:T(8,128)(2,1)} async-done(((bf16[256,2048]{1,0:T(8,128)(2,1)}), bf16[2048,2048]{1,0:T(8,128)(2,1)}) %all-gather.3.cloned.1.call-update) | async-done | bytes 8388624 | tf_op jit(solution)/shard_map/all_gather | solution.py:209
  86.1 19.6 %pairs.4 = f32[8,5,2,128]{3,2,1,0:T(2,128)S(1)} custom-call(s32[8,16]{1,0:T(8,128)S(1)} %shift-left_reduce_fusion.flag_ref, f32[8,16,16,128]{3,2,1,0:T(8,128)S(1)} %copy-done, bf16[8,256,2048]{2,1,0:T(8,128)(2,1)} %bitcast.65, bf16[256,2048]{1,0:T(8,128)(2,1)S(1)} %bitcast.64, bf16[256,2048]{1,0:T(8,128)(2,1)S(1)} %copy-done.3, ...), custom_call_target="tpu_custom_call" | custom-call | flops 2000000000 | bytes 1048576 | tf_op jit(solution)/shard_map/pairs/pallas_call | solution.py:180
  107.3 3.6 %collective-permute-start.12 = (bf16[256,2048]{1,0:T(8,128)(2,1)}, bf16[256,2048]{1,0:T(8,128)(2,1)S(1)}, u32[]{:S(2)}, u32[]{:S(2)}) collective-permute-start(bf16[256,2048]{1,0:T(8,128)(2,1)} %collective-permute-done.6.refs_2_), channel_id=1, source_target_pairs={{32,0},{33,1},{34,2},{35,3},{36,4},{37,5},{38,6},{39,7},{40,8},{41... | collective-permute-start | bytes 3145736 | tf_op jit(solution)/shard_map/ppermute | solution.py:44
  110.9 15.7 %pairs.5 = f32[8,4,2,128]{3,2,1,0:T(2,128)S(1)} custom-call(s32[8,16]{1,0:T(8,128)S(1)} %shift-left_reduce_fusion.flag_ref, f32[8,16,16,128]{3,2,1,0:T(8,128)S(1)} %copy-done, bf16[8,256,2048]{2,1,0:T(8,128)(2,1)} %bitcast.66, bf16[256,2048]{1,0:T(8,128)(2,1)S(1)} %collective-permute-done.10.refs_0_, bf16[256,2048]{1,0:T(8,128)(2,1)} %collective-permute-done.11.refs_1_, ...), custom_call_target="tpu_custom_call" | custom-call | flops 2000000000 | bytes 1048576 | tf_op jit(solution)/shard_map/pairs/pallas_call | solution.py:180
  126.6 4.3 %collective-permute-done.14.refs_0_ = bf16[256,2048]{1,0:T(8,128)(2,1)S(1)} collective-permute-done((bf16[256,2048]{1,0:T(8,128)(2,1)}, bf16[256,2048]{1,0:T(8,128)(2,1)S(1)}, u32[]{:S(2)}, u32[]{:S(2)}) %collective-permute-start.14) | collective-permute-done | bytes 1048608 | tf_op jit(solution)/shard_map/ppermute | solution.py:44
  131.4 5.1 %collective-permute-start.18 = (bf16[256,2048]{1,0:T(8,128)(2,1)S(1)}, bf16[256,2048]{1,0:T(8,128)(2,1)S(1)}, u32[]{:S(2)}, u32[]{:S(2)}) collective-permute-start(bf16[256,2048]{1,0:T(8,128)(2,1)S(1)} %collective-permute-done.14.refs_0_), channel_id=1, source_target_pairs={{32,0},{33,1},{34,2},{35,3},{36,4},{37,5},{38,6},{39,7},{40,8},{41... | collective-permute-start | bytes 3145736 | tf_op jit(solution)/shard_map/ppermute | solution.py:44
  136.7 2.1 %collective-permute-start.16 = (bf16[256,2048]{1,0:T(8,128)(2,1)S(1)}, bf16[256,2048]{1,0:T(8,128)(2,1)S(1)}, u32[]{:S(2)}, u32[]{:S(2)}) collective-permute-start(bf16[256,2048]{1,0:T(8,128)(2,1)S(1)} %collective-permute-done.12.refs_2_), channel_id=1, source_target_pairs={{8,0},{9,1},{10,2},{11,3},{12,4},{13,5},{14,6},{15,7},{16,8},{17,9... | collective-permute-start | bytes 3145736 | tf_op jit(solution)/shard_map/ppermute | solution.py:44
  138.8 13.8 %pairs.6 = f32[8,4,2,128]{3,2,1,0:T(2,128)S(1)} custom-call(s32[8,16]{1,0:T(8,128)S(1)} %shift-left_reduce_fusion.flag_ref, f32[8,16,16,128]{3,2,1,0:T(8,128)S(1)} %copy-done, bf16[8,256,2048]{2,1,0:T(8,128)(2,1)} %bitcast.67, bf16[256,2048]{1,0:T(8,128)(2,1)S(1)} %collective-permute-done.14.refs_0_, bf16[256,2048]{1,0:T(8,128)(2,1)S(1)} %collective-permute-done.15.refs_1_, ...), custom_call_target="tpu_custom_call" | custom-call | flops 2000000000 | bytes 1048576 | tf_op jit(solution)/shard_map/pairs/pallas_call | solution.py:180
  152.6 5.5 %collective-permute-done.18.refs_0_ = bf16[256,2048]{1,0:T(8,128)(2,1)S(1)} collective-permute-done((bf16[256,2048]{1,0:T(8,128)(2,1)S(1)}, bf16[256,2048]{1,0:T(8,128)(2,1)S(1)}, u32[]{:S(2)}, u32[]{:S(2)}) %collective-permute-start.18) | collective-permute-done | bytes 1048608 | tf_op jit(solution)/shard_map/ppermute | solution.py:44
  160.2 2.7 %collective-permute-done.17.refs_2_ = bf16[256,2048]{1,0:T(8,128)(2,1)S(1)} collective-permute-done((bf16[256,2048]{1,0:T(8,128)(2,1)S(1)}, bf16[256,2048]{1,0:T(8,128)(2,1)S(1)}, u32[]{:S(2)}, u32[]{:S(2)}) %collective-permute-start.17) | collective-permute-done | bytes 1048608 | tf_op jit(solution)/shard_map/ppermute | solution.py:44
  162.9 11.3 %pairs.7 = f32[8,3,2,128]{3,2,1,0:T(2,128)S(1)} custom-call(s32[8,16]{1,0:T(8,128)S(1)} %shift-left_reduce_fusion.flag_ref, f32[8,16,16,128]{3,2,1,0:T(8,128)S(1)} %copy-done, bf16[8,256,2048]{2,1,0:T(8,128)(2,1)} %bitcast.68, bf16[256,2048]{1,0:T(8,128)(2,1)S(1)} %collective-permute-done.18.refs_0_, bf16[256,2048]{1,0:T(8,128)(2,1)S(1)} %collective-permute-done.16.refs_1_, ...), custom_call_target="tpu_custom_call" | custom-call | flops 2000000000 | bytes 1048576 | tf_op jit(solution)/shard_map/pairs/pallas_call | solution.py:180
  175.4 12.5 %all_to_all.5 = f32[8,1,4096]{2,1,0:T(1,128)S(1)} all-to-all(f32[8,1,4096]{2,1,0:T(1,128)S(1)} %reshape.116), channel_id=1, replica_groups=mesh['z'=4,'y'=4,'c'=2,'x'=4] {'c','x'}, dimensions={0} | all-to-all | bytes 262144 | tf_op jit(solution)/shard_map/all_to_all | solution.py:261
  (67 shorter events, 24.4 us)
Async XLA Ops:
  6.5 78.4 %all-gather.3.cloned.1.call-start = ((), (), s32[]{:S(2)}) async-start(), calls=%async_computation.1 | async-start | bytes 9437184 | tf_op jit(solution)/shard_map/all_gather | solution.py:209
  6.5 7.1 %copy-start.4 = (s32[4,128,128]{2,1,0:T(8,128)S(1)}, s32[4,128,128]{2,1,0:T(8,128)}, u32[]{:S(2)}) copy-start(s32[4,128,128]{2,1,0:T(8,128)} %param.6) | copy-start | bytes 786436
  6.5 7.1 %copy-start.5 = (s32[4,128]{1,0:T(4,128)S(1)}, s32[4,128]{1,0:T(4,128)}, u32[]{:S(2)}) copy-start(s32[4,128]{1,0:T(4,128)} %param.7) | copy-start | bytes 6148
  9.2 9.5 %collective-permute-start = (bf16[64,2048]{1,0:T(8,128)(2,1)S(1)}, bf16[64,2048]{1,0:T(8,128)(2,1)S(1)}, u32[]{:S(2)}, u32[]{:S(2)}) collective-permute-start(bf16[64,2048]{1,0:T(8,128)(2,1)S(1)} %get-tuple-element.60), channel_id=1, source_target_pairs={{1,0},{2,1},{3,2},{0,3},{5,4},{6,5},{7,6},{4,7},{9,8},{10,9},{11,1... | collective-permute-start | bytes 786440 | tf_op jit(solution)/shard_map/ppermute | solution.py:44
  12.5 8.4 %collective-permute-start.1 = (bf16[64,2048]{1,0:T(8,128)(2,1)S(1)}, bf16[64,2048]{1,0:T(8,128)(2,1)S(1)}, u32[]{:S(2)}, u32[]{:S(2)}) collective-permute-start(bf16[64,2048]{1,0:T(8,128)(2,1)S(1)} %get-tuple-element.59), channel_id=1, source_target_pairs={{2,0},{3,1},{0,2},{1,3},{6,4},{7,5},{4,6},{5,7},{10,8},{11,9},{8,1... | collective-permute-start | bytes 786440 | tf_op jit(solution)/shard_map/ppermute | solution.py:44
  13.0 14.8 %collective-permute-start.2 = (bf16[64,2048]{1,0:T(8,128)(2,1)S(1)}, bf16[64,2048]{1,0:T(8,128)(2,1)S(1)}, u32[]{:S(2)}, u32[]{:S(2)}) collective-permute-start(bf16[64,2048]{1,0:T(8,128)(2,1)S(1)} %get-tuple-element.57), channel_id=1, source_target_pairs={{3,0},{0,1},{1,2},{2,3},{7,4},{4,5},{5,6},{6,7},{11,8},{8,9},{9,10... | collective-permute-start | bytes 786440 | tf_op jit(solution)/shard_map/ppermute | solution.py:44
  13.9 20.0 %collective-permute-start.3 = (s32[4,16,128]{2,1,0:T(8,128)S(1)}, s32[4,16,128]{2,1,0:T(8,128)S(1)}, u32[]{:S(2)}, u32[]{:S(2)}) collective-permute-start(s32[4,16,128]{2,1,0:T(8,128)S(1)} %bitcast.81), channel_id=1, source_target_pairs={{4,0},{5,1},{6,2},{7,3},{0,4},{1,5},{2,6},{3,7},{12,8},{13,9},{14,... | collective-permute-start | bytes 98312 | tf_op jit(solution)/shard_map/ppermute | solution.py:44
  33.9 25.2 %collective-permute-start.8 = (bf16[256,2048]{1,0:T(8,128)(2,1)}, bf16[256,2048]{1,0:T(8,128)(2,1)S(1)}, u32[]{:S(2)}, u32[]{:S(2)}) collective-permute-start(bf16[256,2048]{1,0:T(8,128)(2,1)} %bitcast.60), channel_id=1, source_target_pairs={{8,0},{9,1},{10,2},{11,3},{12,4},{13,5},{14,6},{15,7},{16,8},{17,9... | collective-permute-start | bytes 3145736 | tf_op jit(solution)/shard_map/ppermute | solution.py:44
  36.7 25.4 %collective-permute-start.9 = (bf16[256,2048]{1,0:T(8,128)(2,1)}, bf16[256,2048]{1,0:T(8,128)(2,1)}, u32[]{:S(2)}, u32[]{:S(2)}) collective-permute-start(bf16[256,2048]{1,0:T(8,128)(2,1)} %bitcast.61), channel_id=1, source_target_pairs={{24,0},{25,1},{26,2},{27,3},{28,4},{29,5},{30,6},{31,7},{0,8},{1,9... | collective-permute-start | bytes 3145736 | tf_op jit(solution)/shard_map/ppermute | solution.py:44
  36.7 29.2 %collective-permute-start.4 = (bf16[256,2048]{1,0:T(8,128)(2,1)}, bf16[256,2048]{1,0:T(8,128)(2,1)}, u32[]{:S(2)}, u32[]{:S(2)}) collective-permute-start(bf16[256,2048]{1,0:T(8,128)(2,1)} %bitcast.62), channel_id=1, source_target_pairs={{32,0},{33,1},{34,2},{35,3},{36,4},{37,5},{38,6},{39,7},{40,8},{41... | collective-permute-start | bytes 3145736 | tf_op jit(solution)/shard_map/ppermute | solution.py:44
  40.5 25.4 %collective-permute-start.5 = (bf16[256,2048]{1,0:T(8,128)(2,1)}, bf16[256,2048]{1,0:T(8,128)(2,1)}, u32[]{:S(2)}, u32[]{:S(2)}) collective-permute-start(bf16[256,2048]{1,0:T(8,128)(2,1)} %bitcast.63), channel_id=1, source_target_pairs={{96,0},{97,1},{98,2},{99,3},{100,4},{101,5},{102,6},{103,7},{104,8... | collective-permute-start | bytes 3145736 | tf_op jit(solution)/shard_map/ppermute | solution.py:44
  42.5 42.4 %copy-start.1 = (bf16[4,64,2048]{2,1,0:T(8,128)(2,1)S(1)}, bf16[4,64,2048]{2,1,0:T(8,128)(2,1)}, u32[]{:S(2)}) copy-start(bf16[4,64,2048]{2,1,0:T(8,128)(2,1)} %constant_dynamic-slice_fusion.4) | copy-start | bytes 3145732
  48.3 36.6 %copy-start = (f32[8,16,16,128]{3,2,1,0:T(8,128)S(1)}, f32[8,16,16,128]{3,2,1,0:T(8,128)}, u32[]{:S(2)}) copy-start(f32[8,16,16,128]{3,2,1,0:T(8,128)} %station_counts.1.times_ref) | copy-start | bytes 3145732
  62.2 43.6 %collective-permute-start.10 = (bf16[256,2048]{1,0:T(8,128)(2,1)}, bf16[256,2048]{1,0:T(8,128)(2,1)S(1)}, u32[]{:S(2)}, u32[]{:S(2)}) collective-permute-start(bf16[256,2048]{1,0:T(8,128)(2,1)} %collective-permute-done.9.refs_2_), channel_id=1, source_target_pairs={{32,0},{33,1},{34,2},{35,3},{36,4},{37,5},{38,6},{39,7},{40,8},{41... | collective-permute-start | bytes 3145736 | tf_op jit(solution)/shard_map/ppermute | solution.py:44
  65.9 39.8 %collective-permute-start.11 = (bf16[256,2048]{1,0:T(8,128)(2,1)}, bf16[256,2048]{1,0:T(8,128)(2,1)}, u32[]{:S(2)}, u32[]{:S(2)}) collective-permute-start(bf16[256,2048]{1,0:T(8,128)(2,1)} %copy-done.2), channel_id=1, source_target_pairs={{96,0},{97,1},{98,2},{99,3},{100,4},{101,5},{102,6},{103,7},{104,8... | collective-permute-start | bytes 3145736 | tf_op jit(solution)/shard_map/ppermute | solution.py:44
  65.9 41.3 %collective-permute-start.6 = (bf16[256,2048]{1,0:T(8,128)(2,1)}, bf16[256,2048]{1,0:T(8,128)(2,1)}, u32[]{:S(2)}, u32[]{:S(2)}) collective-permute-start(bf16[256,2048]{1,0:T(8,128)(2,1)} %collective-permute-done.4.refs_3_), channel_id=1, source_target_pairs={{8,0},{9,1},{10,2},{11,3},{12,4},{13,5},{14,6},{15,7},{16,8},{17,9... | collective-permute-start | bytes 3145736 | tf_op jit(solution)/shard_map/ppermute | solution.py:44
  68.0 39.3 %collective-permute-start.7 = (bf16[256,2048]{1,0:T(8,128)(2,1)}, bf16[256,2048]{1,0:T(8,128)(2,1)}, u32[]{:S(2)}, u32[]{:S(2)}) collective-permute-start(bf16[256,2048]{1,0:T(8,128)(2,1)} %collective-permute-done.5.refs_4_), channel_id=1, source_target_pairs={{24,0},{25,1},{26,2},{27,3},{28,4},{29,5},{30,6},{31,7},{0,8},{1,9... | collective-permute-start | bytes 3145736 | tf_op jit(solution)/shard_map/ppermute | solution.py:44
  105.7 25.2 %collective-permute-start.14 = (bf16[256,2048]{1,0:T(8,128)(2,1)}, bf16[256,2048]{1,0:T(8,128)(2,1)S(1)}, u32[]{:S(2)}, u32[]{:S(2)}) collective-permute-start(bf16[256,2048]{1,0:T(8,128)(2,1)} %collective-permute-done.11.refs_1_), channel_id=1, source_target_pairs={{8,0},{9,1},{10,2},{11,3},{12,4},{13,5},{14,6},{15,7},{16,8},{17,9... | collective-permute-start | bytes 3145736 | tf_op jit(solution)/shard_map/ppermute | solution.py:44
  107.0 24.4 %collective-permute-start.15 = (bf16[256,2048]{1,0:T(8,128)(2,1)S(1)}, bf16[256,2048]{1,0:T(8,128)(2,1)S(1)}, u32[]{:S(2)}, u32[]{:S(2)}) collective-permute-start(bf16[256,2048]{1,0:T(8,128)(2,1)S(1)} %collective-permute-done.10.refs_0_), channel_id=1, source_target_pairs={{24,0},{25,1},{26,2},{27,3},{28,4},{29,5},{30,6},{31,7},{0,8},{1,9... | collective-permute-start | bytes 3145736 | tf_op jit(solution)/shard_map/ppermute | solution.py:44
  107.3 29.2 %collective-permute-start.12 = (bf16[256,2048]{1,0:T(8,128)(2,1)}, bf16[256,2048]{1,0:T(8,128)(2,1)S(1)}, u32[]{:S(2)}, u32[]{:S(2)}) collective-permute-start(bf16[256,2048]{1,0:T(8,128)(2,1)} %collective-permute-done.6.refs_2_), channel_id=1, source_target_pairs={{32,0},{33,1},{34,2},{35,3},{36,4},{37,5},{38,6},{39,7},{40,8},{41... | collective-permute-start | bytes 3145736 | tf_op jit(solution)/shard_map/ppermute | solution.py:44
  110.9 25.8 %collective-permute-start.13 = (bf16[256,2048]{1,0:T(8,128)(2,1)}, bf16[256,2048]{1,0:T(8,128)(2,1)S(1)}, u32[]{:S(2)}, u32[]{:S(2)}) collective-permute-start(bf16[256,2048]{1,0:T(8,128)(2,1)} %collective-permute-done.7.refs_3_), channel_id=1, source_target_pairs={{96,0},{97,1},{98,2},{99,3},{100,4},{101,5},{102,6},{103,7},{104,8... | collective-permute-start | bytes 3145736 | tf_op jit(solution)/shard_map/ppermute | solution.py:44
  131.4 26.7 %collective-permute-start.18 = (bf16[256,2048]{1,0:T(8,128)(2,1)S(1)}, bf16[256,2048]{1,0:T(8,128)(2,1)S(1)}, u32[]{:S(2)}, u32[]{:S(2)}) collective-permute-start(bf16[256,2048]{1,0:T(8,128)(2,1)S(1)} %collective-permute-done.14.refs_0_), channel_id=1, source_target_pairs={{32,0},{33,1},{34,2},{35,3},{36,4},{37,5},{38,6},{39,7},{40,8},{41... | collective-permute-start | bytes 3145736 | tf_op jit(solution)/shard_map/ppermute | solution.py:44
  136.7 23.5 %collective-permute-start.16 = (bf16[256,2048]{1,0:T(8,128)(2,1)S(1)}, bf16[256,2048]{1,0:T(8,128)(2,1)S(1)}, u32[]{:S(2)}, u32[]{:S(2)}) collective-permute-start(bf16[256,2048]{1,0:T(8,128)(2,1)S(1)} %collective-permute-done.12.refs_2_), channel_id=1, source_target_pairs={{8,0},{9,1},{10,2},{11,3},{12,4},{13,5},{14,6},{15,7},{16,8},{17,9... | collective-permute-start | bytes 3145736 | tf_op jit(solution)/shard_map/ppermute | solution.py:44
  138.8 24.1 %collective-permute-start.17 = (bf16[256,2048]{1,0:T(8,128)(2,1)S(1)}, bf16[256,2048]{1,0:T(8,128)(2,1)S(1)}, u32[]{:S(2)}, u32[]{:S(2)}) collective-permute-start(bf16[256,2048]{1,0:T(8,128)(2,1)S(1)} %collective-permute-done.12.refs_2_), channel_id=1, source_target_pairs={{24,0},{25,1},{26,2},{27,3},{28,4},{29,5},{30,6},{31,7},{0,8},{1,9... | collective-permute-start | bytes 3145736 | tf_op jit(solution)/shard_map/ppermute | solution.py:44
  (2 other events, 2.2 us)
Sparse Core Ops, SparseCore 0:
  34.1 50.7 all-gather.2

commit v3 on v1

--- a/solution.py
+++ b/solution.py
@@ -178,7 +178,7 @@
         functools.partial(pair_kernel, first_s, count_s),
         grid_spec=grid_spec,
         out_shape=jax.ShapeDtypeStruct((count_r, count_s, 2, LANES), jnp.float32),
-        compiler_params=pltpu.CompilerParams(vmem_limit_bytes=20 << 20),
+        compiler_params=pltpu.CompilerParams(vmem_limit_bytes=46 << 20),
         cost_estimate=pl.CostEstimate(flops=2 * 10**9, bytes_accessed=2**20, transcendentals=0),
         name="pairs",
     )(flags, times, r_shots, *s_shots)
@@ -197,13 +197,8 @@
     theirs = from_offset(lax.dynamic_index_in_dim(lists, 1 - c, 2, keepdims=False), dc=1)
 
     native = lax.optimization_barrier(jnp.transpose(signals, (1, 0, 2)))
-    windows = [lax.dynamic_index_in_dim(native, x, 0, keepdims=False)]
-    for dx in (1, 2, 3):
-        windows.append(from_offset(lax.dynamic_index_in_dim(native, (x - dx) % 4, 0, keepdims=False), dx=dx))
-    windows = jnp.stack(windows + windows)
-    own = lax.dynamic_slice_in_dim(windows, (4 - x) % 4, 4, 0).reshape(4 * length_win, stations)
+    own = lax.all_to_all(native, "x", 0, 0, tiled=True).reshape(4 * length_win, stations)
     r_shots = lax.all_gather(native, ("c", "x"), axis=0).reshape(2, 4, group, length_win, stations)
-    own, mine, theirs = lax.optimization_barrier((own, mine, theirs))
 
     held = {(0, 0): own}
     blocks = []
@@ -235,9 +230,9 @@
     flags, times = meet(0, (flags, times))
 
     travel(1)
-    blocks += meet(1, [made_of(0, 5)])
+    blocks += meet(1, [made_of(0, 4)])
     travel(2)
-    blocks += meet(2, [made_of(5, 4)])
+    blocks += meet(2, [made_of(4, 5)])
     travel(3)
     blocks += meet(3, [made_of(9, 4)])
     blocks.append(made_of(13, 3))

time: 179 us -> 171 us (0.955)
  waiting for transfers between devices: 39.4 us -> 6.41 us
  blocking collectives: 13.8 us -> 36.7 us
  local copies, waits for them, and re-layouts: 14.8 us -> 8.09 us
  Pallas kernels: 66.3 us -> 70.5 us
  starting transfers between devices: 25.4 us -> 27.3 us
    ppermute x19 -> x16, waiting for transfers between devices: 39.4 us -> 4.99 us  [from_offset(): return lax.ppermute(value, AXES, pairs)]
    all_to_all x0 -> x1, blocking collectives: none -> 19.9 us  [body(): lax.all_to_all(native, 'x', 0, 0, tiled=True)]
    unnamed x22 -> x8, local copies, waits for them, and re-layouts: 8.85 us -> 4.31 us
    pallas_call x4, Pallas kernels: 60.6 us -> 64.7 us  [predict(): pl.pallas_call(functools.partial(pair_kernel, first_s, count_s), grid_spe...]
    all_to_all x1, blocking collectives: 13.8 us -> 16.7 us  [body(): made = lax.all_to_all(made, ('c', 'x'), 0, 0, tiled=True)]
    squeeze x1 -> x0, local copies, waits for them, and re-layouts: 2.09 us -> none  [body(): lax.dynamic_index_in_dim(native, (x - dx) % 4, 0, keepdims=False)]
    ppermute x19 -> x16, starting transfers between devices: 25.4 us -> 27.3 us  [from_offset(): return lax.ppermute(value, AXES, pairs)]
  transfers between devices with their start and end apart: 20 -> 17, of which waited for: 10 -> 4; matrix products, arithmetic and copies ran while one was open for 5% -> 4% of each run, Pallas kernels for 31% -> 35%
where the time goes in v3:
time: 171 us; the launch traced here: 170 us
  Pallas kernels  70.5 us (41%)
  blocking collectives  36.7 us (21%)
  starting transfers between devices  27.3 us (16%)
  between operations  13.6 us (8%)
  local copies, waits for them, and re-layouts  8.09 us (5%)
  other arithmetic  7.07 us (4%)
  waiting for transfers between devices  6.41 us (4%)
    pallas_call x4, Pallas kernels, predict(): pl.pallas_call(functools.partial(pair_kernel, first_s, count_s), grid_spe...  64.7 us
    ppermute x16, starting transfers between devices, from_offset(): return lax.ppermute(value, AXES, pairs)  27.3 us
    all_to_all x1, blocking collectives, body(): lax.all_to_all(native, 'x', 0, 0, tiled=True)  19.9 us
    all_to_all x1, blocking collectives, body(): made = lax.all_to_all(made, ('c', 'x'), 0, 0, tiled=True)  16.7 us
    pallas_call x1, Pallas kernels, station_counts(): pl.pallas_call(count_kernel, grid=(count_r,), in_specs=[pl.BlockSpec((1,...  5.75 us
    ppermute x16, waiting for transfers between devices, from_offset(): return lax.ppermute(value, AXES, pairs)  4.99 us
    unnamed x8, local copies, waits for them, and re-layouts  4.31 us
    reduce_max x2, other arithmetic, body(): odd = jnp.max((whole & whole - 1 != 0).astype(jnp.int32), axis=3)  3.56 us
  transfers between devices with their start and end apart: 17, of which 4 were waited for; matrix products, arithmetic and copies ran while one was open for 4% of the time, Pallas kernels for 35%

profile of v3, /device:TPU:1, one launch (start us, length us, event | category | flops | bytes accessed | tf_op | source)
XLA Modules:
  0.0 169.6 jit_solution(9787953263253898694)
XLA Ops:
  6.5 2.8 %copy.21 = bf16[64,4,2048]{2,0,1:T(8,128)(2,1)} copy(bf16[64,4,2048]{2,1,0:T(4,128)(2,1)} %param.5) | data formatting | bytes 2097152 | tf_op args[0]
  9.4 19.9 %all_to_all.10 = bf16[4,64,2048]{2,1,0:T(8,128)(2,1)S(1)} all-to-all(bf16[4,64,2048]{2,1,0:T(8,128)(2,1)} %bitcast.54), channel_id=1, replica_groups=mesh['z'=4,'y'=4,'c'=2,'x'=4] {'x'}, dimensions={0} | all-to-all | bytes 2097152 | tf_op jit(solution)/shard_map/all_to_all | solution.py:200
  29.3 3.0 %collective-permute-start = (bf16[256,2048]{1,0:T(8,128)(2,1)S(1)}, bf16[256,2048]{1,0:T(8,128)(2,1)S(1)}, u32[]{:S(2)}, u32[]{:S(2)}) collective-permute-start(bf16[256,2048]{1,0:T(8,128)(2,1)S(1)} %bitcast.43), channel_id=1, source_target_pairs={{8,0},{9,1},{10,2},{11,3},{12,4},{13,5},{14,6},{15,7},{16,8},{17,9... | collective-permute-start | bytes 3145736 | tf_op jit(solution)/shard_map/ppermute | solution.py:32
  32.2 4.9 %collective-permute-start.2 = (bf16[256,2048]{1,0:T(8,128)(2,1)S(1)}, bf16[256,2048]{1,0:T(8,128)(2,1)}, u32[]{:S(2)}, u32[]{:S(2)}) collective-permute-start(bf16[256,2048]{1,0:T(8,128)(2,1)S(1)} %bitcast.45), channel_id=1, source_target_pairs={{32,0},{33,1},{34,2},{35,3},{36,4},{37,5},{38,6},{39,7},{40,8},{41... | collective-permute-start | bytes 3145736 | tf_op jit(solution)/shard_map/ppermute | solution.py:32
  37.1 1.1 fusion.1
  38.3 5.5 %collective-permute-start.4 = (s32[4,16,128]{2,1,0:T(8,128)S(1)}, s32[4,16,128]{2,1,0:T(8,128)S(1)}, u32[]{:S(2)}, u32[]{:S(2)}) collective-permute-start(s32[4,16,128]{2,1,0:T(8,128)S(1)} %bitcast.63), channel_id=1, source_target_pairs={{4,0},{5,1},{6,2},{7,3},{0,4},{1,5},{2,6},{3,7},{12,8},{13,9},{14,... | collective-permute-start | bytes 98312 | tf_op jit(solution)/shard_map/ppermute | solution.py:32
  44.6 1.2 gather_fusion
  45.8 5.7 %station_counts.1.times_ref = f32[8,16,16,128]{3,2,1,0:T(8,128)} custom-call(s32[8,16,128]{2,1,0:T(8,128)} %bitcast.62), custom_call_target="tpu_custom_call" | custom-call | flops 1000000000 | bytes 1048576 | tf_op jit(solution)/shard_map/station_counts/pallas_call | solution.py:59
  51.6 3.5 %convert_reduce_fusion = s32[8,16,16]{2,1,0:T(8,128)S(1)} fusion(f32[8,16,16,128]{3,2,1,0:T(8,128)} %station_counts.1.times_ref), kind=kLoop, calls=%fused_computation.5 | loop fusion | flops 1570816 | bytes 1056768 | tf_op jit(solution)/shard_map/reduce_max | solution.py:228
  55.3 2.4 %collective-permute-done.3.refs_0_ = bf16[256,2048]{1,0:T(8,128)(2,1)} collective-permute-done((bf16[256,2048]{1,0:T(8,128)(2,1)S(1)}, bf16[256,2048]{1,0:T(8,128)(2,1)}, u32[]{:S(2)}, u32[]{:S(2)}) %collective-permute-start.3) | collective-permute-done | bytes 1048608 | tf_op jit(solution)/shard_map/ppermute | solution.py:32
  57.7 2.4 %collective-permute-start.5 = (bf16[256,2048]{1,0:T(8,128)(2,1)}, bf16[256,2048]{1,0:T(8,128)(2,1)}, u32[]{:S(2)}, u32[]{:S(2)}) collective-permute-start(bf16[256,2048]{1,0:T(8,128)(2,1)} %collective-permute-done.2.refs_3_), channel_id=1, source_target_pairs={{8,0},{9,1},{10,2},{11,3},{12,4},{13,5},{14,6},{15,7},{16,8},{17,9... | collective-permute-start | bytes 3145736 | tf_op jit(solution)/shard_map/ppermute | solution.py:32
  60.1 1.1 collective-permute-start.7
  61.6 2.3 %collective-permute-start.11 = (bf16[256,2048]{1,0:T(8,128)(2,1)}, bf16[256,2048]{1,0:T(8,128)(2,1)}, u32[]{:S(2)}, u32[]{:S(2)}) collective-permute-start(bf16[256,2048]{1,0:T(8,128)(2,1)} %collective-permute-done.2.refs_3_), channel_id=1, source_target_pairs={{32,0},{33,1},{34,2},{35,3},{36,4},{37,5},{38,6},{39,7},{40,8},{41... | collective-permute-start | bytes 3145736 | tf_op jit(solution)/shard_map/ppermute | solution.py:32
  63.9 1.4 all-gather.3.cloned.1.call-done
  65.3 1.2 copy-done
  66.5 16.3 %pairs.4 = f32[8,4,2,128]{3,2,1,0:T(2,128)S(1)} custom-call(s32[8,16]{1,0:T(8,128)S(1)} %shift-left_reduce_fusion.flag_ref, f32[8,16,16,128]{3,2,1,0:T(8,128)S(1)} %copy-done, bf16[2,4,4,64,2048]{4,3,2,1,0:T(8,128)(2,1)} %bitcast.48, bf16[256,2048]{1,0:T(8,128)(2,1)S(1)} %bitcast.47, bf16[256,2048]{1,0:T(8,128)(2,1)S(1)} %collective-permute-done.refs_1_, ...), custom_call_target="tpu_custom_call" | custom-call | flops 2000000000 | bytes 1048576 | tf_op jit(solution)/shard_map/pairs/pallas_call | solution.py:177
  82.8 2.1 %collective-permute-start.9 = (bf16[256,2048]{1,0:T(8,128)(2,1)S(1)}, bf16[256,2048]{1,0:T(8,128)(2,1)S(1)}, u32[]{:S(2)}, u32[]{:S(2)}) collective-permute-start(bf16[256,2048]{1,0:T(8,128)(2,1)S(1)} %collective-permute-done.refs_1_), channel_id=1, source_target_pairs={{8,0},{9,1},{10,2},{11,3},{12,4},{13,5},{14,6},{15,7},{16,8},{17,9... | collective-permute-start | bytes 3145736 | tf_op jit(solution)/shard_map/ppermute | solution.py:32
  85.0 2.2 %collective-permute-start.12 = (bf16[256,2048]{1,0:T(8,128)(2,1)}, bf16[256,2048]{1,0:T(8,128)(2,1)S(1)}, u32[]{:S(2)}, u32[]{:S(2)}) collective-permute-start(bf16[256,2048]{1,0:T(8,128)(2,1)} %collective-permute-done.8.refs_4_), channel_id=1, source_target_pairs={{96,0},{97,1},{98,2},{99,3},{100,4},{101,5},{102,6},{103,7},{104,8... | collective-permute-start | bytes 3145736 | tf_op jit(solution)/shard_map/ppermute | solution.py:32
  87.1 19.7 %pairs.5 = f32[8,5,2,128]{3,2,1,0:T(2,128)S(1)} custom-call(s32[8,16]{1,0:T(8,128)S(1)} %shift-left_reduce_fusion.flag_ref, f32[8,16,16,128]{3,2,1,0:T(8,128)S(1)} %copy-done.1, bf16[2,4,4,64,2048]{4,3,2,1,0:T(8,128)(2,1)} %bitcast.49, bf16[256,2048]{1,0:T(8,128)(2,1)} %collective-permute-done.3.refs_0_, bf16[256,2048]{1,0:T(8,128)(2,1)} %collective-permute-done.5.refs_1_, ...), custom_call_target="tpu_custom_call" | custom-call | flops 2000000000 | bytes 1048576 | tf_op jit(solution)/shard_map/pairs/pallas_call | solution.py:177
  107.1 3.3 %collective-permute-start.13 = (bf16[256,2048]{1,0:T(8,128)(2,1)S(1)}, bf16[256,2048]{1,0:T(8,128)(2,1)S(1)}, u32[]{:S(2)}, u32[]{:S(2)}) collective-permute-start(bf16[256,2048]{1,0:T(8,128)(2,1)S(1)} %collective-permute-done.12.refs_3_), channel_id=1, source_target_pairs={{8,0},{9,1},{10,2},{11,3},{12,4},{13,5},{14,6},{15,7},{16,8},{17,9... | collective-permute-start | bytes 3145736 | tf_op jit(solution)/shard_map/ppermute | solution.py:32
  111.1 17.0 %pairs.6 = f32[8,4,2,128]{3,2,1,0:T(2,128)S(1)} custom-call(s32[8,16]{1,0:T(8,128)S(1)} %shift-left_reduce_fusion.flag_ref, f32[8,16,16,128]{3,2,1,0:T(8,128)S(1)} %copy-done.1, bf16[2,4,4,64,2048]{4,3,2,1,0:T(8,128)(2,1)} %bitcast.50, bf16[256,2048]{1,0:T(8,128)(2,1)S(1)} %collective-permute-done.9.refs_0_, ...), custom_call_target="tpu_custom_call" | custom-call | flops 2000000000 | bytes 1048576 | tf_op jit(solution)/shard_map/pairs/pallas_call | solution.py:177
  128.1 2.4 %collective-permute-done.15.refs_2_ = bf16[256,2048]{1,0:T(8,128)(2,1)S(1)} collective-permute-done((bf16[256,2048]{1,0:T(8,128)(2,1)}, bf16[256,2048]{1,0:T(8,128)(2,1)S(1)}, u32[]{:S(2)}, u32[]{:S(2)}) %collective-permute-start.15) | collective-permute-done | bytes 1048608 | tf_op jit(solution)/shard_map/ppermute | solution.py:32
  130.6 11.7 %pairs.7 = f32[8,3,2,128]{3,2,1,0:T(2,128)S(1)} custom-call(s32[8,16]{1,0:T(8,128)S(1)} %shift-left_reduce_fusion.flag_ref, f32[8,16,16,128]{3,2,1,0:T(8,128)S(1)} %copy-done.1, bf16[2,4,4,64,2048]{4,3,2,1,0:T(8,128)(2,1)} %bitcast.51, bf16[256,2048]{1,0:T(8,128)(2,1)S(1)} %collective-permute-done.13.refs_0_, ...), custom_call_target="tpu_custom_call" | custom-call | flops 2000000000 | bytes 1048576 | tf_op jit(solution)/shard_map/pairs/pallas_call | solution.py:177
  143.5 16.7 %all_to_all.11 = f32[8,1,4096]{2,1,0:T(1,128)S(1)} all-to-all(f32[8,1,4096]{2,1,0:T(1,128)S(1)} %reshape.122), channel_id=1, replica_groups=mesh['z'=4,'y'=4,'c'=2,'x'=4] {'c','x'}, dimensions={0} | all-to-all | bytes 262144 | tf_op jit(solution)/shard_map/all_to_all | solution.py:244
  (46 shorter events, 6.2 us)
Async XLA Ops:
  6.5 58.7 %all-gather.3.cloned.1.call-start = ((), (), s32[]{:S(2)}) async-start(), calls=%async_computation.2 | async-start | bytes 9437184 | tf_op jit(solution)/shard_map/all_gather | solution.py:201
  29.3 26.0 %collective-permute-start = (bf16[256,2048]{1,0:T(8,128)(2,1)S(1)}, bf16[256,2048]{1,0:T(8,128)(2,1)S(1)}, u32[]{:S(2)}, u32[]{:S(2)}) collective-permute-start(bf16[256,2048]{1,0:T(8,128)(2,1)S(1)} %bitcast.43), channel_id=1, source_target_pairs={{8,0},{9,1},{10,2},{11,3},{12,4},{13,5},{14,6},{15,7},{16,8},{17,9... | collective-permute-start | bytes 3145736 | tf_op jit(solution)/shard_map/ppermute | solution.py:32
  32.2 23.0 %collective-permute-start.1 = (bf16[256,2048]{1,0:T(8,128)(2,1)S(1)}, bf16[256,2048]{1,0:T(8,128)(2,1)}, u32[]{:S(2)}, u32[]{:S(2)}) collective-permute-start(bf16[256,2048]{1,0:T(8,128)(2,1)S(1)} %bitcast.44), channel_id=1, source_target_pairs={{24,0},{25,1},{26,2},{27,3},{28,4},{29,5},{30,6},{31,7},{0,8},{1,9... | collective-permute-start | bytes 3145736 | tf_op jit(solution)/shard_map/ppermute | solution.py:32
  32.2 23.1 %collective-permute-start.2 = (bf16[256,2048]{1,0:T(8,128)(2,1)S(1)}, bf16[256,2048]{1,0:T(8,128)(2,1)}, u32[]{:S(2)}, u32[]{:S(2)}) collective-permute-start(bf16[256,2048]{1,0:T(8,128)(2,1)S(1)} %bitcast.45), channel_id=1, source_target_pairs={{32,0},{33,1},{34,2},{35,3},{36,4},{37,5},{38,6},{39,7},{40,8},{41... | collective-permute-start | bytes 3145736 | tf_op jit(solution)/shard_map/ppermute | solution.py:32
  37.1 20.6 %collective-permute-start.3 = (bf16[256,2048]{1,0:T(8,128)(2,1)S(1)}, bf16[256,2048]{1,0:T(8,128)(2,1)}, u32[]{:S(2)}, u32[]{:S(2)}) collective-permute-start(bf16[256,2048]{1,0:T(8,128)(2,1)S(1)} %bitcast.46), channel_id=1, source_target_pairs={{96,0},{97,1},{98,2},{99,3},{100,4},{101,5},{102,6},{103,7},{104,8... | collective-permute-start | bytes 3145736 | tf_op jit(solution)/shard_map/ppermute | solution.py:32
  38.3 6.3 %collective-permute-start.4 = (s32[4,16,128]{2,1,0:T(8,128)S(1)}, s32[4,16,128]{2,1,0:T(8,128)S(1)}, u32[]{:S(2)}, u32[]{:S(2)}) collective-permute-start(s32[4,16,128]{2,1,0:T(8,128)S(1)} %bitcast.63), channel_id=1, source_target_pairs={{4,0},{5,1},{6,2},{7,3},{0,4},{1,5},{2,6},{3,7},{12,8},{13,9},{14,... | collective-permute-start | bytes 98312 | tf_op jit(solution)/shard_map/ppermute | solution.py:32
  51.6 35.6 %copy-start.1 = (f32[8,16,16,128]{3,2,1,0:T(8,128)S(1)}, f32[8,16,16,128]{3,2,1,0:T(8,128)}, u32[]{:S(2)}) copy-start(f32[8,16,16,128]{3,2,1,0:T(8,128)} %station_counts.1.times_ref) | copy-start | bytes 3145732
  57.7 25.1 %collective-permute-start.5 = (bf16[256,2048]{1,0:T(8,128)(2,1)}, bf16[256,2048]{1,0:T(8,128)(2,1)}, u32[]{:S(2)}, u32[]{:S(2)}) collective-permute-start(bf16[256,2048]{1,0:T(8,128)(2,1)} %collective-permute-done.2.refs_3_), channel_id=1, source_target_pairs={{8,0},{9,1},{10,2},{11,3},{12,4},{13,5},{14,6},{15,7},{16,8},{17,9... | collective-permute-start | bytes 3145736 | tf_op jit(solution)/shard_map/ppermute | solution.py:32
  60.1 24.8 %collective-permute-start.6 = (bf16[256,2048]{1,0:T(8,128)(2,1)}, bf16[256,2048]{1,0:T(8,128)(2,1)}, u32[]{:S(2)}, u32[]{:S(2)}) collective-permute-start(bf16[256,2048]{1,0:T(8,128)(2,1)} %collective-permute-done.3.refs_0_), channel_id=1, source_target_pairs={{24,0},{25,1},{26,2},{27,3},{28,4},{29,5},{30,6},{31,7},{0,8},{1,9... | collective-permute-start | bytes 3145736 | tf_op jit(solution)/shard_map/ppermute | solution.py:32
  60.1 24.8 %collective-permute-start.7 = (bf16[256,2048]{1,0:T(8,128)(2,1)}, bf16[256,2048]{1,0:T(8,128)(2,1)}, u32[]{:S(2)}, u32[]{:S(2)}) collective-permute-start(bf16[256,2048]{1,0:T(8,128)(2,1)} %collective-permute-done.1.refs_2_), channel_id=1, source_target_pairs={{32,0},{33,1},{34,2},{35,3},{36,4},{37,5},{38,6},{39,7},{40,8},{41... | collective-permute-start | bytes 3145736 | tf_op jit(solution)/shard_map/ppermute | solution.py:32
  61.2 23.7 %collective-permute-start.8 = (bf16[256,2048]{1,0:T(8,128)(2,1)S(1)}, bf16[256,2048]{1,0:T(8,128)(2,1)}, u32[]{:S(2)}, u32[]{:S(2)}) collective-permute-start(bf16[256,2048]{1,0:T(8,128)(2,1)S(1)} %collective-permute-done.refs_1_), channel_id=1, source_target_pairs={{96,0},{97,1},{98,2},{99,3},{100,4},{101,5},{102,6},{103,7},{104,8... | collective-permute-start | bytes 3145736 | tf_op jit(solution)/shard_map/ppermute | solution.py:32
  61.6 45.3 %collective-permute-start.11 = (bf16[256,2048]{1,0:T(8,128)(2,1)}, bf16[256,2048]{1,0:T(8,128)(2,1)}, u32[]{:S(2)}, u32[]{:S(2)}) collective-permute-start(bf16[256,2048]{1,0:T(8,128)(2,1)} %collective-permute-done.2.refs_3_), channel_id=1, source_target_pairs={{32,0},{33,1},{34,2},{35,3},{36,4},{37,5},{38,6},{39,7},{40,8},{41... | collective-permute-start | bytes 3145736 | tf_op jit(solution)/shard_map/ppermute | solution.py:32
  65.3 1.2 copy-start
  82.8 24.3 %collective-permute-start.9 = (bf16[256,2048]{1,0:T(8,128)(2,1)S(1)}, bf16[256,2048]{1,0:T(8,128)(2,1)S(1)}, u32[]{:S(2)}, u32[]{:S(2)}) collective-permute-start(bf16[256,2048]{1,0:T(8,128)(2,1)S(1)} %collective-permute-done.refs_1_), channel_id=1, source_target_pairs={{8,0},{9,1},{10,2},{11,3},{12,4},{13,5},{14,6},{15,7},{16,8},{17,9... | collective-permute-start | bytes 3145736 | tf_op jit(solution)/shard_map/ppermute | solution.py:32
  84.9 22.2 %collective-permute-start.10 = (bf16[256,2048]{1,0:T(8,128)(2,1)}, bf16[256,2048]{1,0:T(8,128)(2,1)S(1)}, u32[]{:S(2)}, u32[]{:S(2)}) collective-permute-start(bf16[256,2048]{1,0:T(8,128)(2,1)} %collective-permute-done.6.refs_2_), channel_id=1, source_target_pairs={{24,0},{25,1},{26,2},{27,3},{28,4},{29,5},{30,6},{31,7},{0,8},{1,9... | collective-permute-start | bytes 3145736 | tf_op jit(solution)/shard_map/ppermute | solution.py:32
  85.0 22.2 %collective-permute-start.12 = (bf16[256,2048]{1,0:T(8,128)(2,1)}, bf16[256,2048]{1,0:T(8,128)(2,1)S(1)}, u32[]{:S(2)}, u32[]{:S(2)}) collective-permute-start(bf16[256,2048]{1,0:T(8,128)(2,1)} %collective-permute-done.8.refs_4_), channel_id=1, source_target_pairs={{96,0},{97,1},{98,2},{99,3},{100,4},{101,5},{102,6},{103,7},{104,8... | collective-permute-start | bytes 3145736 | tf_op jit(solution)/shard_map/ppermute | solution.py:32
  87.1 41.0 %collective-permute-start.14 = (bf16[256,2048]{1,0:T(8,128)(2,1)}, bf16[256,2048]{1,0:T(8,128)(2,1)S(1)}, u32[]{:S(2)}, u32[]{:S(2)}) collective-permute-start(bf16[256,2048]{1,0:T(8,128)(2,1)} %collective-permute-done.7.refs_3_), channel_id=1, source_target_pairs={{24,0},{25,1},{26,2},{27,3},{28,4},{29,5},{30,6},{31,7},{0,8},{1,9... | collective-permute-start | bytes 3145736 | tf_op jit(solution)/shard_map/ppermute | solution.py:32
  106.9 23.7 %collective-permute-start.15 = (bf16[256,2048]{1,0:T(8,128)(2,1)}, bf16[256,2048]{1,0:T(8,128)(2,1)S(1)}, u32[]{:S(2)}, u32[]{:S(2)}) collective-permute-start(bf16[256,2048]{1,0:T(8,128)(2,1)} %collective-permute-done.6.refs_2_), channel_id=1, source_target_pairs={{96,0},{97,1},{98,2},{99,3},{100,4},{101,5},{102,6},{103,7},{104,8... | collective-permute-start | bytes 3145736 | tf_op jit(solution)/shard_map/ppermute | solution.py:32
  107.1 23.4 %collective-permute-start.13 = (bf16[256,2048]{1,0:T(8,128)(2,1)S(1)}, bf16[256,2048]{1,0:T(8,128)(2,1)S(1)}, u32[]{:S(2)}, u32[]{:S(2)}) collective-permute-start(bf16[256,2048]{1,0:T(8,128)(2,1)S(1)} %collective-permute-done.12.refs_3_), channel_id=1, source_target_pairs={{8,0},{9,1},{10,2},{11,3},{12,4},{13,5},{14,6},{15,7},{16,8},{17,9... | collective-permute-start | bytes 3145736 | tf_op jit(solution)/shard_map/ppermute | solution.py:32
Sparse Core Ops, SparseCore 0:
  9.5 55.7 all-gather.2

commit v4 on v3

--- a/solution.py
+++ b/solution.py
@@ -13,6 +13,7 @@
 AXES = ("z", "y", "c", "x")
 SIZES = (4, 4, 2, 4)
 LANES = 128
+GRANT = 46
 NT_DIMS = (((1,), (1,)), ((), ()))
 
 ROUNDS = (
@@ -85,8 +86,7 @@
     length, stations = s_refs[0].shape
     _, windows, group, window_len, _ = r_ref.shape
     chunks = stations // LANES
-    r = pl.program_id(0)
-    slot = lax.rem(r, 2)
+    count_r = flag_ref.shape[0]
 
     def fetches(number, to):
         for w in range(windows):
@@ -96,76 +96,84 @@
                 sems.at[to, w],
             )
 
-    @pl.when(r == 0)
-    def _():
-        for fetch in fetches(r, 0):
-            fetch.start()
-
-    @pl.when(r + 1 < pl.num_programs(0))
-    def _():
-        for fetch in fetches(r + 1, 1 - slot):
-            fetch.start()
-
-    for fetch in fetches(r, slot):
-        fetch.wait()
-
-    for s in range(count_s):
-        for c in range(chunks):
-            cols = slice(c * LANES, (c + 1) * LANES)
-            times = jnp.broadcast_to(times_ref[0, first_s + s, c : c + 1, :], (16, LANES)).astype(jnp.bfloat16)
-            times = jnp.concatenate([times] * (length // 16), axis=0)
-            scaled[s * length : (s + 1) * length, cols] = s_refs[s][:, cols] * times
-    outer[...] = lax.dot_general(scaled[...], r_buf[slot], NT_DIMS, preferred_element_type=jnp.float32)
-    for s in range(count_s):
-        first, second = antidiagonals(outer[s * length : (s + 1) * length, :])
-        out_ref[0, s, 0:1, :] = first
-        out_ref[0, s, 1:2, :] = second
-
-    for s in range(count_s):
-        rows = slice(s * length, (s + 1) * length)
-        flag = flag_ref[r, first_s + s]
-
-        @pl.when(flag != 0)
+    for fetch in fetches(0, 0):
+        fetch.start()
+
+    def products(r, carry):
+        slot = lax.rem(r, 2)
+
+        @pl.when(r + 1 < count_r)
         def _():
-            rest[...] = jnp.zeros_like(rest)
-
-            def one(pair, carry):
-                @pl.when((flag >> pair) & 1 != 0)
+            for fetch in fetches(r + 1, 1 - slot):
+                fetch.start()
+
+        for fetch in fetches(r, slot):
+            fetch.wait()
+
+        for s in range(count_s):
+            for c in range(chunks):
+                cols = slice(c * LANES, (c + 1) * LANES)
+                times = jnp.broadcast_to(times_ref[r, first_s + s, c : c + 1, :], (16, LANES)).astype(jnp.bfloat16)
+                times = jnp.concatenate([times] * (length // 16), axis=0)
+                scaled[s * length : (s + 1) * length, cols] = s_refs[s][:, cols] * times
+        outer[...] = lax.dot_general(scaled[...], r_buf[slot], NT_DIMS, preferred_element_type=jnp.float32)
+        for s in range(count_s):
+            first, second = antidiagonals(outer[s * length : (s + 1) * length, :])
+            out_ref[r, s, 0:1, :] = first
+            out_ref[r, s, 1:2, :] = second
+
+        odd = flag_ref[r, first_s]
+        for s in range(1, count_s):
+            odd = odd | flag_ref[r, first_s + s]
+
+        @pl.when(odd != 0)
+        def _():
+            for s in range(count_s):
+                rows = slice(s * length, (s + 1) * length)
+                flag = flag_ref[r, first_s + s]
+
+                @pl.when(flag != 0)
                 def _():
-                    parts = []
-                    for half in range(2):
-                        cols = pl.ds(pl.multiple_of((pair * 2 + half) * LANES, LANES), LANES)
-                        times = times_ref[0, first_s + s, pl.ds(pair * 2 + half, 1), :]
-                        whole = s_refs[s][:, cols].astype(jnp.float32) * jnp.broadcast_to(times, (length, LANES))
-                        parts.append((whole - scaled[rows, cols].astype(jnp.float32)).astype(jnp.bfloat16))
-                    both = pl.ds(pl.multiple_of(pair * 2 * LANES, 2 * LANES), 2 * LANES)
-                    rest[...] += lax.dot_general(
-                        jnp.concatenate(parts, axis=1),
-                        r_buf[slot, :, both],
-                        NT_DIMS,
-                        preferred_element_type=jnp.float32,
-                    )
-
-                return carry
-
-            lax.fori_loop(0, chunks // 2, one, 0)
-            first, second = antidiagonals(rest[...])
-            out_ref[0, s, 0:1, :] += first
-            out_ref[0, s, 1:2, :] += second
+                    rest[...] = jnp.zeros_like(rest)
+
+                    def one(pair, carry):
+                        @pl.when((flag >> pair) & 1 != 0)
+                        def _():
+                            parts = []
+                            for half in range(2):
+                                cols = pl.ds(pl.multiple_of((pair * 2 + half) * LANES, LANES), LANES)
+                                times = times_ref[r, first_s + s, pl.ds(pair * 2 + half, 1), :]
+                                whole = s_refs[s][:, cols].astype(jnp.float32) * jnp.broadcast_to(times, (length, LANES))
+                                parts.append((whole - scaled[rows, cols].astype(jnp.float32)).astype(jnp.bfloat16))
+                            both = pl.ds(pl.multiple_of(pair * 2 * LANES, 2 * LANES), 2 * LANES)
+                            rest[...] += lax.dot_general(
+                                jnp.concatenate(parts, axis=1),
+                                r_buf[slot, :, both],
+                                NT_DIMS,
+                                preferred_element_type=jnp.float32,
+                            )
+
+                        return carry
+
+                    lax.fori_loop(0, chunks // 2, one, 0)
+                    first, second = antidiagonals(rest[...])
+                    out_ref[r, s, 0:1, :] += first
+                    out_ref[r, s, 1:2, :] += second
+
+        return carry
+
+    lax.fori_loop(0, count_r, products, 0)
 
 
 def predict(flags, times, r_shots, s_shots, first_s):
     count_r, count_s = flags.shape[0], len(s_shots)
     length, stations = s_shots[0].shape
-    grid_spec = pltpu.PrefetchScalarGridSpec(
-        num_scalar_prefetch=1,
-        grid=(count_r,),
-        in_specs=[
-            pl.BlockSpec((1,) + times.shape[1:], lambda i, f: (i, 0, 0, 0)),
-            pl.BlockSpec(memory_space=pl.ANY),
-        ]
-        + [pl.BlockSpec((length, stations), lambda i, f: (0, 0), pipeline_mode=pl.Buffered(1))] * count_s,
-        out_specs=pl.BlockSpec((1, count_s, 2, LANES), lambda i, f: (i, 0, 0, 0)),
+    on_chip = pl.BlockSpec(memory_space=pltpu.VMEM)
+    return pl.pallas_call(
+        functools.partial(pair_kernel, first_s, count_s),
+        in_specs=[pl.BlockSpec(memory_space=pltpu.SMEM), on_chip, pl.BlockSpec(memory_space=pltpu.HBM)]
+        + [on_chip] * count_s,
+        out_specs=on_chip,
         scratch_shapes=[
             pltpu.VMEM((count_s * length, stations), jnp.bfloat16),
             pltpu.VMEM((count_s * length, length), jnp.float32),
@@ -173,12 +181,8 @@
             pltpu.VMEM((2, length, stations), jnp.bfloat16),
             pltpu.SemaphoreType.DMA((2, 4)),
         ],
-    )
-    return pl.pallas_call(
-        functools.partial(pair_kernel, first_s, count_s),
-        grid_spec=grid_spec,
         out_shape=jax.ShapeDtypeStruct((count_r, count_s, 2, LANES), jnp.float32),
-        compiler_params=pltpu.CompilerParams(vmem_limit_bytes=46 << 20),
+        compiler_params=pltpu.CompilerParams(vmem_limit_bytes=GRANT << 20),
         cost_estimate=pl.CostEstimate(flops=2 * 10**9, bytes_accessed=2**20, transcendentals=0),
         name="pairs",
     )(flags, times, r_shots, *s_shots)
@@ -227,7 +231,7 @@
     whole = times.astype(jnp.int32).reshape(2 * group, 16, 8, 2 * LANES)
     odd = jnp.max((whole & (whole - 1) != 0).astype(jnp.int32), axis=3)
     flags = jnp.sum(odd << jnp.arange(8, dtype=jnp.int32), axis=2)
-    flags, times = meet(0, (flags, times))
+    (flags,) = meet(0, (flags,))
 
     travel(1)
     blocks += meet(1, [made_of(0, 4)])

time: 171 us -> 169 us (0.988)
  Pallas kernels: 70.5 us -> 64.7 us
  waiting for transfers between devices: 6.41 us -> 10.4 us
    pallas_call x4, Pallas kernels: 64.7 us -> 59 us  [predict(): pl.pallas_call(functools.partial(pair_kernel, first_s, count_s), in_specs...]
    ppermute x16, waiting for transfers between devices: 4.99 us -> 9.01 us  [from_offset(): return lax.ppermute(value, AXES, pairs)]
  transfers between devices with their start and end apart: 17 -> 17, of which waited for: 4 -> 4; matrix products, arithmetic and copies ran while one was open for 4% -> 4% of each run, Pallas kernels for 35% -> 32%
where the time goes in v4:
time: 169 us; the launch traced here: 168 us
  Pallas kernels  64.7 us (38%)
  blocking collectives  35.9 us (21%)
  starting transfers between devices  28 us (17%)
  between operations  13.6 us (8%)
  waiting for transfers between devices  10.4 us (6%)
  local copies, waits for them, and re-layouts  8.09 us (5%)
  other arithmetic  7.07 us (4%)
    pallas_call x4, Pallas kernels, predict(): pl.pallas_call(functools.partial(pair_kernel, first_s, count_s), in_specs...  59 us
    ppermute x16, starting transfers between devices, from_offset(): return lax.ppermute(value, AXES, pairs)  28 us
    all_to_all x1, blocking collectives, body(): lax.all_to_all(native, 'x', 0, 0, tiled=True)  19.9 us
    all_to_all x1, blocking collectives, body(): made = lax.all_to_all(made, ('c', 'x'), 0, 0, tiled=True)  16 us
    ppermute x16, waiting for transfers between devices, from_offset(): return lax.ppermute(value, AXES, pairs)  9.01 us
    pallas_call x1, Pallas kernels, station_counts(): pl.pallas_call(count_kernel, grid=(count_r,), in_specs=[pl.BlockSpec((1,...  5.75 us
    unnamed x8, local copies, waits for them, and re-layouts  4.31 us
    reduce_max x2, other arithmetic, body(): odd = jnp.max((whole & whole - 1 != 0).astype(jnp.int32), axis=3)  3.56 us
  transfers between devices with their start and end apart: 17, of which 4 were waited for; matrix products, arithmetic and copies ran while one was open for 4% of the time, Pallas kernels for 32%

profile of v4, /device:TPU:1, one launch (start us, length us, event | category | flops | bytes accessed | tf_op | source)
XLA Modules:
  0.0 167.8 jit_solution(18074370336378820773)
XLA Ops:
  6.5 2.8 %copy.21 = bf16[64,4,2048]{2,0,1:T(8,128)(2,1)} copy(bf16[64,4,2048]{2,1,0:T(4,128)(2,1)} %param.5) | data formatting | bytes 2097152 | tf_op args[0]
  9.4 19.9 %all_to_all.10 = bf16[4,64,2048]{2,1,0:T(8,128)(2,1)S(1)} all-to-all(bf16[4,64,2048]{2,1,0:T(8,128)(2,1)} %bitcast.54), channel_id=1, replica_groups=mesh['z'=4,'y'=4,'c'=2,'x'=4] {'x'}, dimensions={0} | all-to-all | bytes 2097152 | tf_op jit(solution)/shard_map/all_to_all | solution.py:204
  29.3 3.0 %collective-permute-start = (bf16[256,2048]{1,0:T(8,128)(2,1)S(1)}, bf16[256,2048]{1,0:T(8,128)(2,1)S(1)}, u32[]{:S(2)}, u32[]{:S(2)}) collective-permute-start(bf16[256,2048]{1,0:T(8,128)(2,1)S(1)} %bitcast.43), channel_id=1, source_target_pairs={{8,0},{9,1},{10,2},{11,3},{12,4},{13,5},{14,6},{15,7},{16,8},{17,9... | collective-permute-start | bytes 3145736 | tf_op jit(solution)/shard_map/ppermute | solution.py:33
  32.2 4.9 %collective-permute-start.2 = (bf16[256,2048]{1,0:T(8,128)(2,1)S(1)}, bf16[256,2048]{1,0:T(8,128)(2,1)}, u32[]{:S(2)}, u32[]{:S(2)}) collective-permute-start(bf16[256,2048]{1,0:T(8,128)(2,1)S(1)} %bitcast.45), channel_id=1, source_target_pairs={{32,0},{33,1},{34,2},{35,3},{36,4},{37,5},{38,6},{39,7},{40,8},{41... | collective-permute-start | bytes 3145736 | tf_op jit(solution)/shard_map/ppermute | solution.py:33
  37.1 1.1 fusion.1
  38.3 5.5 %collective-permute-start.4 = (s32[4,16,128]{2,1,0:T(8,128)S(1)}, s32[4,16,128]{2,1,0:T(8,128)S(1)}, u32[]{:S(2)}, u32[]{:S(2)}) collective-permute-start(s32[4,16,128]{2,1,0:T(8,128)S(1)} %bitcast.63), channel_id=1, source_target_pairs={{4,0},{5,1},{6,2},{7,3},{0,4},{1,5},{2,6},{3,7},{12,8},{13,9},{14,... | collective-permute-start | bytes 98312 | tf_op jit(solution)/shard_map/ppermute | solution.py:33
  44.6 1.2 gather_fusion
  45.8 5.7 %station_counts.1.times_ref = f32[8,16,16,128]{3,2,1,0:T(8,128)} custom-call(s32[8,16,128]{2,1,0:T(8,128)} %bitcast.62), custom_call_target="tpu_custom_call" | custom-call | flops 1000000000 | bytes 1048576 | tf_op jit(solution)/shard_map/station_counts/pallas_call | solution.py:60
  51.6 3.5 %convert_reduce_fusion = s32[8,16,16]{2,1,0:T(8,128)S(1)} fusion(f32[8,16,16,128]{3,2,1,0:T(8,128)} %station_counts.1.times_ref), kind=kLoop, calls=%fused_computation.5 | loop fusion | flops 1570816 | bytes 1056768 | tf_op jit(solution)/shard_map/reduce_max | solution.py:232
  55.3 2.4 %collective-permute-done.3.refs_0_ = bf16[256,2048]{1,0:T(8,128)(2,1)} collective-permute-done((bf16[256,2048]{1,0:T(8,128)(2,1)S(1)}, bf16[256,2048]{1,0:T(8,128)(2,1)}, u32[]{:S(2)}, u32[]{:S(2)}) %collective-permute-start.3) | collective-permute-done | bytes 1048608 | tf_op jit(solution)/shard_map/ppermute | solution.py:33
  57.7 2.4 %collective-permute-start.5 = (bf16[256,2048]{1,0:T(8,128)(2,1)}, bf16[256,2048]{1,0:T(8,128)(2,1)}, u32[]{:S(2)}, u32[]{:S(2)}) collective-permute-start(bf16[256,2048]{1,0:T(8,128)(2,1)} %collective-permute-done.2.refs_3_), channel_id=1, source_target_pairs={{8,0},{9,1},{10,2},{11,3},{12,4},{13,5},{14,6},{15,7},{16,8},{17,9... | collective-permute-start | bytes 3145736 | tf_op jit(solution)/shard_map/ppermute | solution.py:33
  60.1 1.1 collective-permute-start.7
  61.6 2.3 %collective-permute-start.11 = (bf16[256,2048]{1,0:T(8,128)(2,1)}, bf16[256,2048]{1,0:T(8,128)(2,1)}, u32[]{:S(2)}, u32[]{:S(2)}) collective-permute-start(bf16[256,2048]{1,0:T(8,128)(2,1)} %collective-permute-done.2.refs_3_), channel_id=1, source_target_pairs={{32,0},{33,1},{34,2},{35,3},{36,4},{37,5},{38,6},{39,7},{40,8},{41... | collective-permute-start | bytes 3145736 | tf_op jit(solution)/shard_map/ppermute | solution.py:33
  63.9 1.4 all-gather.3.cloned.1.call-done
  65.3 1.2 copy-done
  66.5 15.0 %pairs.4 = f32[8,4,2,128]{3,2,1,0:T(2,128)S(1)} custom-call(s32[8,16]{1,0:T(8,128)S(1)} %shift-left_reduce_fusion.flag_ref, f32[8,16,16,128]{3,2,1,0:T(8,128)S(1)} %copy-done, bf16[2,4,4,64,2048]{4,3,2,1,0:T(8,128)(2,1)} %bitcast.48, bf16[256,2048]{1,0:T(8,128)(2,1)S(1)} %bitcast.47, bf16[256,2048]{1,0:T(8,128)(2,1)S(1)} %collective-permute-done.refs_1_, ...), custom_call_target="tpu_custom_call" | custom-call | flops 2000000000 | bytes 1048576 | tf_op jit(solution)/shard_map/pairs/pallas_call | solution.py:172
  81.5 2.3 %collective-permute-start.9 = (bf16[256,2048]{1,0:T(8,128)(2,1)S(1)}, bf16[256,2048]{1,0:T(8,128)(2,1)S(1)}, u32[]{:S(2)}, u32[]{:S(2)}) collective-permute-start(bf16[256,2048]{1,0:T(8,128)(2,1)S(1)} %collective-permute-done.refs_1_), channel_id=1, source_target_pairs={{8,0},{9,1},{10,2},{11,3},{12,4},{13,5},{14,6},{15,7},{16,8},{17,9... | collective-permute-start | bytes 3145736 | tf_op jit(solution)/shard_map/ppermute | solution.py:33
  83.9 2.7 %collective-permute-start.12 = (bf16[256,2048]{1,0:T(8,128)(2,1)}, bf16[256,2048]{1,0:T(8,128)(2,1)S(1)}, u32[]{:S(2)}, u32[]{:S(2)}) collective-permute-start(bf16[256,2048]{1,0:T(8,128)(2,1)} %collective-permute-done.8.refs_4_), channel_id=1, source_target_pairs={{96,0},{97,1},{98,2},{99,3},{100,4},{101,5},{102,6},{103,7},{104,8... | collective-permute-start | bytes 3145736 | tf_op jit(solution)/shard_map/ppermute | solution.py:33
  86.6 18.7 %pairs.5 = f32[8,5,2,128]{3,2,1,0:T(2,128)S(1)} custom-call(s32[8,16]{1,0:T(8,128)S(1)} %shift-left_reduce_fusion.flag_ref, f32[8,16,16,128]{3,2,1,0:T(8,128)S(1)} %copy-done.1, bf16[2,4,4,64,2048]{4,3,2,1,0:T(8,128)(2,1)} %bitcast.49, bf16[256,2048]{1,0:T(8,128)(2,1)} %collective-permute-done.3.refs_0_, bf16[256,2048]{1,0:T(8,128)(2,1)} %collective-permute-done.5.refs_1_, ...), custom_call_target="tpu_custom_call" | custom-call | flops 2000000000 | bytes 1048576 | tf_op jit(solution)/shard_map/pairs/pallas_call | solution.py:172
  106.0 2.7 %collective-permute-start.13 = (bf16[256,2048]{1,0:T(8,128)(2,1)S(1)}, bf16[256,2048]{1,0:T(8,128)(2,1)S(1)}, u32[]{:S(2)}, u32[]{:S(2)}) collective-permute-start(bf16[256,2048]{1,0:T(8,128)(2,1)S(1)} %collective-permute-done.12.refs_3_), channel_id=1, source_target_pairs={{8,0},{9,1},{10,2},{11,3},{12,4},{13,5},{14,6},{15,7},{16,8},{17,9... | collective-permute-start | bytes 3145736 | tf_op jit(solution)/shard_map/ppermute | solution.py:33
  109.5 14.2 %pairs.6 = f32[8,4,2,128]{3,2,1,0:T(2,128)S(1)} custom-call(s32[8,16]{1,0:T(8,128)S(1)} %shift-left_reduce_fusion.flag_ref, f32[8,16,16,128]{3,2,1,0:T(8,128)S(1)} %copy-done.1, bf16[2,4,4,64,2048]{4,3,2,1,0:T(8,128)(2,1)} %bitcast.50, bf16[256,2048]{1,0:T(8,128)(2,1)S(1)} %collective-permute-done.9.refs_0_, ...), custom_call_target="tpu_custom_call" | custom-call | flops 2000000000 | bytes 1048576 | tf_op jit(solution)/shard_map/pairs/pallas_call | solution.py:172
  123.7 6.4 %collective-permute-done.15.refs_2_ = bf16[256,2048]{1,0:T(8,128)(2,1)S(1)} collective-permute-done((bf16[256,2048]{1,0:T(8,128)(2,1)}, bf16[256,2048]{1,0:T(8,128)(2,1)S(1)}, u32[]{:S(2)}, u32[]{:S(2)}) %collective-permute-start.15) | collective-permute-done | bytes 1048608 | tf_op jit(solution)/shard_map/ppermute | solution.py:33
  130.2 11.1 %pairs.7 = f32[8,3,2,128]{3,2,1,0:T(2,128)S(1)} custom-call(s32[8,16]{1,0:T(8,128)S(1)} %shift-left_reduce_fusion.flag_ref, f32[8,16,16,128]{3,2,1,0:T(8,128)S(1)} %copy-done.1, bf16[2,4,4,64,2048]{4,3,2,1,0:T(8,128)(2,1)} %bitcast.51, bf16[256,2048]{1,0:T(8,128)(2,1)S(1)} %collective-permute-done.13.refs_0_, ...), custom_call_target="tpu_custom_call" | custom-call | flops 2000000000 | bytes 1048576 | tf_op jit(solution)/shard_map/pairs/pallas_call | solution.py:172
  142.5 16.0 %all_to_all.11 = f32[8,1,4096]{2,1,0:T(1,128)S(1)} all-to-all(f32[8,1,4096]{2,1,0:T(1,128)S(1)} %reshape.122), channel_id=1, replica_groups=mesh['z'=4,'y'=4,'c'=2,'x'=4] {'c','x'}, dimensions={0} | all-to-all | bytes 262144 | tf_op jit(solution)/shard_map/all_to_all | solution.py:248
  (46 shorter events, 6.7 us)
Async XLA Ops:
  6.5 58.7 %all-gather.3.cloned.1.call-start = ((), (), s32[]{:S(2)}) async-start(), calls=%async_computation.2 | async-start | bytes 9437184 | tf_op jit(solution)/shard_map/all_gather | solution.py:205
  29.3 26.0 %collective-permute-start = (bf16[256,2048]{1,0:T(8,128)(2,1)S(1)}, bf16[256,2048]{1,0:T(8,128)(2,1)S(1)}, u32[]{:S(2)}, u32[]{:S(2)}) collective-permute-start(bf16[256,2048]{1,0:T(8,128)(2,1)S(1)} %bitcast.43), channel_id=1, source_target_pairs={{8,0},{9,1},{10,2},{11,3},{12,4},{13,5},{14,6},{15,7},{16,8},{17,9... | collective-permute-start | bytes 3145736 | tf_op jit(solution)/shard_map/ppermute | solution.py:33
  32.2 23.0 %collective-permute-start.1 = (bf16[256,2048]{1,0:T(8,128)(2,1)S(1)}, bf16[256,2048]{1,0:T(8,128)(2,1)}, u32[]{:S(2)}, u32[]{:S(2)}) collective-permute-start(bf16[256,2048]{1,0:T(8,128)(2,1)S(1)} %bitcast.44), channel_id=1, source_target_pairs={{24,0},{25,1},{26,2},{27,3},{28,4},{29,5},{30,6},{31,7},{0,8},{1,9... | collective-permute-start | bytes 3145736 | tf_op jit(solution)/shard_map/ppermute | solution.py:33
  32.2 23.1 %collective-permute-start.2 = (bf16[256,2048]{1,0:T(8,128)(2,1)S(1)}, bf16[256,2048]{1,0:T(8,128)(2,1)}, u32[]{:S(2)}, u32[]{:S(2)}) collective-permute-start(bf16[256,2048]{1,0:T(8,128)(2,1)S(1)} %bitcast.45), channel_id=1, source_target_pairs={{32,0},{33,1},{34,2},{35,3},{36,4},{37,5},{38,6},{39,7},{40,8},{41... | collective-permute-start | bytes 3145736 | tf_op jit(solution)/shard_map/ppermute | solution.py:33
  37.1 20.6 %collective-permute-start.3 = (bf16[256,2048]{1,0:T(8,128)(2,1)S(1)}, bf16[256,2048]{1,0:T(8,128)(2,1)}, u32[]{:S(2)}, u32[]{:S(2)}) collective-permute-start(bf16[256,2048]{1,0:T(8,128)(2,1)S(1)} %bitcast.46), channel_id=1, source_target_pairs={{96,0},{97,1},{98,2},{99,3},{100,4},{101,5},{102,6},{103,7},{104,8... | collective-permute-start | bytes 3145736 | tf_op jit(solution)/shard_map/ppermute | solution.py:33
  38.3 6.3 %collective-permute-start.4 = (s32[4,16,128]{2,1,0:T(8,128)S(1)}, s32[4,16,128]{2,1,0:T(8,128)S(1)}, u32[]{:S(2)}, u32[]{:S(2)}) collective-permute-start(s32[4,16,128]{2,1,0:T(8,128)S(1)} %bitcast.63), channel_id=1, source_target_pairs={{4,0},{5,1},{6,2},{7,3},{0,4},{1,5},{2,6},{3,7},{12,8},{13,9},{14,... | collective-permute-start | bytes 98312 | tf_op jit(solution)/shard_map/ppermute | solution.py:33
  51.6 35.0 %copy-start.1 = (f32[8,16,16,128]{3,2,1,0:T(8,128)S(1)}, f32[8,16,16,128]{3,2,1,0:T(8,128)}, u32[]{:S(2)}) copy-start(f32[8,16,16,128]{3,2,1,0:T(8,128)} %station_counts.1.times_ref) | copy-start | bytes 3145732
  57.7 23.8 %collective-permute-start.5 = (bf16[256,2048]{1,0:T(8,128)(2,1)}, bf16[256,2048]{1,0:T(8,128)(2,1)}, u32[]{:S(2)}, u32[]{:S(2)}) collective-permute-start(bf16[256,2048]{1,0:T(8,128)(2,1)} %collective-permute-done.2.refs_3_), channel_id=1, source_target_pairs={{8,0},{9,1},{10,2},{11,3},{12,4},{13,5},{14,6},{15,7},{16,8},{17,9... | collective-permute-start | bytes 3145736 | tf_op jit(solution)/shard_map/ppermute | solution.py:33
  60.1 23.7 %collective-permute-start.6 = (bf16[256,2048]{1,0:T(8,128)(2,1)}, bf16[256,2048]{1,0:T(8,128)(2,1)}, u32[]{:S(2)}, u32[]{:S(2)}) collective-permute-start(bf16[256,2048]{1,0:T(8,128)(2,1)} %collective-permute-done.3.refs_0_), channel_id=1, source_target_pairs={{24,0},{25,1},{26,2},{27,3},{28,4},{29,5},{30,6},{31,7},{0,8},{1,9... | collective-permute-start | bytes 3145736 | tf_op jit(solution)/shard_map/ppermute | solution.py:33
  60.1 23.7 %collective-permute-start.7 = (bf16[256,2048]{1,0:T(8,128)(2,1)}, bf16[256,2048]{1,0:T(8,128)(2,1)}, u32[]{:S(2)}, u32[]{:S(2)}) collective-permute-start(bf16[256,2048]{1,0:T(8,128)(2,1)} %collective-permute-done.1.refs_2_), channel_id=1, source_target_pairs={{32,0},{33,1},{34,2},{35,3},{36,4},{37,5},{38,6},{39,7},{40,8},{41... | collective-permute-start | bytes 3145736 | tf_op jit(solution)/shard_map/ppermute | solution.py:33
  61.2 22.6 %collective-permute-start.8 = (bf16[256,2048]{1,0:T(8,128)(2,1)S(1)}, bf16[256,2048]{1,0:T(8,128)(2,1)}, u32[]{:S(2)}, u32[]{:S(2)}) collective-permute-start(bf16[256,2048]{1,0:T(8,128)(2,1)S(1)} %collective-permute-done.refs_1_), channel_id=1, source_target_pairs={{96,0},{97,1},{98,2},{99,3},{100,4},{101,5},{102,6},{103,7},{104,8... | collective-permute-start | bytes 3145736 | tf_op jit(solution)/shard_map/ppermute | solution.py:33
  61.6 43.7 %collective-permute-start.11 = (bf16[256,2048]{1,0:T(8,128)(2,1)}, bf16[256,2048]{1,0:T(8,128)(2,1)}, u32[]{:S(2)}, u32[]{:S(2)}) collective-permute-start(bf16[256,2048]{1,0:T(8,128)(2,1)} %collective-permute-done.2.refs_3_), channel_id=1, source_target_pairs={{32,0},{33,1},{34,2},{35,3},{36,4},{37,5},{38,6},{39,7},{40,8},{41... | collective-permute-start | bytes 3145736 | tf_op jit(solution)/shard_map/ppermute | solution.py:33
  65.3 1.2 copy-start
  81.5 24.5 %collective-permute-start.9 = (bf16[256,2048]{1,0:T(8,128)(2,1)S(1)}, bf16[256,2048]{1,0:T(8,128)(2,1)S(1)}, u32[]{:S(2)}, u32[]{:S(2)}) collective-permute-start(bf16[256,2048]{1,0:T(8,128)(2,1)S(1)} %collective-permute-done.refs_1_), channel_id=1, source_target_pairs={{8,0},{9,1},{10,2},{11,3},{12,4},{13,5},{14,6},{15,7},{16,8},{17,9... | collective-permute-start | bytes 3145736 | tf_op jit(solution)/shard_map/ppermute | solution.py:33
  83.8 22.2 %collective-permute-start.10 = (bf16[256,2048]{1,0:T(8,128)(2,1)}, bf16[256,2048]{1,0:T(8,128)(2,1)S(1)}, u32[]{:S(2)}, u32[]{:S(2)}) collective-permute-start(bf16[256,2048]{1,0:T(8,128)(2,1)} %collective-permute-done.6.refs_2_), channel_id=1, source_target_pairs={{24,0},{25,1},{26,2},{27,3},{28,4},{29,5},{30,6},{31,7},{0,8},{1,9... | collective-permute-start | bytes 3145736 | tf_op jit(solution)/shard_map/ppermute | solution.py:33
  83.9 22.1 %collective-permute-start.12 = (bf16[256,2048]{1,0:T(8,128)(2,1)}, bf16[256,2048]{1,0:T(8,128)(2,1)S(1)}, u32[]{:S(2)}, u32[]{:S(2)}) collective-permute-start(bf16[256,2048]{1,0:T(8,128)(2,1)} %collective-permute-done.8.refs_4_), channel_id=1, source_target_pairs={{96,0},{97,1},{98,2},{99,3},{100,4},{101,5},{102,6},{103,7},{104,8... | collective-permute-start | bytes 3145736 | tf_op jit(solution)/shard_map/ppermute | solution.py:33
  86.6 37.1 %collective-permute-start.14 = (bf16[256,2048]{1,0:T(8,128)(2,1)}, bf16[256,2048]{1,0:T(8,128)(2,1)S(1)}, u32[]{:S(2)}, u32[]{:S(2)}) collective-permute-start(bf16[256,2048]{1,0:T(8,128)(2,1)} %collective-permute-done.7.refs_3_), channel_id=1, source_target_pairs={{24,0},{25,1},{26,2},{27,3},{28,4},{29,5},{30,6},{31,7},{0,8},{1,9... | collective-permute-start | bytes 3145736 | tf_op jit(solution)/shard_map/ppermute | solution.py:33
  105.3 24.9 %collective-permute-start.15 = (bf16[256,2048]{1,0:T(8,128)(2,1)}, bf16[256,2048]{1,0:T(8,128)(2,1)S(1)}, u32[]{:S(2)}, u32[]{:S(2)}) collective-permute-start(bf16[256,2048]{1,0:T(8,128)(2,1)} %collective-permute-done.6.refs_2_), channel_id=1, source_target_pairs={{96,0},{97,1},{98,2},{99,3},{100,4},{101,5},{102,6},{103,7},{104,8... | collective-permute-start | bytes 3145736 | tf_op jit(solution)/shard_map/ppermute | solution.py:33
  106.0 24.1 %collective-permute-start.13 = (bf16[256,2048]{1,0:T(8,128)(2,1)S(1)}, bf16[256,2048]{1,0:T(8,128)(2,1)S(1)}, u32[]{:S(2)}, u32[]{:S(2)}) collective-permute-start(bf16[256,2048]{1,0:T(8,128)(2,1)S(1)} %collective-permute-done.12.refs_3_), channel_id=1, source_target_pairs={{8,0},{9,1},{10,2},{11,3},{12,4},{13,5},{14,6},{15,7},{16,8},{17,9... | collective-permute-start | bytes 3145736 | tf_op jit(solution)/shard_map/ppermute | solution.py:33
Sparse Core Ops, SparseCore 0:
  9.5 55.7 all-gather.2

commit v5 on v4

--- a/solution.py
+++ b/solution.py
@@ -44,24 +44,30 @@
 
 
 def count_kernel(list_ref, out_ref):
-    stations = list_ref[0]
-    high = stations >> 7
-    low = stations & (LANES - 1)
+    count_r, count_s, _ = list_ref.shape
     chunk = lax.broadcasted_iota(jnp.int32, (16, LANES), 0)
     lane = lax.broadcasted_iota(jnp.int32, (LANES, LANES), 0)
-    for s in range(stations.shape[0]):
-        is_high = (high[s : s + 1, :] == chunk).astype(jnp.float32).astype(jnp.bfloat16)
-        is_low = (low[s : s + 1, :] == lane).astype(jnp.float32).astype(jnp.bfloat16)
-        out_ref[0, s] = lax.dot_general(is_high, is_low, NT_DIMS, preferred_element_type=jnp.float32)
+
+    def counts(r, carry):
+        stations = list_ref[r]
+        high = stations >> 7
+        low = stations & (LANES - 1)
+        for s in range(count_s):
+            is_high = (high[s : s + 1, :] == chunk).astype(jnp.float32).astype(jnp.bfloat16)
+            is_low = (low[s : s + 1, :] == lane).astype(jnp.float32).astype(jnp.bfloat16)
+            out_ref[r, s] = lax.dot_general(is_high, is_low, NT_DIMS, preferred_element_type=jnp.float32)
+        return carry
+
+    lax.fori_loop(0, count_r, counts, 0)
 
 
 def station_counts(lists):
     count_r, count_s, _ = lists.shape
+    on_chip = pl.BlockSpec(memory_space=pltpu.VMEM)
     return pl.pallas_call(
         count_kernel,
-        grid=(count_r,),
-        in_specs=[pl.BlockSpec((1, count_s, LANES), lambda i: (i, 0, 0))],
-        out_specs=pl.BlockSpec((1, count_s, 16, LANES), lambda i: (i, 0, 0, 0)),
+        in_specs=[on_chip],
+        out_specs=on_chip,
         out_shape=jax.ShapeDtypeStruct((count_r, count_s, 16, LANES), jnp.float32),
         cost_estimate=pl.CostEstimate(flops=10**9, bytes_accessed=2**20, transcendentals=0),
         name="station_counts",
@@ -82,7 +88,7 @@
 
 def pair_kernel(first_s, count_s, flag_ref, times_ref, r_ref, *refs):
     s_refs = refs[:count_s]
-    out_ref, scaled, outer, rest, r_buf, sems = refs[count_s:]
+    out_ref, scaled, outer, times_buf, r_buf, sems = refs[count_s:]
     length, stations = s_refs[0].shape
     _, windows, group, window_len, _ = r_ref.shape
     chunks = stations // LANES
@@ -95,6 +101,9 @@
                 r_buf.at[to, pl.ds(w * window_len, window_len)],
                 sems.at[to, w],
             )
+        yield pltpu.make_async_copy(
+            times_ref.at[number, pl.ds(first_s, count_s)], times_buf.at[to], sems.at[to, windows]
+        )
 
     for fetch in fetches(0, 0):
         fetch.start()
@@ -113,7 +122,7 @@
         for s in range(count_s):
             for c in range(chunks):
                 cols = slice(c * LANES, (c + 1) * LANES)
-                times = jnp.broadcast_to(times_ref[r, first_s + s, c : c + 1, :], (16, LANES)).astype(jnp.bfloat16)
+                times = jnp.broadcast_to(times_buf[slot, s, c : c + 1, :], (16, LANES)).astype(jnp.bfloat16)
                 times = jnp.concatenate([times] * (length // 16), axis=0)
                 scaled[s * length : (s + 1) * length, cols] = s_refs[s][:, cols] * times
         outer[...] = lax.dot_general(scaled[...], r_buf[slot], NT_DIMS, preferred_element_type=jnp.float32)
@@ -134,31 +143,29 @@
 
                 @pl.when(flag != 0)
                 def _():
-                    rest[...] = jnp.zeros_like(rest)
-
                     def one(pair, carry):
                         @pl.when((flag >> pair) & 1 != 0)
                         def _():
                             parts = []
                             for half in range(2):
                                 cols = pl.ds(pl.multiple_of((pair * 2 + half) * LANES, LANES), LANES)
-                                times = times_ref[r, first_s + s, pl.ds(pair * 2 + half, 1), :]
+                                times = times_buf[slot, s, pl.ds(pair * 2 + half, 1), :]
                                 whole = s_refs[s][:, cols].astype(jnp.float32) * jnp.broadcast_to(times, (length, LANES))
                                 parts.append((whole - scaled[rows, cols].astype(jnp.float32)).astype(jnp.bfloat16))
                             both = pl.ds(pl.multiple_of(pair * 2 * LANES, 2 * LANES), 2 * LANES)
-                            rest[...] += lax.dot_general(
+                            rest = lax.dot_general(
                                 jnp.concatenate(parts, axis=1),
                                 r_buf[slot, :, both],
                                 NT_DIMS,
                                 preferred_element_type=jnp.float32,
                             )
+                            first, second = antidiagonals(rest)
+                            out_ref[r, s, 0:1, :] += first
+                            out_ref[r, s, 1:2, :] += second
 
                         return carry
 
                     lax.fori_loop(0, chunks // 2, one, 0)
-                    first, second = antidiagonals(rest[...])
-                    out_ref[r, s, 0:1, :] += first
-                    out_ref[r, s, 1:2, :] += second
 
         return carry
 
@@ -171,15 +178,16 @@
     on_chip = pl.BlockSpec(memory_space=pltpu.VMEM)
     return pl.pallas_call(
         functools.partial(pair_kernel, first_s, count_s),
-        in_specs=[pl.BlockSpec(memory_space=pltpu.SMEM), on_chip, pl.BlockSpec(memory_space=pltpu.HBM)]
+        in_specs=[pl.BlockSpec(memory_space=pltpu.SMEM)]
+        + [pl.BlockSpec(memory_space=pltpu.HBM)] * 2
         + [on_chip] * count_s,
         out_specs=on_chip,
         scratch_shapes=[
             pltpu.VMEM((count_s * length, stations), jnp.bfloat16),
             pltpu.VMEM((count_s * length, length), jnp.float32),
-            pltpu.VMEM((length, length), jnp.float32),
+            pltpu.VMEM((2, count_s) + times.shape[2:], jnp.float32),
             pltpu.VMEM((2, length, stations), jnp.bfloat16),
-            pltpu.SemaphoreType.DMA((2, 4)),
+            pltpu.SemaphoreType.DMA((2, 5)),
         ],
         out_shape=jax.ShapeDtypeStruct((count_r, count_s, 2, LANES), jnp.float32),
         compiler_params=pltpu.CompilerParams(vmem_limit_bytes=GRANT << 20),
@@ -244,7 +252,7 @@
 
     rows = lax.dynamic_index_in_dim(jnp.asarray(made_rows), device, 0, keepdims=False)
     made = made.at[rows].get(mode="promise_in_bounds").reshape(2, group, 16, 4, length_win)
-    made = jnp.transpose(made, (0, 3, 4, 1, 2)).reshape(8, length_win, group, 16)
+    made = jnp.transpose(made, (0, 3, 4, 1, 2)).reshape(8, -1, LANES)
     made = lax.all_to_all(made, ("c", "x"), 0, 0, tiled=True)
     made = made.reshape(2, 4, length_win, group, 16)
     return jnp.transpose(made, (2, 4, 0, 1, 3)).reshape(length_win, shots, group)

time: 169 us -> 169 us (level)
    unnamed x8 -> x6, local copies, waits for them, and re-layouts: 4.31 us -> 4.03 us
  transfers between devices with their start and end apart: 17 -> 17, of which waited for: 4 -> 4; matrix products, arithmetic and copies ran while one was open for 4% -> 4% of each run, Pallas kernels for 32% -> 31%
where the time goes in v5:
time: 169 us; the launch traced here: 168 us
  Pallas kernels  64.1 us (38%)
  blocking collectives  35.8 us (21%)
  starting transfers between devices  28.2 us (17%)
  between operations  13.6 us (8%)
  waiting for transfers between devices  10.6 us (6%)
  local copies, waits for them, and re-layouts  9.28 us (5%)
  other arithmetic  6.13 us (4%)
    pallas_call x4, Pallas kernels, predict(): pl.pallas_call(functools.partial(pair_kernel, first_s, count_s), in_specs...  59.2 us
    ppermute x16, starting transfers between devices, from_offset(): return lax.ppermute(value, AXES, pairs)  28.2 us
    all_to_all x1, blocking collectives, body(): lax.all_to_all(native, 'x', 0, 0, tiled=True)  19.9 us
    all_to_all x1, blocking collectives, body(): made = lax.all_to_all(made, ('c', 'x'), 0, 0, tiled=True)  15.8 us
    ppermute x16, waiting for transfers between devices, from_offset(): return lax.ppermute(value, AXES, pairs)  8.5 us
    pallas_call x1, Pallas kernels, station_counts(): pl.pallas_call(count_kernel, in_specs=[on_chip], out_specs=on_chip, out_s...  4.93 us
    unnamed x6, local copies, waits for them, and re-layouts  4.03 us
    reduce_max x2, other arithmetic, body(): odd = jnp.max((whole & whole - 1 != 0).astype(jnp.int32), axis=3)  3.57 us
  transfers between devices with their start and end apart: 17, of which 4 were waited for; matrix products, arithmetic and copies ran while one was open for 4% of the time, Pallas kernels for 31%

profile of v5, /device:TPU:1, one launch (start us, length us, event | category | flops | bytes accessed | tf_op | source)
XLA Modules:
  0.0 167.7 jit_solution(4573275672072323971)
XLA Ops:
  6.5 2.8 %copy.21 = bf16[64,4,2048]{2,0,1:T(8,128)(2,1)} copy(bf16[64,4,2048]{2,1,0:T(4,128)(2,1)} %param.5) | data formatting | bytes 2097152 | tf_op args[0]
  9.4 19.9 %all_to_all.10 = bf16[4,64,2048]{2,1,0:T(8,128)(2,1)S(1)} all-to-all(bf16[4,64,2048]{2,1,0:T(8,128)(2,1)} %bitcast.48), channel_id=1, replica_groups=mesh['z'=4,'y'=4,'c'=2,'x'=4] {'x'}, dimensions={0} | all-to-all | bytes 2097152 | tf_op jit(solution)/shard_map/all_to_all | solution.py:212
  29.3 3.0 %collective-permute-start = (bf16[256,2048]{1,0:T(8,128)(2,1)S(1)}, bf16[256,2048]{1,0:T(8,128)(2,1)S(1)}, u32[]{:S(2)}, u32[]{:S(2)}) collective-permute-start(bf16[256,2048]{1,0:T(8,128)(2,1)S(1)} %bitcast.37), channel_id=1, source_target_pairs={{8,0},{9,1},{10,2},{11,3},{12,4},{13,5},{14,6},{15,7},{16,8},{17,9... | collective-permute-start | bytes 3145736 | tf_op jit(solution)/shard_map/ppermute | solution.py:33
  32.2 4.9 %collective-permute-start.2 = (bf16[256,2048]{1,0:T(8,128)(2,1)S(1)}, bf16[256,2048]{1,0:T(8,128)(2,1)}, u32[]{:S(2)}, u32[]{:S(2)}) collective-permute-start(bf16[256,2048]{1,0:T(8,128)(2,1)S(1)} %bitcast.39), channel_id=1, source_target_pairs={{32,0},{33,1},{34,2},{35,3},{36,4},{37,5},{38,6},{39,7},{40,8},{41... | collective-permute-start | bytes 3145736 | tf_op jit(solution)/shard_map/ppermute | solution.py:33
  37.1 1.1 fusion.1
  38.3 5.5 %collective-permute-start.4 = (s32[4,16,128]{2,1,0:T(8,128)S(1)}, s32[4,16,128]{2,1,0:T(8,128)S(1)}, u32[]{:S(2)}, u32[]{:S(2)}) collective-permute-start(s32[4,16,128]{2,1,0:T(8,128)S(1)} %bitcast.57), channel_id=1, source_target_pairs={{4,0},{5,1},{6,2},{7,3},{0,4},{1,5},{2,6},{3,7},{12,8},{13,9},{14,... | collective-permute-start | bytes 98312 | tf_op jit(solution)/shard_map/ppermute | solution.py:33
  44.6 1.2 gather_fusion
  45.8 4.9 %station_counts.1.times_ref = f32[8,16,16,128]{3,2,1,0:T(8,128)} custom-call(s32[8,16,128]{2,1,0:T(8,128)} %bitcast.56), custom_call_target="tpu_custom_call" | custom-call | flops 1000000000 | bytes 1048576 | tf_op jit(solution)/shard_map/station_counts/pallas_call | solution.py:67
  50.8 3.6 %convert_reduce_fusion = s32[8,16,16]{2,1,0:T(8,128)S(1)} fusion(f32[8,16,16,128]{3,2,1,0:T(8,128)} %station_counts.1.times_ref), kind=kLoop, calls=%fused_computation.5 | loop fusion | flops 1570816 | bytes 1056768 | tf_op jit(solution)/shard_map/reduce_max | solution.py:240
  54.5 3.2 %collective-permute-done.3.refs_0_ = bf16[256,2048]{1,0:T(8,128)(2,1)} collective-permute-done((bf16[256,2048]{1,0:T(8,128)(2,1)S(1)}, bf16[256,2048]{1,0:T(8,128)(2,1)}, u32[]{:S(2)}, u32[]{:S(2)}) %collective-permute-start.3) | collective-permute-done | bytes 1048608 | tf_op jit(solution)/shard_map/ppermute | solution.py:33
  57.7 2.4 %collective-permute-start.5 = (bf16[256,2048]{1,0:T(8,128)(2,1)}, bf16[256,2048]{1,0:T(8,128)(2,1)}, u32[]{:S(2)}, u32[]{:S(2)}) collective-permute-start(bf16[256,2048]{1,0:T(8,128)(2,1)} %collective-permute-done.2.refs_3_), channel_id=1, source_target_pairs={{8,0},{9,1},{10,2},{11,3},{12,4},{13,5},{14,6},{15,7},{16,8},{17,9... | collective-permute-start | bytes 3145736 | tf_op jit(solution)/shard_map/ppermute | solution.py:33
  61.6 1.6 collective-permute-start.11
  63.2 2.1 %all-gather.3.cloned.1.call-done = bf16[32,64,2048]{2,1,0:T(8,128)(2,1)} async-done(((bf16[4,64,2048]{2,1,0:T(8,128)(2,1)}), bf16[32,64,2048]{2,1,0:T(8,128)(2,1)}) %all-gather.3.cloned.1.call-update) | async-done | bytes 8388624 | tf_op jit(solution)/shard_map/all_gather | solution.py:213
  65.3 1.2 copy-done
  66.5 14.3 %pairs.4 = f32[8,4,2,128]{3,2,1,0:T(2,128)S(1)} custom-call(s32[8,16]{1,0:T(8,128)S(1)} %shift-left_reduce_fusion.flag_ref, f32[8,16,16,128]{3,2,1,0:T(8,128)S(1)} %copy-done, bf16[2,4,4,64,2048]{4,3,2,1,0:T(8,128)(2,1)} %bitcast.42, bf16[256,2048]{1,0:T(8,128)(2,1)S(1)} %bitcast.41, bf16[256,2048]{1,0:T(8,128)(2,1)S(1)} %collective-permute-done.refs_1_, ...), custom_call_target="tpu_custom_call" | custom-call | flops 2000000000 | bytes 1048576 | tf_op jit(solution)/shard_map/pairs/pallas_call | solution.py:179
  80.9 3.2 %collective-permute-start.9 = (bf16[256,2048]{1,0:T(8,128)(2,1)S(1)}, bf16[256,2048]{1,0:T(8,128)(2,1)S(1)}, u32[]{:S(2)}, u32[]{:S(2)}) collective-permute-start(bf16[256,2048]{1,0:T(8,128)(2,1)S(1)} %collective-permute-done.refs_1_), channel_id=1, source_target_pairs={{8,0},{9,1},{10,2},{11,3},{12,4},{13,5},{14,6},{15,7},{16,8},{17,9... | collective-permute-start | bytes 3145736 | tf_op jit(solution)/shard_map/ppermute | solution.py:33
  84.2 1.2 collective-permute-start.12
  86.2 18.7 %pairs.5 = f32[8,5,2,128]{3,2,1,0:T(2,128)S(1)} custom-call(s32[8,16]{1,0:T(8,128)S(1)} %shift-left_reduce_fusion.flag_ref, f32[8,16,16,128]{3,2,1,0:T(8,128)S(1)} %copy-done.1, bf16[2,4,4,64,2048]{4,3,2,1,0:T(8,128)(2,1)} %bitcast.43, bf16[256,2048]{1,0:T(8,128)(2,1)} %collective-permute-done.3.refs_0_, bf16[256,2048]{1,0:T(8,128)(2,1)} %collective-permute-done.5.refs_1_, ...), custom_call_target="tpu_custom_call" | custom-call | flops 2000000000 | bytes 1048576 | tf_op jit(solution)/shard_map/pairs/pallas_call | solution.py:179
  104.8 2.2 %collective-permute-start.15 = (bf16[256,2048]{1,0:T(8,128)(2,1)}, bf16[256,2048]{1,0:T(8,128)(2,1)S(1)}, u32[]{:S(2)}, u32[]{:S(2)}) collective-permute-start(bf16[256,2048]{1,0:T(8,128)(2,1)} %collective-permute-done.6.refs_2_), channel_id=1, source_target_pairs={{96,0},{97,1},{98,2},{99,3},{100,4},{101,5},{102,6},{103,7},{104,8... | collective-permute-start | bytes 3145736 | tf_op jit(solution)/shard_map/ppermute | solution.py:33
  107.1 1.9 %collective-permute-start.13 = (bf16[256,2048]{1,0:T(8,128)(2,1)S(1)}, bf16[256,2048]{1,0:T(8,128)(2,1)S(1)}, u32[]{:S(2)}, u32[]{:S(2)}) collective-permute-start(bf16[256,2048]{1,0:T(8,128)(2,1)S(1)} %collective-permute-done.12.refs_3_), channel_id=1, source_target_pairs={{8,0},{9,1},{10,2},{11,3},{12,4},{13,5},{14,6},{15,7},{16,8},{17,9... | collective-permute-start | bytes 3145736 | tf_op jit(solution)/shard_map/ppermute | solution.py:33
  109.8 14.5 %pairs.6 = f32[8,4,2,128]{3,2,1,0:T(2,128)S(1)} custom-call(s32[8,16]{1,0:T(8,128)S(1)} %shift-left_reduce_fusion.flag_ref, f32[8,16,16,128]{3,2,1,0:T(8,128)S(1)} %copy-done.1, bf16[2,4,4,64,2048]{4,3,2,1,0:T(8,128)(2,1)} %bitcast.44, bf16[256,2048]{1,0:T(8,128)(2,1)S(1)} %collective-permute-done.9.refs_0_, ...), custom_call_target="tpu_custom_call" | custom-call | flops 2000000000 | bytes 1048576 | tf_op jit(solution)/shard_map/pairs/pallas_call | solution.py:179
  124.3 5.1 %collective-permute-done.15.refs_2_ = bf16[256,2048]{1,0:T(8,128)(2,1)S(1)} collective-permute-done((bf16[256,2048]{1,0:T(8,128)(2,1)}, bf16[256,2048]{1,0:T(8,128)(2,1)S(1)}, u32[]{:S(2)}, u32[]{:S(2)}) %collective-permute-start.15) | collective-permute-done | bytes 1048608 | tf_op jit(solution)/shard_map/ppermute | solution.py:33
  129.4 11.6 %pairs.7 = f32[8,3,2,128]{3,2,1,0:T(2,128)S(1)} custom-call(s32[8,16]{1,0:T(8,128)S(1)} %shift-left_reduce_fusion.flag_ref, f32[8,16,16,128]{3,2,1,0:T(8,128)S(1)} %copy-done.1, bf16[2,4,4,64,2048]{4,3,2,1,0:T(8,128)(2,1)} %bitcast.45, bf16[256,2048]{1,0:T(8,128)(2,1)S(1)} %collective-permute-done.13.refs_0_, ...), custom_call_target="tpu_custom_call" | custom-call | flops 2000000000 | bytes 1048576 | tf_op jit(solution)/shard_map/pairs/pallas_call | solution.py:179
  143.1 15.8 %all_to_all.11 = f32[8,32,128]{2,1,0:T(8,128)S(1)} all-to-all(f32[8,32,128]{2,1,0:T(8,128)S(1)} %reshape.101), channel_id=1, replica_groups=mesh['z'=4,'y'=4,'c'=2,'x'=4] {'c','x'}, dimensions={0} | all-to-all | bytes 262144 | tf_op jit(solution)/shard_map/all_to_all | solution.py:256
  (44 shorter events, 8.0 us)
Async XLA Ops:
  6.5 58.7 %all-gather.3.cloned.1.call-start = ((), (), s32[]{:S(2)}) async-start(), calls=%async_computation.2 | async-start | bytes 9437184 | tf_op jit(solution)/shard_map/all_gather | solution.py:213
  29.3 25.2 %collective-permute-start = (bf16[256,2048]{1,0:T(8,128)(2,1)S(1)}, bf16[256,2048]{1,0:T(8,128)(2,1)S(1)}, u32[]{:S(2)}, u32[]{:S(2)}) collective-permute-start(bf16[256,2048]{1,0:T(8,128)(2,1)S(1)} %bitcast.37), channel_id=1, source_target_pairs={{8,0},{9,1},{10,2},{11,3},{12,4},{13,5},{14,6},{15,7},{16,8},{17,9... | collective-permute-start | bytes 3145736 | tf_op jit(solution)/shard_map/ppermute | solution.py:33
  32.2 22.2 %collective-permute-start.1 = (bf16[256,2048]{1,0:T(8,128)(2,1)S(1)}, bf16[256,2048]{1,0:T(8,128)(2,1)}, u32[]{:S(2)}, u32[]{:S(2)}) collective-permute-start(bf16[256,2048]{1,0:T(8,128)(2,1)S(1)} %bitcast.38), channel_id=1, source_target_pairs={{24,0},{25,1},{26,2},{27,3},{28,4},{29,5},{30,6},{31,7},{0,8},{1,9... | collective-permute-start | bytes 3145736 | tf_op jit(solution)/shard_map/ppermute | solution.py:33
  32.2 22.3 %collective-permute-start.2 = (bf16[256,2048]{1,0:T(8,128)(2,1)S(1)}, bf16[256,2048]{1,0:T(8,128)(2,1)}, u32[]{:S(2)}, u32[]{:S(2)}) collective-permute-start(bf16[256,2048]{1,0:T(8,128)(2,1)S(1)} %bitcast.39), channel_id=1, source_target_pairs={{32,0},{33,1},{34,2},{35,3},{36,4},{37,5},{38,6},{39,7},{40,8},{41... | collective-permute-start | bytes 3145736 | tf_op jit(solution)/shard_map/ppermute | solution.py:33
  37.1 20.6 %collective-permute-start.3 = (bf16[256,2048]{1,0:T(8,128)(2,1)S(1)}, bf16[256,2048]{1,0:T(8,128)(2,1)}, u32[]{:S(2)}, u32[]{:S(2)}) collective-permute-start(bf16[256,2048]{1,0:T(8,128)(2,1)S(1)} %bitcast.40), channel_id=1, source_target_pairs={{96,0},{97,1},{98,2},{99,3},{100,4},{101,5},{102,6},{103,7},{104,8... | collective-permute-start | bytes 3145736 | tf_op jit(solution)/shard_map/ppermute | solution.py:33
  38.3 6.3 %collective-permute-start.4 = (s32[4,16,128]{2,1,0:T(8,128)S(1)}, s32[4,16,128]{2,1,0:T(8,128)S(1)}, u32[]{:S(2)}, u32[]{:S(2)}) collective-permute-start(s32[4,16,128]{2,1,0:T(8,128)S(1)} %bitcast.57), channel_id=1, source_target_pairs={{4,0},{5,1},{6,2},{7,3},{0,4},{1,5},{2,6},{3,7},{12,8},{13,9},{14,... | collective-permute-start | bytes 98312 | tf_op jit(solution)/shard_map/ppermute | solution.py:33
  50.8 35.4 %copy-start.1 = (f32[8,16,16,128]{3,2,1,0:T(8,128)S(1)}, f32[8,16,16,128]{3,2,1,0:T(8,128)}, u32[]{:S(2)}) copy-start(f32[8,16,16,128]{3,2,1,0:T(8,128)} %station_counts.1.times_ref) | copy-start | bytes 3145732
  57.7 23.2 %collective-permute-start.5 = (bf16[256,2048]{1,0:T(8,128)(2,1)}, bf16[256,2048]{1,0:T(8,128)(2,1)}, u32[]{:S(2)}, u32[]{:S(2)}) collective-permute-start(bf16[256,2048]{1,0:T(8,128)(2,1)} %collective-permute-done.2.refs_3_), channel_id=1, source_target_pairs={{8,0},{9,1},{10,2},{11,3},{12,4},{13,5},{14,6},{15,7},{16,8},{17,9... | collective-permute-start | bytes 3145736 | tf_op jit(solution)/shard_map/ppermute | solution.py:33
  60.1 24.0 %collective-permute-start.6 = (bf16[256,2048]{1,0:T(8,128)(2,1)}, bf16[256,2048]{1,0:T(8,128)(2,1)}, u32[]{:S(2)}, u32[]{:S(2)}) collective-permute-start(bf16[256,2048]{1,0:T(8,128)(2,1)} %collective-permute-done.3.refs_0_), channel_id=1, source_target_pairs={{24,0},{25,1},{26,2},{27,3},{28,4},{29,5},{30,6},{31,7},{0,8},{1,9... | collective-permute-start | bytes 3145736 | tf_op jit(solution)/shard_map/ppermute | solution.py:33
  60.1 24.0 %collective-permute-start.7 = (bf16[256,2048]{1,0:T(8,128)(2,1)}, bf16[256,2048]{1,0:T(8,128)(2,1)}, u32[]{:S(2)}, u32[]{:S(2)}) collective-permute-start(bf16[256,2048]{1,0:T(8,128)(2,1)} %collective-permute-done.1.refs_2_), channel_id=1, source_target_pairs={{32,0},{33,1},{34,2},{35,3},{36,4},{37,5},{38,6},{39,7},{40,8},{41... | collective-permute-start | bytes 3145736 | tf_op jit(solution)/shard_map/ppermute | solution.py:33
  60.5 23.6 %collective-permute-start.8 = (bf16[256,2048]{1,0:T(8,128)(2,1)S(1)}, bf16[256,2048]{1,0:T(8,128)(2,1)}, u32[]{:S(2)}, u32[]{:S(2)}) collective-permute-start(bf16[256,2048]{1,0:T(8,128)(2,1)S(1)} %collective-permute-done.refs_1_), channel_id=1, source_target_pairs={{96,0},{97,1},{98,2},{99,3},{100,4},{101,5},{102,6},{103,7},{104,8... | collective-permute-start | bytes 3145736 | tf_op jit(solution)/shard_map/ppermute | solution.py:33
  61.6 43.3 %collective-permute-start.11 = (bf16[256,2048]{1,0:T(8,128)(2,1)}, bf16[256,2048]{1,0:T(8,128)(2,1)}, u32[]{:S(2)}, u32[]{:S(2)}) collective-permute-start(bf16[256,2048]{1,0:T(8,128)(2,1)} %collective-permute-done.2.refs_3_), channel_id=1, source_target_pairs={{32,0},{33,1},{34,2},{35,3},{36,4},{37,5},{38,6},{39,7},{40,8},{41... | collective-permute-start | bytes 3145736 | tf_op jit(solution)/shard_map/ppermute | solution.py:33
  65.3 1.2 copy-start
  80.9 26.2 %collective-permute-start.9 = (bf16[256,2048]{1,0:T(8,128)(2,1)S(1)}, bf16[256,2048]{1,0:T(8,128)(2,1)S(1)}, u32[]{:S(2)}, u32[]{:S(2)}) collective-permute-start(bf16[256,2048]{1,0:T(8,128)(2,1)S(1)} %collective-permute-done.refs_1_), channel_id=1, source_target_pairs={{8,0},{9,1},{10,2},{11,3},{12,4},{13,5},{14,6},{15,7},{16,8},{17,9... | collective-permute-start | bytes 3145736 | tf_op jit(solution)/shard_map/ppermute | solution.py:33
  84.1 23.0 %collective-permute-start.10 = (bf16[256,2048]{1,0:T(8,128)(2,1)}, bf16[256,2048]{1,0:T(8,128)(2,1)S(1)}, u32[]{:S(2)}, u32[]{:S(2)}) collective-permute-start(bf16[256,2048]{1,0:T(8,128)(2,1)} %collective-permute-done.6.refs_2_), channel_id=1, source_target_pairs={{24,0},{25,1},{26,2},{27,3},{28,4},{29,5},{30,6},{31,7},{0,8},{1,9... | collective-permute-start | bytes 3145736 | tf_op jit(solution)/shard_map/ppermute | solution.py:33
  84.2 22.9 %collective-permute-start.12 = (bf16[256,2048]{1,0:T(8,128)(2,1)}, bf16[256,2048]{1,0:T(8,128)(2,1)S(1)}, u32[]{:S(2)}, u32[]{:S(2)}) collective-permute-start(bf16[256,2048]{1,0:T(8,128)(2,1)} %collective-permute-done.8.refs_4_), channel_id=1, source_target_pairs={{96,0},{97,1},{98,2},{99,3},{100,4},{101,5},{102,6},{103,7},{104,8... | collective-permute-start | bytes 3145736 | tf_op jit(solution)/shard_map/ppermute | solution.py:33
  85.4 38.8 %collective-permute-start.14 = (bf16[256,2048]{1,0:T(8,128)(2,1)}, bf16[256,2048]{1,0:T(8,128)(2,1)S(1)}, u32[]{:S(2)}, u32[]{:S(2)}) collective-permute-start(bf16[256,2048]{1,0:T(8,128)(2,1)} %collective-permute-done.7.refs_3_), channel_id=1, source_target_pairs={{24,0},{25,1},{26,2},{27,3},{28,4},{29,5},{30,6},{31,7},{0,8},{1,9... | collective-permute-start | bytes 3145736 | tf_op jit(solution)/shard_map/ppermute | solution.py:33
  104.8 24.6 %collective-permute-start.15 = (bf16[256,2048]{1,0:T(8,128)(2,1)}, bf16[256,2048]{1,0:T(8,128)(2,1)S(1)}, u32[]{:S(2)}, u32[]{:S(2)}) collective-permute-start(bf16[256,2048]{1,0:T(8,128)(2,1)} %collective-permute-done.6.refs_2_), channel_id=1, source_target_pairs={{96,0},{97,1},{98,2},{99,3},{100,4},{101,5},{102,6},{103,7},{104,8... | collective-permute-start | bytes 3145736 | tf_op jit(solution)/shard_map/ppermute | solution.py:33
  107.1 22.3 %collective-permute-start.13 = (bf16[256,2048]{1,0:T(8,128)(2,1)S(1)}, bf16[256,2048]{1,0:T(8,128)(2,1)S(1)}, u32[]{:S(2)}, u32[]{:S(2)}) collective-permute-start(bf16[256,2048]{1,0:T(8,128)(2,1)S(1)} %collective-permute-done.12.refs_3_), channel_id=1, source_target_pairs={{8,0},{9,1},{10,2},{11,3},{12,4},{13,5},{14,6},{15,7},{16,8},{17,9... | collective-permute-start | bytes 3145736 | tf_op jit(solution)/shard_map/ppermute | solution.py:33
Sparse Core Ops, SparseCore 0:
  9.5 55.7 all-gather.2

commit v6 on v5

--- a/solution.py
+++ b/solution.py
@@ -239,19 +239,19 @@
     whole = times.astype(jnp.int32).reshape(2 * group, 16, 8, 2 * LANES)
     odd = jnp.max((whole & (whole - 1) != 0).astype(jnp.int32), axis=3)
     flags = jnp.sum(odd << jnp.arange(8, dtype=jnp.int32), axis=2)
-    (flags,) = meet(0, (flags,))
+    made_row = lax.dynamic_index_in_dim(jnp.asarray(made_rows), device, 0, keepdims=False)
+    flags, made_row = meet(0, (flags, made_row))
 
     travel(1)
-    blocks += meet(1, [made_of(0, 4)])
+    blocks += meet(1, [made_of(0, 3)])
     travel(2)
-    blocks += meet(2, [made_of(4, 5)])
+    blocks += meet(2, [made_of(3, 6)])
     travel(3)
     blocks += meet(3, [made_of(9, 4)])
     blocks.append(made_of(13, 3))
     made = jnp.concatenate(blocks, axis=1).reshape(2 * group * 16, 4 * length_win)
 
-    rows = lax.dynamic_index_in_dim(jnp.asarray(made_rows), device, 0, keepdims=False)
-    made = made.at[rows].get(mode="promise_in_bounds").reshape(2, group, 16, 4, length_win)
+    made = made.at[made_row].get(mode="promise_in_bounds").reshape(2, group, 16, 4, length_win)
     made = jnp.transpose(made, (0, 3, 4, 1, 2)).reshape(8, -1, LANES)
     made = lax.all_to_all(made, ("c", "x"), 0, 0, tiled=True)
     made = made.reshape(2, 4, length_win, group, 16)

time: 169 us -> 167 us (0.988)
  blocking collectives: 35.8 us -> 17.8 us
  waiting for transfers between devices: 10.6 us -> 20.3 us
  starting transfers between devices: 28.2 us -> 31.7 us
  Pallas kernels: 64.1 us -> 66.8 us
    all_to_all x1 -> x0, blocking collectives: 19.9 us -> none  [body(): lax.all_to_all(native, 'x', 0, 0, tiled=True)]
    all_to_all x0 -> x1, waiting for transfers between devices: none -> 14 us  [body(): lax.all_to_all(native, 'x', 0, 0, tiled=True)]
    all_to_all x0 -> x1, starting transfers between devices: none -> 4.87 us  [body(): lax.all_to_all(native, 'x', 0, 0, tiled=True)]
    ppermute x16, waiting for transfers between devices: 8.5 us -> 3.8 us  [from_offset(): return lax.ppermute(value, AXES, pairs)]
    pallas_call x4, Pallas kernels: 59.2 us -> 61.8 us  [predict(): pl.pallas_call(functools.partial(pair_kernel, first_s, count_s), in_specs...]
    all_to_all x1, blocking collectives: 15.8 us -> 17.8 us  [body(): made = lax.all_to_all(made, ('c', 'x'), 0, 0, tiled=True)]
  transfers between devices with their start and end apart: 17 -> 18, of which waited for: 4 -> 4; matrix products, arithmetic and copies ran while one was open for 4% -> 5% of each run, Pallas kernels for 31% -> 33%
where the time goes in v6:
time: 167 us; the launch traced here: 166 us
  Pallas kernels  66.8 us (40%)
  starting transfers between devices  31.7 us (19%)
  waiting for transfers between devices  20.3 us (12%)
  blocking collectives  17.8 us (11%)
  between operations  13.6 us (8%)
  local copies, waits for them, and re-layouts  9.96 us (6%)
  other arithmetic  5.45 us (3%)
    pallas_call x4, Pallas kernels, predict(): pl.pallas_call(functools.partial(pair_kernel, first_s, count_s), in_specs...  61.8 us
    ppermute x16, starting transfers between devices, from_offset(): return lax.ppermute(value, AXES, pairs)  26.8 us
    all_to_all x1, blocking collectives, body(): made = lax.all_to_all(made, ('c', 'x'), 0, 0, tiled=True)  17.8 us
    all_to_all x1, waiting for transfers between devices, body(): lax.all_to_all(native, 'x', 0, 0, tiled=True)  14 us
    pallas_call x1, Pallas kernels, station_counts(): pl.pallas_call(count_kernel, in_specs=[on_chip], out_specs=on_chip, out_s...  4.94 us
    all_to_all x1, starting transfers between devices, body(): lax.all_to_all(native, 'x', 0, 0, tiled=True)  4.87 us
    unnamed x6, local copies, waits for them, and re-layouts  4.02 us
    ppermute x16, waiting for transfers between devices, from_offset(): return lax.ppermute(value, AXES, pairs)  3.8 us
  transfers between devices with their start and end apart: 18, of which 4 were waited for; matrix products, arithmetic and copies ran while one was open for 5% of the time, Pallas kernels for 33%

profile of v6, /device:TPU:1, one launch (start us, length us, event | category | flops | bytes accessed | tf_op | source)
XLA Modules:
  0.0 165.5 jit_solution(11752371852952465306)
XLA Ops:
  6.5 2.8 %copy.21 = bf16[64,4,2048]{2,0,1:T(8,128)(2,1)} copy(bf16[64,4,2048]{2,1,0:T(4,128)(2,1)} %param.5) | data formatting | bytes 2097152 | tf_op args[0]
  9.3 4.9 %all-to-all-start = ((bf16[4,64,2048]{2,1,0:T(8,128)(2,1)}), bf16[4,64,2048]{2,1,0:T(8,128)(2,1)S(1)}, u32[]{:S(2)}, u32[]{:S(2)}) async-start(bf16[4,64,2048]{2,1,0:T(8,128)(2,1)} %bitcast.42), calls=%async_computation | async-start | bytes 2097152 | tf_op jit(solution)/shard_map/all_to_all | solution.py:212
  15.3 14.0 %all-to-all-done = bf16[4,64,2048]{2,1,0:T(8,128)(2,1)S(1)} async-done(((bf16[4,64,2048]{2,1,0:T(8,128)(2,1)}), bf16[4,64,2048]{2,1,0:T(8,128)(2,1)S(1)}, u32[]{:S(2)}, u32[]{:S(2)}) %all-to-all-start) | async-done | bytes 1048608 | tf_op jit(solution)/shard_map/all_to_all | solution.py:212
  29.3 3.0 %collective-permute-start = (bf16[256,2048]{1,0:T(8,128)(2,1)S(1)}, bf16[256,2048]{1,0:T(8,128)(2,1)S(1)}, u32[]{:S(2)}, u32[]{:S(2)}) collective-permute-start(bf16[256,2048]{1,0:T(8,128)(2,1)S(1)} %bitcast.31), channel_id=1, source_target_pairs={{8,0},{9,1},{10,2},{11,3},{12,4},{13,5},{14,6},{15,7},{16,8},{17,9... | collective-permute-start | bytes 3145736 | tf_op jit(solution)/shard_map/ppermute | solution.py:33
  32.2 4.8 %collective-permute-start.2 = (bf16[256,2048]{1,0:T(8,128)(2,1)S(1)}, bf16[256,2048]{1,0:T(8,128)(2,1)}, u32[]{:S(2)}, u32[]{:S(2)}) collective-permute-start(bf16[256,2048]{1,0:T(8,128)(2,1)S(1)} %bitcast.33), channel_id=1, source_target_pairs={{32,0},{33,1},{34,2},{35,3},{36,4},{37,5},{38,6},{39,7},{40,8},{41... | collective-permute-start | bytes 3145736 | tf_op jit(solution)/shard_map/ppermute | solution.py:33
  37.2 5.4 %collective-permute-start.4 = (s32[4,16,128]{2,1,0:T(8,128)S(1)}, s32[4,16,128]{2,1,0:T(8,128)S(1)}, u32[]{:S(2)}, u32[]{:S(2)}) collective-permute-start(s32[4,16,128]{2,1,0:T(8,128)S(1)} %bitcast.51), channel_id=1, source_target_pairs={{4,0},{5,1},{6,2},{7,3},{0,4},{1,5},{2,6},{3,7},{12,8},{13,9},{14,... | collective-permute-start | bytes 98312 | tf_op jit(solution)/shard_map/ppermute | solution.py:33
  44.0 1.2 gather_fusion
  45.3 4.9 %station_counts.1.times_ref = f32[8,16,16,128]{3,2,1,0:T(8,128)} custom-call(s32[8,16,128]{2,1,0:T(8,128)} %bitcast.50), custom_call_target="tpu_custom_call" | custom-call | flops 1000000000 | bytes 1048576 | tf_op jit(solution)/shard_map/station_counts/pallas_call | solution.py:67
  50.2 3.6 %convert_reduce_fusion = s32[8,16,16]{2,1,0:T(8,128)S(1)} fusion(f32[8,16,16,128]{3,2,1,0:T(8,128)} %station_counts.1.times_ref), kind=kLoop, calls=%fused_computation.5 | loop fusion | flops 1570816 | bytes 1056768 | tf_op jit(solution)/shard_map/reduce_max | solution.py:240
  54.5 3.2 %collective-permute-done.3.refs_1_ = bf16[256,2048]{1,0:T(8,128)(2,1)} collective-permute-done((bf16[256,2048]{1,0:T(8,128)(2,1)S(1)}, bf16[256,2048]{1,0:T(8,128)(2,1)}, u32[]{:S(2)}, u32[]{:S(2)}) %collective-permute-start.3) | collective-permute-done | bytes 1048608 | tf_op jit(solution)/shard_map/ppermute | solution.py:33
  57.7 2.4 %collective-permute-start.5 = (bf16[256,2048]{1,0:T(8,128)(2,1)}, bf16[256,2048]{1,0:T(8,128)(2,1)}, u32[]{:S(2)}, u32[]{:S(2)}) collective-permute-start(bf16[256,2048]{1,0:T(8,128)(2,1)} %collective-permute-done.2.refs_0_), channel_id=1, source_target_pairs={{8,0},{9,1},{10,2},{11,3},{12,4},{13,5},{14,6},{15,7},{16,8},{17,9... | collective-permute-start | bytes 3145736 | tf_op jit(solution)/shard_map/ppermute | solution.py:33
  60.4 1.2 collective-permute-start.8
  61.6 1.5 collective-permute-start.11
  63.0 2.5 %all-gather.3.cloned.1.call-done = bf16[32,64,2048]{2,1,0:T(8,128)(2,1)} async-done(((bf16[4,64,2048]{2,1,0:T(8,128)(2,1)}), bf16[32,64,2048]{2,1,0:T(8,128)(2,1)}) %all-gather.3.cloned.1.call-update) | async-done | bytes 8388624 | tf_op jit(solution)/shard_map/all_gather | solution.py:213
  65.6 1.2 copy-done
  66.8 12.3 %pairs.4 = f32[8,3,2,128]{3,2,1,0:T(2,128)S(1)} custom-call(s32[8,16]{1,0:T(8,128)S(1)} %shift-left_reduce_fusion.flag_ref, f32[8,16,16,128]{3,2,1,0:T(8,128)S(1)} %copy-done, bf16[2,4,4,64,2048]{4,3,2,1,0:T(8,128)(2,1)} %bitcast.36, bf16[256,2048]{1,0:T(8,128)(2,1)S(1)} %bitcast.35, bf16[256,2048]{1,0:T(8,128)(2,1)S(1)} %collective-permute-done.refs_1_, ...), custom_call_target="tpu_custom_call" | custom-call | flops 2000000000 | bytes 1048576 | tf_op jit(solution)/shard_map/pairs/pallas_call | solution.py:179
  79.2 2.8 %collective-permute-start.9 = (bf16[256,2048]{1,0:T(8,128)(2,1)S(1)}, bf16[256,2048]{1,0:T(8,128)(2,1)S(1)}, u32[]{:S(2)}, u32[]{:S(2)}) collective-permute-start(bf16[256,2048]{1,0:T(8,128)(2,1)S(1)} %collective-permute-done.refs_1_), channel_id=1, source_target_pairs={{8,0},{9,1},{10,2},{11,3},{12,4},{13,5},{14,6},{15,7},{16,8},{17,9... | collective-permute-start | bytes 3145736 | tf_op jit(solution)/shard_map/ppermute | solution.py:33
  82.0 2.6 %collective-permute-start.12 = (bf16[256,2048]{1,0:T(8,128)(2,1)}, bf16[256,2048]{1,0:T(8,128)(2,1)S(1)}, u32[]{:S(2)}, u32[]{:S(2)}) collective-permute-start(bf16[256,2048]{1,0:T(8,128)(2,1)} %collective-permute-done.8.refs_5_), channel_id=1, source_target_pairs={{96,0},{97,1},{98,2},{99,3},{100,4},{101,5},{102,6},{103,7},{104,8... | collective-permute-start | bytes 3145736 | tf_op jit(solution)/shard_map/ppermute | solution.py:33
  84.6 23.0 %pairs.5 = f32[8,6,2,128]{3,2,1,0:T(2,128)S(1)} custom-call(s32[8,16]{1,0:T(8,128)S(1)} %shift-left_reduce_fusion.flag_ref, f32[8,16,16,128]{3,2,1,0:T(8,128)S(1)} %copy-done.1, bf16[2,4,4,64,2048]{4,3,2,1,0:T(8,128)(2,1)} %bitcast.37, bf16[256,2048]{1,0:T(8,128)(2,1)} %collective-permute-done.2.refs_0_, bf16[256,2048]{1,0:T(8,128)(2,1)} %collective-permute-done.3.refs_1_, ...), custom_call_target="tpu_custom_call" | custom-call | flops 2000000000 | bytes 1048576 | tf_op jit(solution)/shard_map/pairs/pallas_call | solution.py:179
  107.6 1.1 collective-permute-start.15
  108.8 1.7 %collective-permute-start.13 = (bf16[256,2048]{1,0:T(8,128)(2,1)S(1)}, bf16[256,2048]{1,0:T(8,128)(2,1)S(1)}, u32[]{:S(2)}, u32[]{:S(2)}) collective-permute-start(bf16[256,2048]{1,0:T(8,128)(2,1)S(1)} %collective-permute-done.12.refs_3_), channel_id=1, source_target_pairs={{8,0},{9,1},{10,2},{11,3},{12,4},{13,5},{14,6},{15,7},{16,8},{17,9... | collective-permute-start | bytes 3145736 | tf_op jit(solution)/shard_map/ppermute | solution.py:33
  110.4 14.5 %pairs.6 = f32[8,4,2,128]{3,2,1,0:T(2,128)S(1)} custom-call(s32[8,16]{1,0:T(8,128)S(1)} %shift-left_reduce_fusion.flag_ref, f32[8,16,16,128]{3,2,1,0:T(8,128)S(1)} %copy-done.1, bf16[2,4,4,64,2048]{4,3,2,1,0:T(8,128)(2,1)} %bitcast.38, bf16[256,2048]{1,0:T(8,128)(2,1)S(1)} %collective-permute-done.9.refs_0_, ...), custom_call_target="tpu_custom_call" | custom-call | flops 2000000000 | bytes 1048576 | tf_op jit(solution)/shard_map/pairs/pallas_call | solution.py:179
  124.9 12.0 %pairs.7 = f32[8,3,2,128]{3,2,1,0:T(2,128)S(1)} custom-call(s32[8,16]{1,0:T(8,128)S(1)} %shift-left_reduce_fusion.flag_ref, f32[8,16,16,128]{3,2,1,0:T(8,128)S(1)} %copy-done.1, bf16[2,4,4,64,2048]{4,3,2,1,0:T(8,128)(2,1)} %bitcast.39, bf16[256,2048]{1,0:T(8,128)(2,1)S(1)} %collective-permute-done.13.refs_0_, ...), custom_call_target="tpu_custom_call" | custom-call | flops 2000000000 | bytes 1048576 | tf_op jit(solution)/shard_map/pairs/pallas_call | solution.py:179
  139.0 17.8 %all_to_all.10 = f32[8,32,128]{2,1,0:T(8,128)S(1)} all-to-all(f32[8,32,128]{2,1,0:T(8,128)S(1)} %reshape.73), channel_id=1, replica_groups=mesh['z'=4,'y'=4,'c'=2,'x'=4] {'c','x'}, dimensions={0} | all-to-all | bytes 262144 | tf_op jit(solution)/shard_map/all_to_all | solution.py:256
  (46 shorter events, 7.5 us)
Async XLA Ops:
  6.5 59.0 %all-gather.3.cloned.1.call-start = ((), (), s32[]{:S(2)}) async-start(), calls=%async_computation.2 | async-start | bytes 9437184 | tf_op jit(solution)/shard_map/all_gather | solution.py:213
  9.3 19.9 %all-to-all-start = ((bf16[4,64,2048]{2,1,0:T(8,128)(2,1)}), bf16[4,64,2048]{2,1,0:T(8,128)(2,1)S(1)}, u32[]{:S(2)}, u32[]{:S(2)}) async-start(bf16[4,64,2048]{2,1,0:T(8,128)(2,1)} %bitcast.42), calls=%async_computation | async-start | bytes 2097152 | tf_op jit(solution)/shard_map/all_to_all | solution.py:212
  29.3 24.6 %collective-permute-start = (bf16[256,2048]{1,0:T(8,128)(2,1)S(1)}, bf16[256,2048]{1,0:T(8,128)(2,1)S(1)}, u32[]{:S(2)}, u32[]{:S(2)}) collective-permute-start(bf16[256,2048]{1,0:T(8,128)(2,1)S(1)} %bitcast.31), channel_id=1, source_target_pairs={{8,0},{9,1},{10,2},{11,3},{12,4},{13,5},{14,6},{15,7},{16,8},{17,9... | collective-permute-start | bytes 3145736 | tf_op jit(solution)/shard_map/ppermute | solution.py:33
  32.2 21.7 %collective-permute-start.1 = (bf16[256,2048]{1,0:T(8,128)(2,1)S(1)}, bf16[256,2048]{1,0:T(8,128)(2,1)}, u32[]{:S(2)}, u32[]{:S(2)}) collective-permute-start(bf16[256,2048]{1,0:T(8,128)(2,1)S(1)} %bitcast.32), channel_id=1, source_target_pairs={{24,0},{25,1},{26,2},{27,3},{28,4},{29,5},{30,6},{31,7},{0,8},{1,9... | collective-permute-start | bytes 3145736 | tf_op jit(solution)/shard_map/ppermute | solution.py:33
  32.2 22.2 %collective-permute-start.2 = (bf16[256,2048]{1,0:T(8,128)(2,1)S(1)}, bf16[256,2048]{1,0:T(8,128)(2,1)}, u32[]{:S(2)}, u32[]{:S(2)}) collective-permute-start(bf16[256,2048]{1,0:T(8,128)(2,1)S(1)} %bitcast.33), channel_id=1, source_target_pairs={{32,0},{33,1},{34,2},{35,3},{36,4},{37,5},{38,6},{39,7},{40,8},{41... | collective-permute-start | bytes 3145736 | tf_op jit(solution)/shard_map/ppermute | solution.py:33
  37.1 20.6 %collective-permute-start.3 = (bf16[256,2048]{1,0:T(8,128)(2,1)S(1)}, bf16[256,2048]{1,0:T(8,128)(2,1)}, u32[]{:S(2)}, u32[]{:S(2)}) collective-permute-start(bf16[256,2048]{1,0:T(8,128)(2,1)S(1)} %bitcast.34), channel_id=1, source_target_pairs={{96,0},{97,1},{98,2},{99,3},{100,4},{101,5},{102,6},{103,7},{104,8... | collective-permute-start | bytes 3145736 | tf_op jit(solution)/shard_map/ppermute | solution.py:33
  37.2 6.8 %collective-permute-start.4 = (s32[4,16,128]{2,1,0:T(8,128)S(1)}, s32[4,16,128]{2,1,0:T(8,128)S(1)}, u32[]{:S(2)}, u32[]{:S(2)}) collective-permute-start(s32[4,16,128]{2,1,0:T(8,128)S(1)} %bitcast.51), channel_id=1, source_target_pairs={{4,0},{5,1},{6,2},{7,3},{0,4},{1,5},{2,6},{3,7},{12,8},{13,9},{14,... | collective-permute-start | bytes 98312 | tf_op jit(solution)/shard_map/ppermute | solution.py:33
  50.2 34.4 %copy-start.1 = (f32[8,16,16,128]{3,2,1,0:T(8,128)S(1)}, f32[8,16,16,128]{3,2,1,0:T(8,128)}, u32[]{:S(2)}) copy-start(f32[8,16,16,128]{3,2,1,0:T(8,128)} %station_counts.1.times_ref) | copy-start | bytes 3145732
  57.7 21.5 %collective-permute-start.5 = (bf16[256,2048]{1,0:T(8,128)(2,1)}, bf16[256,2048]{1,0:T(8,128)(2,1)}, u32[]{:S(2)}, u32[]{:S(2)}) collective-permute-start(bf16[256,2048]{1,0:T(8,128)(2,1)} %collective-permute-done.2.refs_0_), channel_id=1, source_target_pairs={{8,0},{9,1},{10,2},{11,3},{12,4},{13,5},{14,6},{15,7},{16,8},{17,9... | collective-permute-start | bytes 3145736 | tf_op jit(solution)/shard_map/ppermute | solution.py:33
  60.1 21.9 %collective-permute-start.6 = (bf16[256,2048]{1,0:T(8,128)(2,1)}, bf16[256,2048]{1,0:T(8,128)(2,1)}, u32[]{:S(2)}, u32[]{:S(2)}) collective-permute-start(bf16[256,2048]{1,0:T(8,128)(2,1)} %collective-permute-done.3.refs_1_), channel_id=1, source_target_pairs={{24,0},{25,1},{26,2},{27,3},{28,4},{29,5},{30,6},{31,7},{0,8},{1,9... | collective-permute-start | bytes 3145736 | tf_op jit(solution)/shard_map/ppermute | solution.py:33
  60.1 21.9 %collective-permute-start.7 = (bf16[256,2048]{1,0:T(8,128)(2,1)}, bf16[256,2048]{1,0:T(8,128)(2,1)}, u32[]{:S(2)}, u32[]{:S(2)}) collective-permute-start(bf16[256,2048]{1,0:T(8,128)(2,1)} %collective-permute-done.1.refs_2_), channel_id=1, source_target_pairs={{32,0},{33,1},{34,2},{35,3},{36,4},{37,5},{38,6},{39,7},{40,8},{41... | collective-permute-start | bytes 3145736 | tf_op jit(solution)/shard_map/ppermute | solution.py:33
  60.4 21.6 %collective-permute-start.8 = (bf16[256,2048]{1,0:T(8,128)(2,1)S(1)}, bf16[256,2048]{1,0:T(8,128)(2,1)}, u32[]{:S(2)}, u32[]{:S(2)}) collective-permute-start(bf16[256,2048]{1,0:T(8,128)(2,1)S(1)} %collective-permute-done.refs_1_), channel_id=1, source_target_pairs={{96,0},{97,1},{98,2},{99,3},{100,4},{101,5},{102,6},{103,7},{104,8... | collective-permute-start | bytes 3145736 | tf_op jit(solution)/shard_map/ppermute | solution.py:33
  61.6 46.1 %collective-permute-start.11 = (bf16[256,2048]{1,0:T(8,128)(2,1)}, bf16[256,2048]{1,0:T(8,128)(2,1)}, u32[]{:S(2)}, u32[]{:S(2)}) collective-permute-start(bf16[256,2048]{1,0:T(8,128)(2,1)} %collective-permute-done.2.refs_0_), channel_id=1, source_target_pairs={{32,0},{33,1},{34,2},{35,3},{36,4},{37,5},{38,6},{39,7},{40,8},{41... | collective-permute-start | bytes 3145736 | tf_op jit(solution)/shard_map/ppermute | solution.py:33
  65.6 1.2 copy-start
  79.2 29.6 %collective-permute-start.9 = (bf16[256,2048]{1,0:T(8,128)(2,1)S(1)}, bf16[256,2048]{1,0:T(8,128)(2,1)S(1)}, u32[]{:S(2)}, u32[]{:S(2)}) collective-permute-start(bf16[256,2048]{1,0:T(8,128)(2,1)S(1)} %collective-permute-done.refs_1_), channel_id=1, source_target_pairs={{8,0},{9,1},{10,2},{11,3},{12,4},{13,5},{14,6},{15,7},{16,8},{17,9... | collective-permute-start | bytes 3145736 | tf_op jit(solution)/shard_map/ppermute | solution.py:33
  82.0 26.8 %collective-permute-start.10 = (bf16[256,2048]{1,0:T(8,128)(2,1)}, bf16[256,2048]{1,0:T(8,128)(2,1)S(1)}, u32[]{:S(2)}, u32[]{:S(2)}) collective-permute-start(bf16[256,2048]{1,0:T(8,128)(2,1)} %collective-permute-done.6.refs_3_), channel_id=1, source_target_pairs={{24,0},{25,1},{26,2},{27,3},{28,4},{29,5},{30,6},{31,7},{0,8},{1,9... | collective-permute-start | bytes 3145736 | tf_op jit(solution)/shard_map/ppermute | solution.py:33
  82.0 26.7 %collective-permute-start.12 = (bf16[256,2048]{1,0:T(8,128)(2,1)}, bf16[256,2048]{1,0:T(8,128)(2,1)S(1)}, u32[]{:S(2)}, u32[]{:S(2)}) collective-permute-start(bf16[256,2048]{1,0:T(8,128)(2,1)} %collective-permute-done.8.refs_5_), channel_id=1, source_target_pairs={{96,0},{97,1},{98,2},{99,3},{100,4},{101,5},{102,6},{103,7},{104,8... | collective-permute-start | bytes 3145736 | tf_op jit(solution)/shard_map/ppermute | solution.py:33
  84.6 40.3 %collective-permute-start.14 = (bf16[256,2048]{1,0:T(8,128)(2,1)}, bf16[256,2048]{1,0:T(8,128)(2,1)S(1)}, u32[]{:S(2)}, u32[]{:S(2)}) collective-permute-start(bf16[256,2048]{1,0:T(8,128)(2,1)} %collective-permute-done.7.refs_4_), channel_id=1, source_target_pairs={{24,0},{25,1},{26,2},{27,3},{28,4},{29,5},{30,6},{31,7},{0,8},{1,9... | collective-permute-start | bytes 3145736 | tf_op jit(solution)/shard_map/ppermute | solution.py:33
  107.6 17.3 %collective-permute-start.15 = (bf16[256,2048]{1,0:T(8,128)(2,1)}, bf16[256,2048]{1,0:T(8,128)(2,1)S(1)}, u32[]{:S(2)}, u32[]{:S(2)}) collective-permute-start(bf16[256,2048]{1,0:T(8,128)(2,1)} %collective-permute-done.6.refs_3_), channel_id=1, source_target_pairs={{96,0},{97,1},{98,2},{99,3},{100,4},{101,5},{102,6},{103,7},{104,8... | collective-permute-start | bytes 3145736 | tf_op jit(solution)/shard_map/ppermute | solution.py:33
  108.8 16.2 %collective-permute-start.13 = (bf16[256,2048]{1,0:T(8,128)(2,1)S(1)}, bf16[256,2048]{1,0:T(8,128)(2,1)S(1)}, u32[]{:S(2)}, u32[]{:S(2)}) collective-permute-start(bf16[256,2048]{1,0:T(8,128)(2,1)S(1)} %collective-permute-done.12.refs_3_), channel_id=1, source_target_pairs={{8,0},{9,1},{10,2},{11,3},{12,4},{13,5},{14,6},{15,7},{16,8},{17,9... | collective-permute-start | bytes 3145736 | tf_op jit(solution)/shard_map/ppermute | solution.py:33
Sparse Core Ops, SparseCore 0:
  9.5 56.0 all-gather.2

commit v7 on v6

--- a/solution.py
+++ b/solution.py
@@ -209,8 +209,15 @@
     theirs = from_offset(lax.dynamic_index_in_dim(lists, 1 - c, 2, keepdims=False), dc=1)
 
     native = lax.optimization_barrier(jnp.transpose(signals, (1, 0, 2)))
-    own = lax.all_to_all(native, "x", 0, 0, tiled=True).reshape(4 * length_win, stations)
-    r_shots = lax.all_gather(native, ("c", "x"), axis=0).reshape(2, 4, group, length_win, stations)
+    windows = {0: lax.dynamic_index_in_dim(native, x, 0)}
+    for dx in (1, 3, 2):
+        windows[dx] = from_offset(lax.dynamic_index_in_dim(native, (x - dx) % 4, 0), dx=dx)
+    windows[1], later = lax.optimization_barrier((windows[1], native))
+    own = jnp.zeros_like(native)
+    for dx, window in windows.items():
+        own = lax.dynamic_update_slice_in_dim(own, window, (x + dx) % 4, 0)
+    own = own.reshape(4 * length_win, stations)
+    r_shots = lax.all_gather(later, ("c", "x"), axis=0).reshape(2, 4, group, length_win, stations)
 
     held = {(0, 0): own}
     blocks = []

time: 167 us -> 172 us (1.030)
  waiting for transfers between devices: 20.3 us -> 27.6 us
  blocking collectives: 17.8 us -> 14.9 us
  starting transfers between devices: 31.7 us -> 33.5 us
    ppermute x16 -> x19, waiting for transfers between devices: 3.8 us -> 24.6 us  [from_offset(): return lax.ppermute(value, AXES, pairs)]
    all_to_all x1 -> x0, waiting for transfers between devices: 14 us -> none  [body(): lax.all_to_all(native, 'x', 0, 0, tiled=True)]
    ppermute x16 -> x19, starting transfers between devices: 26.8 us -> 33.5 us  [from_offset(): return lax.ppermute(value, AXES, pairs)]
    all_to_all x1 -> x0, starting transfers between devices: 4.87 us -> none  [body(): lax.all_to_all(native, 'x', 0, 0, tiled=True)]
    all_to_all x1, blocking collectives: 17.8 us -> 14.9 us  [body(): made = lax.all_to_all(made, ('c', 'x'), 0, 0, tiled=True)]
    unnamed x6 -> x8, local copies, waits for them, and re-layouts: 4.02 us -> 3.05 us
  transfers between devices with their start and end apart: 18 -> 20, of which waited for: 4 -> 10; matrix products, arithmetic and copies ran while one was open for 5% -> 4% of each run, Pallas kernels for 33% -> 31%
where the time goes in v7:
time: 172 us; the launch traced here: 171 us
  Pallas kernels  66.1 us (38%)
  starting transfers between devices  33.5 us (19%)
  waiting for transfers between devices  27.6 us (16%)
  blocking collectives  14.9 us (9%)
  between operations  13.7 us (8%)
  local copies, waits for them, and re-layouts  9.28 us (5%)
  other arithmetic  5.54 us (3%)
    pallas_call x4, Pallas kernels, predict(): pl.pallas_call(functools.partial(pair_kernel, first_s, count_s), in_specs...  61.2 us
    ppermute x19, starting transfers between devices, from_offset(): return lax.ppermute(value, AXES, pairs)  33.5 us
    ppermute x19, waiting for transfers between devices, from_offset(): return lax.ppermute(value, AXES, pairs)  24.6 us
    all_to_all x1, blocking collectives, body(): made = lax.all_to_all(made, ('c', 'x'), 0, 0, tiled=True)  14.9 us
    pallas_call x1, Pallas kernels, station_counts(): pl.pallas_call(count_kernel, in_specs=[on_chip], out_specs=on_chip, out_s...  4.95 us
    reduce_max x2, other arithmetic, body(): odd = jnp.max((whole & whole - 1 != 0).astype(jnp.int32), axis=3)  3.67 us
  transfers between devices with their start and end apart: 20, of which 10 were waited for; matrix products, arithmetic and copies ran while one was open for 4% of the time, Pallas kernels for 31%

profile of v7, /device:TPU:1, one launch (start us, length us, event | category | flops | bytes accessed | tf_op | source)
XLA Modules:
  0.0 170.7 jit_solution(11405024666786139053)
XLA Ops:
  6.5 1.8 %copy.27 = bf16[64,4,2048]{2,0,1:T(8,128)(2,1)S(1)} copy(bf16[64,4,2048]{2,1,0:T(4,128)(2,1)} %param.5) | data formatting | bytes 2097152 | tf_op args[0]
  8.6 3.4 %collective-permute-start = (bf16[1,64,2048]{2,1,0:T(8,128)(2,1)S(1)}, bf16[1,64,2048]{2,1,0:T(8,128)(2,1)S(1)}, u32[]{:S(2)}, u32[]{:S(2)}) collective-permute-start(bf16[1,64,2048]{2,1,0:T(8,128)(2,1)S(1)} %get-tuple-element.51), channel_id=1, source_target_pairs={{1,0},{2,1},{3,2},{0,3},{5,4},{6,5},{7,6},{4,7},{9,8},{10,9},{11,1... | collective-permute-start | bytes 786440 | tf_op jit(solution)/shard_map/ppermute | solution.py:33
  12.0 5.0 %collective-permute-done = bf16[1,64,2048]{2,1,0:T(8,128)(2,1)S(1)} collective-permute-done((bf16[1,64,2048]{2,1,0:T(8,128)(2,1)S(1)}, bf16[1,64,2048]{2,1,0:T(8,128)(2,1)S(1)}, u32[]{:S(2)}, u32[]{:S(2)}) %collective-permute-start) | collective-permute-done | bytes 262176 | tf_op jit(solution)/shard_map/ppermute | solution.py:33
  18.0 3.7 %collective-permute-start.2 = (bf16[1,64,2048]{2,1,0:T(8,128)(2,1)S(1)}, bf16[1,64,2048]{2,1,0:T(8,128)(2,1)S(1)}, u32[]{:S(2)}, u32[]{:S(2)}) collective-permute-start(bf16[1,64,2048]{2,1,0:T(8,128)(2,1)S(1)} %get-tuple-element.49), channel_id=1, source_target_pairs={{2,0},{3,1},{0,2},{1,3},{6,4},{7,5},{4,6},{5,7},{10,8},{11,9},{8,1... | collective-permute-start | bytes 786440 | tf_op jit(solution)/shard_map/ppermute | solution.py:33
  22.8 2.7 %collective-permute-done.1 = bf16[1,64,2048]{2,1,0:T(8,128)(2,1)S(1)} collective-permute-done((bf16[1,64,2048]{2,1,0:T(8,128)(2,1)S(1)}, bf16[1,64,2048]{2,1,0:T(8,128)(2,1)S(1)}, u32[]{:S(2)}, u32[]{:S(2)}) %collective-permute-start.1) | collective-permute-done | bytes 262176 | tf_op jit(solution)/shard_map/ppermute | solution.py:33
  25.6 6.5 %collective-permute-done.2 = bf16[1,64,2048]{2,1,0:T(8,128)(2,1)S(1)} collective-permute-done((bf16[1,64,2048]{2,1,0:T(8,128)(2,1)S(1)}, bf16[1,64,2048]{2,1,0:T(8,128)(2,1)S(1)}, u32[]{:S(2)}, u32[]{:S(2)}) %collective-permute-start.2) | collective-permute-done | bytes 262176 | tf_op jit(solution)/shard_map/ppermute | solution.py:33
  32.1 2.8 %collective-permute-start.3 = (bf16[256,2048]{1,0:T(8,128)(2,1)S(1)}, bf16[256,2048]{1,0:T(8,128)(2,1)S(1)}, u32[]{:S(2)}, u32[]{:S(2)}) collective-permute-start(bf16[256,2048]{1,0:T(8,128)(2,1)S(1)} %bitcast.29), channel_id=1, source_target_pairs={{8,0},{9,1},{10,2},{11,3},{12,4},{13,5},{14,6},{15,7},{16,8},{17,9... | collective-permute-start | bytes 3145736 | tf_op jit(solution)/shard_map/ppermute | solution.py:33
  34.9 3.8 %collective-permute-start.5 = (bf16[256,2048]{1,0:T(8,128)(2,1)S(1)}, bf16[256,2048]{1,0:T(8,128)(2,1)}, u32[]{:S(2)}, u32[]{:S(2)}) collective-permute-start(bf16[256,2048]{1,0:T(8,128)(2,1)S(1)} %bitcast.31), channel_id=1, source_target_pairs={{32,0},{33,1},{34,2},{35,3},{36,4},{37,5},{38,6},{39,7},{40,8},{41... | collective-permute-start | bytes 3145736 | tf_op jit(solution)/shard_map/ppermute | solution.py:33
  38.7 3.1 %collective-permute-start.7 = (s32[4,16,128]{2,1,0:T(8,128)S(1)}, s32[4,16,128]{2,1,0:T(8,128)S(1)}, u32[]{:S(2)}, u32[]{:S(2)}) collective-permute-start(s32[4,16,128]{2,1,0:T(8,128)S(1)} %bitcast.49), channel_id=1, source_target_pairs={{4,0},{5,1},{6,2},{7,3},{0,4},{1,5},{2,6},{3,7},{12,8},{13,9},{14,... | collective-permute-start | bytes 98312 | tf_op jit(solution)/shard_map/ppermute | solution.py:33
  44.5 4.9 %station_counts.1.times_ref = f32[8,16,16,128]{3,2,1,0:T(8,128)} custom-call(s32[8,16,128]{2,1,0:T(8,128)} %bitcast.48), custom_call_target="tpu_custom_call" | custom-call | flops 1000000000 | bytes 1048576 | tf_op jit(solution)/shard_map/station_counts/pallas_call | solution.py:67
  49.4 3.7 %convert_reduce_fusion = s32[8,16,16]{2,1,0:T(8,128)S(1)} fusion(f32[8,16,16,128]{3,2,1,0:T(8,128)} %station_counts.1.times_ref), kind=kLoop, calls=%fused_computation.5 | loop fusion | flops 1570816 | bytes 1056768 | tf_op jit(solution)/shard_map/reduce_max | solution.py:247
  53.2 1.6 collective-permute-done.3.refs_1_
  54.9 3.2 %collective-permute-done.4.refs_2_ = bf16[256,2048]{1,0:T(8,128)(2,1)} collective-permute-done((bf16[256,2048]{1,0:T(8,128)(2,1)S(1)}, bf16[256,2048]{1,0:T(8,128)(2,1)}, u32[]{:S(2)}, u32[]{:S(2)}) %collective-permute-start.4) | collective-permute-done | bytes 1048608 | tf_op jit(solution)/shard_map/ppermute | solution.py:33
  58.4 3.2 %collective-permute-done.6.refs_1_ = bf16[256,2048]{1,0:T(8,128)(2,1)} collective-permute-done((bf16[256,2048]{1,0:T(8,128)(2,1)S(1)}, bf16[256,2048]{1,0:T(8,128)(2,1)}, u32[]{:S(2)}, u32[]{:S(2)}) %collective-permute-start.6) | collective-permute-done | bytes 1048608 | tf_op jit(solution)/shard_map/ppermute | solution.py:33
  63.1 2.4 %collective-permute-start.8 = (bf16[256,2048]{1,0:T(8,128)(2,1)}, bf16[256,2048]{1,0:T(8,128)(2,1)}, u32[]{:S(2)}, u32[]{:S(2)}) collective-permute-start(bf16[256,2048]{1,0:T(8,128)(2,1)} %collective-permute-done.5.refs_0_), channel_id=1, source_target_pairs={{8,0},{9,1},{10,2},{11,3},{12,4},{13,5},{14,6},{15,7},{16,8},{17,9... | collective-permute-start | bytes 3145736 | tf_op jit(solution)/shard_map/ppermute | solution.py:33
  65.5 2.7 %collective-permute-start.12 = (bf16[256,2048]{1,0:T(8,128)(2,1)S(1)}, bf16[256,2048]{1,0:T(8,128)(2,1)}, u32[]{:S(2)}, u32[]{:S(2)}) collective-permute-start(bf16[256,2048]{1,0:T(8,128)(2,1)S(1)} %collective-permute-done.3.refs_1_), channel_id=1, source_target_pairs={{8,0},{9,1},{10,2},{11,3},{12,4},{13,5},{14,6},{15,7},{16,8},{17,9... | collective-permute-start | bytes 3145736 | tf_op jit(solution)/shard_map/ppermute | solution.py:33
  68.1 3.0 %all-gather.3.cloned.1.call-done = bf16[32,64,2048]{2,1,0:T(8,128)(2,1)} async-done(((bf16[4,64,2048]{2,1,0:T(8,128)(2,1)}), bf16[32,64,2048]{2,1,0:T(8,128)(2,1)}) %all-gather.3.cloned.1.call-update) | async-done | bytes 8388624 | tf_op jit(solution)/shard_map/all_gather | solution.py:220
  72.4 12.3 %pairs.4 = f32[8,3,2,128]{3,2,1,0:T(2,128)S(1)} custom-call(s32[8,16]{1,0:T(8,128)S(1)} %shift-left_reduce_fusion.flag_ref, f32[8,16,16,128]{3,2,1,0:T(8,128)S(1)} %copy-done, bf16[2,4,4,64,2048]{4,3,2,1,0:T(8,128)(2,1)} %bitcast.34, bf16[256,2048]{1,0:T(8,128)(2,1)S(1)} %bitcast.33, bf16[256,2048]{1,0:T(8,128)(2,1)S(1)} %collective-permute-done.3.refs_1_, ...), custom_call_target="tpu_custom_call" | custom-call | flops 2000000000 | bytes 1048576 | tf_op jit(solution)/shard_map/pairs/pallas_call | solution.py:179
  84.7 2.7 %collective-permute-start.14 = (bf16[256,2048]{1,0:T(8,128)(2,1)}, bf16[256,2048]{1,0:T(8,128)(2,1)S(1)}, u32[]{:S(2)}, u32[]{:S(2)}) collective-permute-start(bf16[256,2048]{1,0:T(8,128)(2,1)} %collective-permute-done.5.refs_0_), channel_id=1, source_target_pairs={{32,0},{33,1},{34,2},{35,3},{36,4},{37,5},{38,6},{39,7},{40,8},{41... | collective-permute-start | bytes 3145736 | tf_op jit(solution)/shard_map/ppermute | solution.py:33
  89.9 21.3 %pairs.5 = f32[8,6,2,128]{3,2,1,0:T(2,128)S(1)} custom-call(s32[8,16]{1,0:T(8,128)S(1)} %shift-left_reduce_fusion.flag_ref, f32[8,16,16,128]{3,2,1,0:T(8,128)S(1)} %copy-done.1, bf16[2,4,4,64,2048]{4,3,2,1,0:T(8,128)(2,1)} %bitcast.35, bf16[256,2048]{1,0:T(8,128)(2,1)} %collective-permute-done.5.refs_0_, bf16[256,2048]{1,0:T(8,128)(2,1)} %collective-permute-done.6.refs_1_, ...), custom_call_target="tpu_custom_call" | custom-call | flops 2000000000 | bytes 1048576 | tf_op jit(solution)/shard_map/pairs/pallas_call | solution.py:179
  111.2 3.8 %collective-permute-start.18 = (bf16[256,2048]{1,0:T(8,128)(2,1)}, bf16[256,2048]{1,0:T(8,128)(2,1)S(1)}, u32[]{:S(2)}, u32[]{:S(2)}) collective-permute-start(bf16[256,2048]{1,0:T(8,128)(2,1)} %collective-permute-done.9.refs_3_), channel_id=1, source_target_pairs={{96,0},{97,1},{98,2},{99,3},{100,4},{101,5},{102,6},{103,7},{104,8... | collective-permute-start | bytes 3145736 | tf_op jit(solution)/shard_map/ppermute | solution.py:33
  115.3 15.0 %pairs.6 = f32[8,4,2,128]{3,2,1,0:T(2,128)S(1)} custom-call(s32[8,16]{1,0:T(8,128)S(1)} %shift-left_reduce_fusion.flag_ref, f32[8,16,16,128]{3,2,1,0:T(8,128)S(1)} %copy-done.1, bf16[2,4,4,64,2048]{4,3,2,1,0:T(8,128)(2,1)} %bitcast.36, bf16[256,2048]{1,0:T(8,128)(2,1)} %collective-permute-done.12.refs_0_, ...), custom_call_target="tpu_custom_call" | custom-call | flops 2000000000 | bytes 1048576 | tf_op jit(solution)/shard_map/pairs/pallas_call | solution.py:179
  132.3 12.6 %pairs.7 = f32[8,3,2,128]{3,2,1,0:T(2,128)S(1)} custom-call(s32[8,16]{1,0:T(8,128)S(1)} %shift-left_reduce_fusion.flag_ref, f32[8,16,16,128]{3,2,1,0:T(8,128)S(1)} %copy-done.1, bf16[2,4,4,64,2048]{4,3,2,1,0:T(8,128)(2,1)} %bitcast.37, bf16[256,2048]{1,0:T(8,128)(2,1)S(1)} %collective-permute-done.16.refs_0_, ...), custom_call_target="tpu_custom_call" | custom-call | flops 2000000000 | bytes 1048576 | tf_op jit(solution)/shard_map/pairs/pallas_call | solution.py:179
  147.0 14.9 %all_to_all.5 = f32[8,32,128]{2,1,0:T(8,128)S(1)} all-to-all(f32[8,32,128]{2,1,0:T(8,128)S(1)} %reshape.73), channel_id=1, replica_groups=mesh['z'=4,'y'=4,'c'=2,'x'=4] {'c','x'}, dimensions={0} | all-to-all | bytes 262144 | tf_op jit(solution)/shard_map/all_to_all | solution.py:263
  (57 shorter events, 16.9 us)
Async XLA Ops:
  6.5 64.6 %all-gather.3.cloned.1.call-start = ((), (), s32[]{:S(2)}) async-start(), calls=%async_computation.1 | async-start | bytes 9437184 | tf_op jit(solution)/shard_map/all_gather | solution.py:220
  8.3 8.6 %copy-start.2 = (bf16[64,4,2048]{2,0,1:T(8,128)(2,1)}, bf16[64,4,2048]{2,0,1:T(8,128)(2,1)S(1)}, u32[]{:S(2)}) copy-start(bf16[64,4,2048]{2,0,1:T(8,128)(2,1)S(1)} %copy.27) | copy-start | bytes 3145732
  8.6 8.4 %collective-permute-start = (bf16[1,64,2048]{2,1,0:T(8,128)(2,1)S(1)}, bf16[1,64,2048]{2,1,0:T(8,128)(2,1)S(1)}, u32[]{:S(2)}, u32[]{:S(2)}) collective-permute-start(bf16[1,64,2048]{2,1,0:T(8,128)(2,1)S(1)} %get-tuple-element.51), channel_id=1, source_target_pairs={{1,0},{2,1},{3,2},{0,3},{5,4},{6,5},{7,6},{4,7},{9,8},{10,9},{11,1... | collective-permute-start | bytes 786440 | tf_op jit(solution)/shard_map/ppermute | solution.py:33
  17.0 8.6 %collective-permute-start.1 = (bf16[1,64,2048]{2,1,0:T(8,128)(2,1)S(1)}, bf16[1,64,2048]{2,1,0:T(8,128)(2,1)S(1)}, u32[]{:S(2)}, u32[]{:S(2)}) collective-permute-start(bf16[1,64,2048]{2,1,0:T(8,128)(2,1)S(1)} %get-tuple-element.50), channel_id=1, source_target_pairs={{3,0},{0,1},{1,2},{2,3},{7,4},{4,5},{5,6},{6,7},{11,8},{8,9},{9,10... | collective-permute-start | bytes 786440 | tf_op jit(solution)/shard_map/ppermute | solution.py:33
  18.0 14.1 %collective-permute-start.2 = (bf16[1,64,2048]{2,1,0:T(8,128)(2,1)S(1)}, bf16[1,64,2048]{2,1,0:T(8,128)(2,1)S(1)}, u32[]{:S(2)}, u32[]{:S(2)}) collective-permute-start(bf16[1,64,2048]{2,1,0:T(8,128)(2,1)S(1)} %get-tuple-element.49), channel_id=1, source_target_pairs={{2,0},{3,1},{0,2},{1,3},{6,4},{7,5},{4,6},{5,7},{10,8},{11,9},{8,1... | collective-permute-start | bytes 786440 | tf_op jit(solution)/shard_map/ppermute | solution.py:33
  32.1 22.8 %collective-permute-start.3 = (bf16[256,2048]{1,0:T(8,128)(2,1)S(1)}, bf16[256,2048]{1,0:T(8,128)(2,1)S(1)}, u32[]{:S(2)}, u32[]{:S(2)}) collective-permute-start(bf16[256,2048]{1,0:T(8,128)(2,1)S(1)} %bitcast.29), channel_id=1, source_target_pairs={{8,0},{9,1},{10,2},{11,3},{12,4},{13,5},{14,6},{15,7},{16,8},{17,9... | collective-permute-start | bytes 3145736 | tf_op jit(solution)/shard_map/ppermute | solution.py:33
  34.9 23.2 %collective-permute-start.4 = (bf16[256,2048]{1,0:T(8,128)(2,1)S(1)}, bf16[256,2048]{1,0:T(8,128)(2,1)}, u32[]{:S(2)}, u32[]{:S(2)}) collective-permute-start(bf16[256,2048]{1,0:T(8,128)(2,1)S(1)} %bitcast.30), channel_id=1, source_target_pairs={{24,0},{25,1},{26,2},{27,3},{28,4},{29,5},{30,6},{31,7},{0,8},{1,9... | collective-permute-start | bytes 3145736 | tf_op jit(solution)/shard_map/ppermute | solution.py:33
  34.9 23.5 %collective-permute-start.5 = (bf16[256,2048]{1,0:T(8,128)(2,1)S(1)}, bf16[256,2048]{1,0:T(8,128)(2,1)}, u32[]{:S(2)}, u32[]{:S(2)}) collective-permute-start(bf16[256,2048]{1,0:T(8,128)(2,1)S(1)} %bitcast.31), channel_id=1, source_target_pairs={{32,0},{33,1},{34,2},{35,3},{36,4},{37,5},{38,6},{39,7},{40,8},{41... | collective-permute-start | bytes 3145736 | tf_op jit(solution)/shard_map/ppermute | solution.py:33
  38.6 22.9 %collective-permute-start.6 = (bf16[256,2048]{1,0:T(8,128)(2,1)S(1)}, bf16[256,2048]{1,0:T(8,128)(2,1)}, u32[]{:S(2)}, u32[]{:S(2)}) collective-permute-start(bf16[256,2048]{1,0:T(8,128)(2,1)S(1)} %bitcast.32), channel_id=1, source_target_pairs={{96,0},{97,1},{98,2},{99,3},{100,4},{101,5},{102,6},{103,7},{104,8... | collective-permute-start | bytes 3145736 | tf_op jit(solution)/shard_map/ppermute | solution.py:33
  38.7 4.5 %collective-permute-start.7 = (s32[4,16,128]{2,1,0:T(8,128)S(1)}, s32[4,16,128]{2,1,0:T(8,128)S(1)}, u32[]{:S(2)}, u32[]{:S(2)}) collective-permute-start(s32[4,16,128]{2,1,0:T(8,128)S(1)} %bitcast.49), channel_id=1, source_target_pairs={{4,0},{5,1},{6,2},{7,3},{0,4},{1,5},{2,6},{3,7},{12,8},{13,9},{14,... | collective-permute-start | bytes 98312 | tf_op jit(solution)/shard_map/ppermute | solution.py:33
  49.4 40.5 %copy-start.1 = (f32[8,16,16,128]{3,2,1,0:T(8,128)S(1)}, f32[8,16,16,128]{3,2,1,0:T(8,128)}, u32[]{:S(2)}) copy-start(f32[8,16,16,128]{3,2,1,0:T(8,128)} %station_counts.1.times_ref) | copy-start | bytes 3145732
  61.6 23.1 %collective-permute-start.10 = (bf16[256,2048]{1,0:T(8,128)(2,1)}, bf16[256,2048]{1,0:T(8,128)(2,1)}, u32[]{:S(2)}, u32[]{:S(2)}) collective-permute-start(bf16[256,2048]{1,0:T(8,128)(2,1)} %collective-permute-done.4.refs_2_), channel_id=1, source_target_pairs={{32,0},{33,1},{34,2},{35,3},{36,4},{37,5},{38,6},{39,7},{40,8},{41... | collective-permute-start | bytes 3145736 | tf_op jit(solution)/shard_map/ppermute | solution.py:33
  61.9 25.6 %collective-permute-start.11 = (bf16[256,2048]{1,0:T(8,128)(2,1)S(1)}, bf16[256,2048]{1,0:T(8,128)(2,1)}, u32[]{:S(2)}, u32[]{:S(2)}) collective-permute-start(bf16[256,2048]{1,0:T(8,128)(2,1)S(1)} %collective-permute-done.3.refs_1_), channel_id=1, source_target_pairs={{96,0},{97,1},{98,2},{99,3},{100,4},{101,5},{102,6},{103,7},{104,8... | collective-permute-start | bytes 3145736 | tf_op jit(solution)/shard_map/ppermute | solution.py:33
  63.1 24.4 %collective-permute-start.8 = (bf16[256,2048]{1,0:T(8,128)(2,1)}, bf16[256,2048]{1,0:T(8,128)(2,1)}, u32[]{:S(2)}, u32[]{:S(2)}) collective-permute-start(bf16[256,2048]{1,0:T(8,128)(2,1)} %collective-permute-done.5.refs_0_), channel_id=1, source_target_pairs={{8,0},{9,1},{10,2},{11,3},{12,4},{13,5},{14,6},{15,7},{16,8},{17,9... | collective-permute-start | bytes 3145736 | tf_op jit(solution)/shard_map/ppermute | solution.py:33
  65.5 22.0 %collective-permute-start.9 = (bf16[256,2048]{1,0:T(8,128)(2,1)}, bf16[256,2048]{1,0:T(8,128)(2,1)}, u32[]{:S(2)}, u32[]{:S(2)}) collective-permute-start(bf16[256,2048]{1,0:T(8,128)(2,1)} %collective-permute-done.6.refs_1_), channel_id=1, source_target_pairs={{24,0},{25,1},{26,2},{27,3},{28,4},{29,5},{30,6},{31,7},{0,8},{1,9... | collective-permute-start | bytes 3145736 | tf_op jit(solution)/shard_map/ppermute | solution.py:33
  65.5 45.7 %collective-permute-start.12 = (bf16[256,2048]{1,0:T(8,128)(2,1)S(1)}, bf16[256,2048]{1,0:T(8,128)(2,1)}, u32[]{:S(2)}, u32[]{:S(2)}) collective-permute-start(bf16[256,2048]{1,0:T(8,128)(2,1)S(1)} %collective-permute-done.3.refs_1_), channel_id=1, source_target_pairs={{8,0},{9,1},{10,2},{11,3},{12,4},{13,5},{14,6},{15,7},{16,8},{17,9... | collective-permute-start | bytes 3145736 | tf_op jit(solution)/shard_map/ppermute | solution.py:33
  71.2 1.2 copy-start
  84.7 30.3 %collective-permute-start.14 = (bf16[256,2048]{1,0:T(8,128)(2,1)}, bf16[256,2048]{1,0:T(8,128)(2,1)S(1)}, u32[]{:S(2)}, u32[]{:S(2)}) collective-permute-start(bf16[256,2048]{1,0:T(8,128)(2,1)} %collective-permute-done.5.refs_0_), channel_id=1, source_target_pairs={{32,0},{33,1},{34,2},{35,3},{36,4},{37,5},{38,6},{39,7},{40,8},{41... | collective-permute-start | bytes 3145736 | tf_op jit(solution)/shard_map/ppermute | solution.py:33
  87.4 27.5 %collective-permute-start.13 = (bf16[256,2048]{1,0:T(8,128)(2,1)}, bf16[256,2048]{1,0:T(8,128)(2,1)S(1)}, u32[]{:S(2)}, u32[]{:S(2)}) collective-permute-start(bf16[256,2048]{1,0:T(8,128)(2,1)} %collective-permute-done.9.refs_3_), channel_id=1, source_target_pairs={{24,0},{25,1},{26,2},{27,3},{28,4},{29,5},{30,6},{31,7},{0,8},{1,9... | collective-permute-start | bytes 3145736 | tf_op jit(solution)/shard_map/ppermute | solution.py:33
  88.7 26.2 %collective-permute-start.15 = (bf16[256,2048]{1,0:T(8,128)(2,1)}, bf16[256,2048]{1,0:T(8,128)(2,1)S(1)}, u32[]{:S(2)}, u32[]{:S(2)}) collective-permute-start(bf16[256,2048]{1,0:T(8,128)(2,1)} %collective-permute-done.11.refs_5_), channel_id=1, source_target_pairs={{96,0},{97,1},{98,2},{99,3},{100,4},{101,5},{102,6},{103,7},{104,8... | collective-permute-start | bytes 3145736 | tf_op jit(solution)/shard_map/ppermute | solution.py:33
  88.7 41.6 %collective-permute-start.17 = (bf16[256,2048]{1,0:T(8,128)(2,1)}, bf16[256,2048]{1,0:T(8,128)(2,1)S(1)}, u32[]{:S(2)}, u32[]{:S(2)}) collective-permute-start(bf16[256,2048]{1,0:T(8,128)(2,1)} %collective-permute-done.10.refs_4_), channel_id=1, source_target_pairs={{24,0},{25,1},{26,2},{27,3},{28,4},{29,5},{30,6},{31,7},{0,8},{1,9... | collective-permute-start | bytes 3145736 | tf_op jit(solution)/shard_map/ppermute | solution.py:33
  111.2 20.5 %collective-permute-start.18 = (bf16[256,2048]{1,0:T(8,128)(2,1)}, bf16[256,2048]{1,0:T(8,128)(2,1)S(1)}, u32[]{:S(2)}, u32[]{:S(2)}) collective-permute-start(bf16[256,2048]{1,0:T(8,128)(2,1)} %collective-permute-done.9.refs_3_), channel_id=1, source_target_pairs={{96,0},{97,1},{98,2},{99,3},{100,4},{101,5},{102,6},{103,7},{104,8... | collective-permute-start | bytes 3145736 | tf_op jit(solution)/shard_map/ppermute | solution.py:33
  115.0 17.3 %collective-permute-start.16 = (bf16[256,2048]{1,0:T(8,128)(2,1)S(1)}, bf16[256,2048]{1,0:T(8,128)(2,1)S(1)}, u32[]{:S(2)}, u32[]{:S(2)}) collective-permute-start(bf16[256,2048]{1,0:T(8,128)(2,1)S(1)} %collective-permute-done.15.refs_3_), channel_id=1, source_target_pairs={{8,0},{9,1},{10,2},{11,3},{12,4},{13,5},{14,6},{15,7},{16,8},{17,9... | collective-permute-start | bytes 3145736 | tf_op jit(solution)/shard_map/ppermute | solution.py:33
Sparse Core Ops, SparseCore 0:
  17.1 54.0 all-gather.2

commit v8 on v6

--- a/solution.py
+++ b/solution.py
@@ -20,7 +20,7 @@
     (((0, 1), (0, 1), (0, 0)), ((0, 3), (0, 3), (0, 0)), ((1, 0), (1, 0), (0, 0)), ((3, 0), (3, 0), (0, 0))),
     (((1, 1), (0, 1), (1, 0)), ((3, 3), (0, 3), (3, 0)), ((1, 3), (1, 0), (0, 3)), ((3, 1), (3, 0), (0, 1))),
     (((0, 2), (0, 1), (0, 1)), ((3, 2), (0, 3), (3, 3)), ((2, 0), (1, 0), (1, 0)), ((2, 1), (3, 0), (3, 1))),
-    (((2, 2), (0, 1), (2, 1)), ((1, 2), (0, 3), (1, 3)), ((2, 3), (3, 0), (3, 3))),
+    (((2, 2), (0, 1), (2, 1)), ((2, 3), (1, 0), (1, 3)), ((1, 2), (0, 3), (1, 3))),
 )
 S_OFFSETS = ((0, 0),) + tuple(hop[0] for hops in ROUNDS for hop in hops)
 

time: 167 us -> 169 us (1.012)
  blocking collectives: 17.8 us -> 20.5 us
  starting transfers between devices: 31.7 us -> 33.9 us
  Pallas kernels: 66.8 us -> 65.1 us
    all_to_all x1, blocking collectives: 17.8 us -> 20.5 us  [body(): made = lax.all_to_all(made, ('c', 'x'), 0, 0, tiled=True)]
    ppermute x16, starting transfers between devices: 26.8 us -> 29 us  [from_offset(): return lax.ppermute(value, AXES, pairs)]
    pallas_call x4, Pallas kernels: 61.8 us -> 60.1 us  [predict(): pl.pallas_call(functools.partial(pair_kernel, first_s, count_s), in_specs...]
  transfers between devices with their start and end apart: 18 -> 18, of which waited for: 4 -> 4; matrix products, arithmetic and copies ran while one was open for 5% -> 4% of each run, Pallas kernels for 33% -> 32%
where the time goes in v8:
time: 169 us
  Pallas kernels  65.1 us (39%)
  starting transfers between devices  33.9 us (20%)
  blocking collectives  20.5 us (12%)
  waiting for transfers between devices  20.3 us (12%)
  between operations  13.6 us (8%)
  local copies, waits for them, and re-layouts  9.96 us (6%)
  other arithmetic  5.45 us (3%)
    pallas_call x4, Pallas kernels, predict(): pl.pallas_call(functools.partial(pair_kernel, first_s, count_s), in_specs...  60.1 us
    ppermute x16, starting transfers between devices, from_offset(): return lax.ppermute(value, AXES, pairs)  29 us
    all_to_all x1, blocking collectives, body(): made = lax.all_to_all(made, ('c', 'x'), 0, 0, tiled=True)  20.5 us
    all_to_all x1, waiting for transfers between devices, body(): lax.all_to_all(native, 'x', 0, 0, tiled=True)  14 us
    pallas_call x1, Pallas kernels, station_counts(): pl.pallas_call(count_kernel, in_specs=[on_chip], out_specs=on_chip, out_s...  4.96 us
    all_to_all x1, starting transfers between devices, body(): lax.all_to_all(native, 'x', 0, 0, tiled=True)  4.87 us
    unnamed x6, local copies, waits for them, and re-layouts  4.02 us
    ppermute x16, waiting for transfers between devices, from_offset(): return lax.ppermute(value, AXES, pairs)  3.78 us
  transfers between devices with their start and end apart: 18, of which 4 were waited for; matrix products, arithmetic and copies ran while one was open for 4% of the time, Pallas kernels for 32%

profile of v8, /device:TPU:1, one launch (start us, length us, event | category | flops | bytes accessed | tf_op | source)
XLA Modules:
  0.0 168.7 jit_solution(8883387349747196767)
XLA Ops:
  6.5 2.8 %copy.21 = bf16[64,4,2048]{2,0,1:T(8,128)(2,1)} copy(bf16[64,4,2048]{2,1,0:T(4,128)(2,1)} %param.5) | data formatting | bytes 2097152 | tf_op args[0]
  9.3 4.9 %all-to-all-start = ((bf16[4,64,2048]{2,1,0:T(8,128)(2,1)}), bf16[4,64,2048]{2,1,0:T(8,128)(2,1)S(1)}, u32[]{:S(2)}, u32[]{:S(2)}) async-start(bf16[4,64,2048]{2,1,0:T(8,128)(2,1)} %bitcast.42), calls=%async_computation | async-start | bytes 2097152 | tf_op jit(solution)/shard_map/all_to_all | solution.py:212
  15.3 14.0 %all-to-all-done = bf16[4,64,2048]{2,1,0:T(8,128)(2,1)S(1)} async-done(((bf16[4,64,2048]{2,1,0:T(8,128)(2,1)}), bf16[4,64,2048]{2,1,0:T(8,128)(2,1)S(1)}, u32[]{:S(2)}, u32[]{:S(2)}) %all-to-all-start) | async-done | bytes 1048608 | tf_op jit(solution)/shard_map/all_to_all | solution.py:212
  29.3 3.0 %collective-permute-start = (bf16[256,2048]{1,0:T(8,128)(2,1)S(1)}, bf16[256,2048]{1,0:T(8,128)(2,1)S(1)}, u32[]{:S(2)}, u32[]{:S(2)}) collective-permute-start(bf16[256,2048]{1,0:T(8,128)(2,1)S(1)} %bitcast.31), channel_id=1, source_target_pairs={{8,0},{9,1},{10,2},{11,3},{12,4},{13,5},{14,6},{15,7},{16,8},{17,9... | collective-permute-start | bytes 3145736 | tf_op jit(solution)/shard_map/ppermute | solution.py:33
  32.2 4.8 %collective-permute-start.2 = (bf16[256,2048]{1,0:T(8,128)(2,1)S(1)}, bf16[256,2048]{1,0:T(8,128)(2,1)}, u32[]{:S(2)}, u32[]{:S(2)}) collective-permute-start(bf16[256,2048]{1,0:T(8,128)(2,1)S(1)} %bitcast.33), channel_id=1, source_target_pairs={{32,0},{33,1},{34,2},{35,3},{36,4},{37,5},{38,6},{39,7},{40,8},{41... | collective-permute-start | bytes 3145736 | tf_op jit(solution)/shard_map/ppermute | solution.py:33
  37.2 5.4 %collective-permute-start.4 = (s32[4,16,128]{2,1,0:T(8,128)S(1)}, s32[4,16,128]{2,1,0:T(8,128)S(1)}, u32[]{:S(2)}, u32[]{:S(2)}) collective-permute-start(s32[4,16,128]{2,1,0:T(8,128)S(1)} %bitcast.51), channel_id=1, source_target_pairs={{4,0},{5,1},{6,2},{7,3},{0,4},{1,5},{2,6},{3,7},{12,8},{13,9},{14,... | collective-permute-start | bytes 98312 | tf_op jit(solution)/shard_map/ppermute | solution.py:33
  44.0 1.2 gather_fusion
  45.3 5.0 %station_counts.1.times_ref = f32[8,16,16,128]{3,2,1,0:T(8,128)} custom-call(s32[8,16,128]{2,1,0:T(8,128)} %bitcast.50), custom_call_target="tpu_custom_call" | custom-call | flops 1000000000 | bytes 1048576 | tf_op jit(solution)/shard_map/station_counts/pallas_call | solution.py:67
  50.2 3.6 %convert_reduce_fusion = s32[8,16,16]{2,1,0:T(8,128)S(1)} fusion(f32[8,16,16,128]{3,2,1,0:T(8,128)} %station_counts.1.times_ref), kind=kLoop, calls=%fused_computation.5 | loop fusion | flops 1570816 | bytes 1056768 | tf_op jit(solution)/shard_map/reduce_max | solution.py:240
  54.5 3.2 %collective-permute-done.3.refs_1_ = bf16[256,2048]{1,0:T(8,128)(2,1)} collective-permute-done((bf16[256,2048]{1,0:T(8,128)(2,1)S(1)}, bf16[256,2048]{1,0:T(8,128)(2,1)}, u32[]{:S(2)}, u32[]{:S(2)}) %collective-permute-start.3) | collective-permute-done | bytes 1048608 | tf_op jit(solution)/shard_map/ppermute | solution.py:33
  57.7 2.4 %collective-permute-start.5 = (bf16[256,2048]{1,0:T(8,128)(2,1)}, bf16[256,2048]{1,0:T(8,128)(2,1)}, u32[]{:S(2)}, u32[]{:S(2)}) collective-permute-start(bf16[256,2048]{1,0:T(8,128)(2,1)} %collective-permute-done.2.refs_0_), channel_id=1, source_target_pairs={{8,0},{9,1},{10,2},{11,3},{12,4},{13,5},{14,6},{15,7},{16,8},{17,9... | collective-permute-start | bytes 3145736 | tf_op jit(solution)/shard_map/ppermute | solution.py:33
  60.4 1.2 collective-permute-start.8
  61.6 1.5 collective-permute-start.11
  63.0 2.5 %all-gather.3.cloned.1.call-done = bf16[32,64,2048]{2,1,0:T(8,128)(2,1)} async-done(((bf16[4,64,2048]{2,1,0:T(8,128)(2,1)}), bf16[32,64,2048]{2,1,0:T(8,128)(2,1)}) %all-gather.3.cloned.1.call-update) | async-done | bytes 8388624 | tf_op jit(solution)/shard_map/all_gather | solution.py:213
  65.6 1.2 copy-done
  66.8 12.8 %pairs.4 = f32[8,3,2,128]{3,2,1,0:T(2,128)S(1)} custom-call(s32[8,16]{1,0:T(8,128)S(1)} %shift-left_reduce_fusion.flag_ref, f32[8,16,16,128]{3,2,1,0:T(8,128)S(1)} %copy-done, bf16[2,4,4,64,2048]{4,3,2,1,0:T(8,128)(2,1)} %bitcast.36, bf16[256,2048]{1,0:T(8,128)(2,1)S(1)} %bitcast.35, bf16[256,2048]{1,0:T(8,128)(2,1)S(1)} %collective-permute-done.refs_1_, ...), custom_call_target="tpu_custom_call" | custom-call | flops 2000000000 | bytes 1048576 | tf_op jit(solution)/shard_map/pairs/pallas_call | solution.py:179
  79.6 2.8 %collective-permute-start.9 = (bf16[256,2048]{1,0:T(8,128)(2,1)S(1)}, bf16[256,2048]{1,0:T(8,128)(2,1)S(1)}, u32[]{:S(2)}, u32[]{:S(2)}) collective-permute-start(bf16[256,2048]{1,0:T(8,128)(2,1)S(1)} %collective-permute-done.refs_1_), channel_id=1, source_target_pairs={{8,0},{9,1},{10,2},{11,3},{12,4},{13,5},{14,6},{15,7},{16,8},{17,9... | collective-permute-start | bytes 3145736 | tf_op jit(solution)/shard_map/ppermute | solution.py:33
  82.5 1.3 collective-permute-start.12
  83.7 2.0 %collective-permute-start.14 = (bf16[256,2048]{1,0:T(8,128)(2,1)}, bf16[256,2048]{1,0:T(8,128)(2,1)S(1)}, u32[]{:S(2)}, u32[]{:S(2)}) collective-permute-start(bf16[256,2048]{1,0:T(8,128)(2,1)} %collective-permute-done.7.refs_4_), channel_id=1, source_target_pairs={{32,0},{33,1},{34,2},{35,3},{36,4},{37,5},{38,6},{39,7},{40,8},{41... | collective-permute-start | bytes 3145736 | tf_op jit(solution)/shard_map/ppermute | solution.py:33
  85.7 21.7 %pairs.5 = f32[8,6,2,128]{3,2,1,0:T(2,128)S(1)} custom-call(s32[8,16]{1,0:T(8,128)S(1)} %shift-left_reduce_fusion.flag_ref, f32[8,16,16,128]{3,2,1,0:T(8,128)S(1)} %copy-done.1, bf16[2,4,4,64,2048]{4,3,2,1,0:T(8,128)(2,1)} %bitcast.37, bf16[256,2048]{1,0:T(8,128)(2,1)} %collective-permute-done.2.refs_0_, bf16[256,2048]{1,0:T(8,128)(2,1)} %collective-permute-done.3.refs_1_, ...), custom_call_target="tpu_custom_call" | custom-call | flops 2000000000 | bytes 1048576 | tf_op jit(solution)/shard_map/pairs/pallas_call | solution.py:179
  108.4 3.3 %collective-permute-start.13 = (bf16[256,2048]{1,0:T(8,128)(2,1)S(1)}, bf16[256,2048]{1,0:T(8,128)(2,1)S(1)}, u32[]{:S(2)}, u32[]{:S(2)}) collective-permute-start(bf16[256,2048]{1,0:T(8,128)(2,1)S(1)} %collective-permute-done.12.refs_3_), channel_id=1, source_target_pairs={{8,0},{9,1},{10,2},{11,3},{12,4},{13,5},{14,6},{15,7},{16,8},{17,9... | collective-permute-start | bytes 3145736 | tf_op jit(solution)/shard_map/ppermute | solution.py:33
  111.8 14.4 %pairs.6 = f32[8,4,2,128]{3,2,1,0:T(2,128)S(1)} custom-call(s32[8,16]{1,0:T(8,128)S(1)} %shift-left_reduce_fusion.flag_ref, f32[8,16,16,128]{3,2,1,0:T(8,128)S(1)} %copy-done.1, bf16[2,4,4,64,2048]{4,3,2,1,0:T(8,128)(2,1)} %bitcast.38, bf16[256,2048]{1,0:T(8,128)(2,1)S(1)} %collective-permute-done.9.refs_0_, ...), custom_call_target="tpu_custom_call" | custom-call | flops 2000000000 | bytes 1048576 | tf_op jit(solution)/shard_map/pairs/pallas_call | solution.py:179
  126.3 11.1 %pairs.7 = f32[8,3,2,128]{3,2,1,0:T(2,128)S(1)} custom-call(s32[8,16]{1,0:T(8,128)S(1)} %shift-left_reduce_fusion.flag_ref, f32[8,16,16,128]{3,2,1,0:T(8,128)S(1)} %copy-done.1, bf16[2,4,4,64,2048]{4,3,2,1,0:T(8,128)(2,1)} %bitcast.39, bf16[256,2048]{1,0:T(8,128)(2,1)S(1)} %collective-permute-done.13.refs_0_, ...), custom_call_target="tpu_custom_call" | custom-call | flops 2000000000 | bytes 1048576 | tf_op jit(solution)/shard_map/pairs/pallas_call | solution.py:179
  139.5 20.5 %all_to_all.10 = f32[8,32,128]{2,1,0:T(8,128)S(1)} all-to-all(f32[8,32,128]{2,1,0:T(8,128)S(1)} %reshape.73), channel_id=1, replica_groups=mesh['z'=4,'y'=4,'c'=2,'x'=4] {'c','x'}, dimensions={0} | all-to-all | bytes 262144 | tf_op jit(solution)/shard_map/all_to_all | solution.py:256
  (46 shorter events, 8.5 us)
Async XLA Ops:
  6.5 59.0 %all-gather.3.cloned.1.call-start = ((), (), s32[]{:S(2)}) async-start(), calls=%async_computation.2 | async-start | bytes 9437184 | tf_op jit(solution)/shard_map/all_gather | solution.py:213
  9.3 19.9 %all-to-all-start = ((bf16[4,64,2048]{2,1,0:T(8,128)(2,1)}), bf16[4,64,2048]{2,1,0:T(8,128)(2,1)S(1)}, u32[]{:S(2)}, u32[]{:S(2)}) async-start(bf16[4,64,2048]{2,1,0:T(8,128)(2,1)} %bitcast.42), calls=%async_computation | async-start | bytes 2097152 | tf_op jit(solution)/shard_map/all_to_all | solution.py:212
  29.3 24.6 %collective-permute-start = (bf16[256,2048]{1,0:T(8,128)(2,1)S(1)}, bf16[256,2048]{1,0:T(8,128)(2,1)S(1)}, u32[]{:S(2)}, u32[]{:S(2)}) collective-permute-start(bf16[256,2048]{1,0:T(8,128)(2,1)S(1)} %bitcast.31), channel_id=1, source_target_pairs={{8,0},{9,1},{10,2},{11,3},{12,4},{13,5},{14,6},{15,7},{16,8},{17,9... | collective-permute-start | bytes 3145736 | tf_op jit(solution)/shard_map/ppermute | solution.py:33
  32.2 21.7 %collective-permute-start.1 = (bf16[256,2048]{1,0:T(8,128)(2,1)S(1)}, bf16[256,2048]{1,0:T(8,128)(2,1)}, u32[]{:S(2)}, u32[]{:S(2)}) collective-permute-start(bf16[256,2048]{1,0:T(8,128)(2,1)S(1)} %bitcast.32), channel_id=1, source_target_pairs={{24,0},{25,1},{26,2},{27,3},{28,4},{29,5},{30,6},{31,7},{0,8},{1,9... | collective-permute-start | bytes 3145736 | tf_op jit(solution)/shard_map/ppermute | solution.py:33
  32.2 22.2 %collective-permute-start.2 = (bf16[256,2048]{1,0:T(8,128)(2,1)S(1)}, bf16[256,2048]{1,0:T(8,128)(2,1)}, u32[]{:S(2)}, u32[]{:S(2)}) collective-permute-start(bf16[256,2048]{1,0:T(8,128)(2,1)S(1)} %bitcast.33), channel_id=1, source_target_pairs={{32,0},{33,1},{34,2},{35,3},{36,4},{37,5},{38,6},{39,7},{40,8},{41... | collective-permute-start | bytes 3145736 | tf_op jit(solution)/shard_map/ppermute | solution.py:33
  37.1 20.6 %collective-permute-start.3 = (bf16[256,2048]{1,0:T(8,128)(2,1)S(1)}, bf16[256,2048]{1,0:T(8,128)(2,1)}, u32[]{:S(2)}, u32[]{:S(2)}) collective-permute-start(bf16[256,2048]{1,0:T(8,128)(2,1)S(1)} %bitcast.34), channel_id=1, source_target_pairs={{96,0},{97,1},{98,2},{99,3},{100,4},{101,5},{102,6},{103,7},{104,8... | collective-permute-start | bytes 3145736 | tf_op jit(solution)/shard_map/ppermute | solution.py:33
  37.2 6.8 %collective-permute-start.4 = (s32[4,16,128]{2,1,0:T(8,128)S(1)}, s32[4,16,128]{2,1,0:T(8,128)S(1)}, u32[]{:S(2)}, u32[]{:S(2)}) collective-permute-start(s32[4,16,128]{2,1,0:T(8,128)S(1)} %bitcast.51), channel_id=1, source_target_pairs={{4,0},{5,1},{6,2},{7,3},{0,4},{1,5},{2,6},{3,7},{12,8},{13,9},{14,... | collective-permute-start | bytes 98312 | tf_op jit(solution)/shard_map/ppermute | solution.py:33
  50.2 35.5 %copy-start.1 = (f32[8,16,16,128]{3,2,1,0:T(8,128)S(1)}, f32[8,16,16,128]{3,2,1,0:T(8,128)}, u32[]{:S(2)}) copy-start(f32[8,16,16,128]{3,2,1,0:T(8,128)} %station_counts.1.times_ref) | copy-start | bytes 3145732
  57.7 21.9 %collective-permute-start.5 = (bf16[256,2048]{1,0:T(8,128)(2,1)}, bf16[256,2048]{1,0:T(8,128)(2,1)}, u32[]{:S(2)}, u32[]{:S(2)}) collective-permute-start(bf16[256,2048]{1,0:T(8,128)(2,1)} %collective-permute-done.2.refs_0_), channel_id=1, source_target_pairs={{8,0},{9,1},{10,2},{11,3},{12,4},{13,5},{14,6},{15,7},{16,8},{17,9... | collective-permute-start | bytes 3145736 | tf_op jit(solution)/shard_map/ppermute | solution.py:33
  60.1 22.3 %collective-permute-start.6 = (bf16[256,2048]{1,0:T(8,128)(2,1)}, bf16[256,2048]{1,0:T(8,128)(2,1)}, u32[]{:S(2)}, u32[]{:S(2)}) collective-permute-start(bf16[256,2048]{1,0:T(8,128)(2,1)} %collective-permute-done.3.refs_1_), channel_id=1, source_target_pairs={{24,0},{25,1},{26,2},{27,3},{28,4},{29,5},{30,6},{31,7},{0,8},{1,9... | collective-permute-start | bytes 3145736 | tf_op jit(solution)/shard_map/ppermute | solution.py:33
  60.1 22.3 %collective-permute-start.7 = (bf16[256,2048]{1,0:T(8,128)(2,1)}, bf16[256,2048]{1,0:T(8,128)(2,1)}, u32[]{:S(2)}, u32[]{:S(2)}) collective-permute-start(bf16[256,2048]{1,0:T(8,128)(2,1)} %collective-permute-done.1.refs_2_), channel_id=1, source_target_pairs={{32,0},{33,1},{34,2},{35,3},{36,4},{37,5},{38,6},{39,7},{40,8},{41... | collective-permute-start | bytes 3145736 | tf_op jit(solution)/shard_map/ppermute | solution.py:33
  60.4 22.0 %collective-permute-start.8 = (bf16[256,2048]{1,0:T(8,128)(2,1)S(1)}, bf16[256,2048]{1,0:T(8,128)(2,1)}, u32[]{:S(2)}, u32[]{:S(2)}) collective-permute-start(bf16[256,2048]{1,0:T(8,128)(2,1)S(1)} %collective-permute-done.refs_1_), channel_id=1, source_target_pairs={{96,0},{97,1},{98,2},{99,3},{100,4},{101,5},{102,6},{103,7},{104,8... | collective-permute-start | bytes 3145736 | tf_op jit(solution)/shard_map/ppermute | solution.py:33
  61.6 45.9 %collective-permute-start.11 = (bf16[256,2048]{1,0:T(8,128)(2,1)}, bf16[256,2048]{1,0:T(8,128)(2,1)}, u32[]{:S(2)}, u32[]{:S(2)}) collective-permute-start(bf16[256,2048]{1,0:T(8,128)(2,1)} %collective-permute-done.2.refs_0_), channel_id=1, source_target_pairs={{32,0},{33,1},{34,2},{35,3},{36,4},{37,5},{38,6},{39,7},{40,8},{41... | collective-permute-start | bytes 3145736 | tf_op jit(solution)/shard_map/ppermute | solution.py:33
  65.6 1.2 copy-start
  79.6 28.9 %collective-permute-start.9 = (bf16[256,2048]{1,0:T(8,128)(2,1)S(1)}, bf16[256,2048]{1,0:T(8,128)(2,1)S(1)}, u32[]{:S(2)}, u32[]{:S(2)}) collective-permute-start(bf16[256,2048]{1,0:T(8,128)(2,1)S(1)} %collective-permute-done.refs_1_), channel_id=1, source_target_pairs={{8,0},{9,1},{10,2},{11,3},{12,4},{13,5},{14,6},{15,7},{16,8},{17,9... | collective-permute-start | bytes 3145736 | tf_op jit(solution)/shard_map/ppermute | solution.py:33
  82.4 26.1 %collective-permute-start.10 = (bf16[256,2048]{1,0:T(8,128)(2,1)}, bf16[256,2048]{1,0:T(8,128)(2,1)S(1)}, u32[]{:S(2)}, u32[]{:S(2)}) collective-permute-start(bf16[256,2048]{1,0:T(8,128)(2,1)} %collective-permute-done.6.refs_3_), channel_id=1, source_target_pairs={{24,0},{25,1},{26,2},{27,3},{28,4},{29,5},{30,6},{31,7},{0,8},{1,9... | collective-permute-start | bytes 3145736 | tf_op jit(solution)/shard_map/ppermute | solution.py:33
  82.5 26.0 %collective-permute-start.12 = (bf16[256,2048]{1,0:T(8,128)(2,1)}, bf16[256,2048]{1,0:T(8,128)(2,1)S(1)}, u32[]{:S(2)}, u32[]{:S(2)}) collective-permute-start(bf16[256,2048]{1,0:T(8,128)(2,1)} %collective-permute-done.8.refs_5_), channel_id=1, source_target_pairs={{96,0},{97,1},{98,2},{99,3},{100,4},{101,5},{102,6},{103,7},{104,8... | collective-permute-start | bytes 3145736 | tf_op jit(solution)/shard_map/ppermute | solution.py:33
  83.7 42.5 %collective-permute-start.14 = (bf16[256,2048]{1,0:T(8,128)(2,1)}, bf16[256,2048]{1,0:T(8,128)(2,1)S(1)}, u32[]{:S(2)}, u32[]{:S(2)}) collective-permute-start(bf16[256,2048]{1,0:T(8,128)(2,1)} %collective-permute-done.7.refs_4_), channel_id=1, source_target_pairs={{32,0},{33,1},{34,2},{35,3},{36,4},{37,5},{38,6},{39,7},{40,8},{41... | collective-permute-start | bytes 3145736 | tf_op jit(solution)/shard_map/ppermute | solution.py:33
  107.4 18.8 %collective-permute-start.15 = (bf16[256,2048]{1,0:T(8,128)(2,1)}, bf16[256,2048]{1,0:T(8,128)(2,1)S(1)}, u32[]{:S(2)}, u32[]{:S(2)}) collective-permute-start(bf16[256,2048]{1,0:T(8,128)(2,1)} %collective-permute-done.7.refs_4_), channel_id=1, source_target_pairs={{24,0},{25,1},{26,2},{27,3},{28,4},{29,5},{30,6},{31,7},{0,8},{1,9... | collective-permute-start | bytes 3145736 | tf_op jit(solution)/shard_map/ppermute | solution.py:33
  108.4 17.8 %collective-permute-start.13 = (bf16[256,2048]{1,0:T(8,128)(2,1)S(1)}, bf16[256,2048]{1,0:T(8,128)(2,1)S(1)}, u32[]{:S(2)}, u32[]{:S(2)}) collective-permute-start(bf16[256,2048]{1,0:T(8,128)(2,1)S(1)} %collective-permute-done.12.refs_3_), channel_id=1, source_target_pairs={{8,0},{9,1},{10,2},{11,3},{12,4},{13,5},{14,6},{15,7},{16,8},{17,9... | collective-permute-start | bytes 3145736 | tf_op jit(solution)/shard_map/ppermute | solution.py:33
Sparse Core Ops, SparseCore 0:
  9.5 56.0 all-gather.2

commit v9 on v6

--- a/solution.py
+++ b/solution.py
@@ -220,7 +220,7 @@
             held[offset] = from_offset(held[forwarded], dz=dz, dy=dy)
 
     def meet(number, others):
-        names = [hop[0] for hop in ROUNDS[number]]
+        names = list(held) if number == 1 else [hop[0] for hop in ROUNDS[number]]
         values = lax.optimization_barrier([held[name] for name in names] + list(others))
         held.update(zip(names, values))
         return values[len(names) :]

time: 167 us -> 168 us (level)
  waiting for transfers between devices: 20.3 us -> 23.8 us
    ppermute x16, waiting for transfers between devices: 3.8 us -> 5.8 us  [from_offset(): return lax.ppermute(value, AXES, pairs)]
  transfers between devices with their start and end apart: 18 -> 18, of which waited for: 4 -> 5; matrix products, arithmetic and copies ran while one was open for 5% -> 4% of each run, Pallas kernels for 33% -> 32%
where the time goes in v9:
time: 168 us; the launch traced here: 167 us
  Pallas kernels  65.8 us (39%)
  starting transfers between devices  32.2 us (19%)
  waiting for transfers between devices  23.8 us (14%)
  blocking collectives  16.3 us (10%)
  between operations  13.6 us (8%)
  local copies, waits for them, and re-layouts  9.96 us (6%)
  other arithmetic  5.45 us (3%)
    pallas_call x4, Pallas kernels, predict(): pl.pallas_call(functools.partial(pair_kernel, first_s, count_s), in_specs...  60.8 us
    ppermute x16, starting transfers between devices, from_offset(): return lax.ppermute(value, AXES, pairs)  27.3 us
    all_to_all x1, blocking collectives, body(): made = lax.all_to_all(made, ('c', 'x'), 0, 0, tiled=True)  16.3 us
    all_to_all x1, waiting for transfers between devices, body(): lax.all_to_all(native, 'x', 0, 0, tiled=True)  14 us
    ppermute x16, waiting for transfers between devices, from_offset(): return lax.ppermute(value, AXES, pairs)  5.8 us
    pallas_call x1, Pallas kernels, station_counts(): pl.pallas_call(count_kernel, in_specs=[on_chip], out_specs=on_chip, out_s...  4.94 us
    all_to_all x1, starting transfers between devices, body(): lax.all_to_all(native, 'x', 0, 0, tiled=True)  4.87 us
    unnamed x6, local copies, waits for them, and re-layouts  4.02 us
  transfers between devices with their start and end apart: 18, of which 5 were waited for; matrix products, arithmetic and copies ran while one was open for 4% of the time, Pallas kernels for 32%

profile of v9, /device:TPU:1, one launch (start us, length us, event | category | flops | bytes accessed | tf_op | source)
XLA Modules:
  0.0 167.1 jit_solution(189346217502600621)
XLA Ops:
  6.5 2.8 %copy.21 = bf16[64,4,2048]{2,0,1:T(8,128)(2,1)} copy(bf16[64,4,2048]{2,1,0:T(4,128)(2,1)} %param.5) | data formatting | bytes 2097152 | tf_op args[0]
  9.3 4.9 %all-to-all-start = ((bf16[4,64,2048]{2,1,0:T(8,128)(2,1)}), bf16[4,64,2048]{2,1,0:T(8,128)(2,1)S(1)}, u32[]{:S(2)}, u32[]{:S(2)}) async-start(bf16[4,64,2048]{2,1,0:T(8,128)(2,1)} %bitcast.42), calls=%async_computation | async-start | bytes 2097152 | tf_op jit(solution)/shard_map/all_to_all | solution.py:212
  14.2 1.1 fusion.1
  15.3 14.0 %all-to-all-done = bf16[4,64,2048]{2,1,0:T(8,128)(2,1)S(1)} async-done(((bf16[4,64,2048]{2,1,0:T(8,128)(2,1)}), bf16[4,64,2048]{2,1,0:T(8,128)(2,1)S(1)}, u32[]{:S(2)}, u32[]{:S(2)}) %all-to-all-start) | async-done | bytes 1048608 | tf_op jit(solution)/shard_map/all_to_all | solution.py:212
  29.3 3.0 %collective-permute-start = (bf16[256,2048]{1,0:T(8,128)(2,1)S(1)}, bf16[256,2048]{1,0:T(8,128)(2,1)S(1)}, u32[]{:S(2)}, u32[]{:S(2)}) collective-permute-start(bf16[256,2048]{1,0:T(8,128)(2,1)S(1)} %bitcast.31), channel_id=1, source_target_pairs={{8,0},{9,1},{10,2},{11,3},{12,4},{13,5},{14,6},{15,7},{16,8},{17,9... | collective-permute-start | bytes 3145736 | tf_op jit(solution)/shard_map/ppermute | solution.py:33
  32.2 4.8 %collective-permute-start.2 = (bf16[256,2048]{1,0:T(8,128)(2,1)S(1)}, bf16[256,2048]{1,0:T(8,128)(2,1)}, u32[]{:S(2)}, u32[]{:S(2)}) collective-permute-start(bf16[256,2048]{1,0:T(8,128)(2,1)S(1)} %bitcast.33), channel_id=1, source_target_pairs={{32,0},{33,1},{34,2},{35,3},{36,4},{37,5},{38,6},{39,7},{40,8},{41... | collective-permute-start | bytes 3145736 | tf_op jit(solution)/shard_map/ppermute | solution.py:33
  37.2 5.4 %collective-permute-start.4 = (s32[4,16,128]{2,1,0:T(8,128)S(1)}, s32[4,16,128]{2,1,0:T(8,128)S(1)}, u32[]{:S(2)}, u32[]{:S(2)}) collective-permute-start(s32[4,16,128]{2,1,0:T(8,128)S(1)} %bitcast.51), channel_id=1, source_target_pairs={{4,0},{5,1},{6,2},{7,3},{0,4},{1,5},{2,6},{3,7},{12,8},{13,9},{14,... | collective-permute-start | bytes 98312 | tf_op jit(solution)/shard_map/ppermute | solution.py:33
  44.0 1.2 gather_fusion
  45.3 4.9 %station_counts.1.times_ref = f32[8,16,16,128]{3,2,1,0:T(8,128)} custom-call(s32[8,16,128]{2,1,0:T(8,128)} %bitcast.50), custom_call_target="tpu_custom_call" | custom-call | flops 1000000000 | bytes 1048576 | tf_op jit(solution)/shard_map/station_counts/pallas_call | solution.py:67
  50.2 3.6 %convert_reduce_fusion = s32[8,16,16]{2,1,0:T(8,128)S(1)} fusion(f32[8,16,16,128]{3,2,1,0:T(8,128)} %station_counts.1.times_ref), kind=kLoop, calls=%fused_computation.5 | loop fusion | flops 1570816 | bytes 1056768 | tf_op jit(solution)/shard_map/reduce_max | solution.py:240
  54.5 3.2 %collective-permute-done.3.refs_1_ = bf16[256,2048]{1,0:T(8,128)(2,1)} collective-permute-done((bf16[256,2048]{1,0:T(8,128)(2,1)S(1)}, bf16[256,2048]{1,0:T(8,128)(2,1)}, u32[]{:S(2)}, u32[]{:S(2)}) %collective-permute-start.3) | collective-permute-done | bytes 1048608 | tf_op jit(solution)/shard_map/ppermute | solution.py:33
  57.7 2.4 %collective-permute-start.5 = (bf16[256,2048]{1,0:T(8,128)(2,1)}, bf16[256,2048]{1,0:T(8,128)(2,1)}, u32[]{:S(2)}, u32[]{:S(2)}) collective-permute-start(bf16[256,2048]{1,0:T(8,128)(2,1)} %collective-permute-done.2.refs_0_), channel_id=1, source_target_pairs={{8,0},{9,1},{10,2},{11,3},{12,4},{13,5},{14,6},{15,7},{16,8},{17,9... | collective-permute-start | bytes 3145736 | tf_op jit(solution)/shard_map/ppermute | solution.py:33
  60.4 1.2 collective-permute-start.8
  61.6 4.0 %all-gather.3.cloned.1.call-done = bf16[32,64,2048]{2,1,0:T(8,128)(2,1)} async-done(((bf16[4,64,2048]{2,1,0:T(8,128)(2,1)}), bf16[32,64,2048]{2,1,0:T(8,128)(2,1)}) %all-gather.3.cloned.1.call-update) | async-done | bytes 8388624 | tf_op jit(solution)/shard_map/all_gather | solution.py:213
  65.6 1.2 copy-done
  66.8 13.2 %pairs.4 = f32[8,3,2,128]{3,2,1,0:T(2,128)S(1)} custom-call(s32[8,16]{1,0:T(8,128)S(1)} %shift-left_reduce_fusion.flag_ref, f32[8,16,16,128]{3,2,1,0:T(8,128)S(1)} %copy-done, bf16[2,4,4,64,2048]{4,3,2,1,0:T(8,128)(2,1)} %bitcast.36, bf16[256,2048]{1,0:T(8,128)(2,1)S(1)} %bitcast.35, bf16[256,2048]{1,0:T(8,128)(2,1)S(1)} %collective-permute-done.refs_1_, ...), custom_call_target="tpu_custom_call" | custom-call | flops 2000000000 | bytes 1048576 | tf_op jit(solution)/shard_map/pairs/pallas_call | solution.py:179
  80.5 3.4 %collective-permute-start.11 = (bf16[256,2048]{1,0:T(8,128)(2,1)}, bf16[256,2048]{1,0:T(8,128)(2,1)S(1)}, u32[]{:S(2)}, u32[]{:S(2)}) collective-permute-start(bf16[256,2048]{1,0:T(8,128)(2,1)} %collective-permute-done.2.refs_0_), channel_id=1, source_target_pairs={{32,0},{33,1},{34,2},{35,3},{36,4},{37,5},{38,6},{39,7},{40,8},{41... | collective-permute-start | bytes 3145736 | tf_op jit(solution)/shard_map/ppermute | solution.py:33
  83.9 2.6 %collective-permute-start.9 = (bf16[256,2048]{1,0:T(8,128)(2,1)S(1)}, bf16[256,2048]{1,0:T(8,128)(2,1)S(1)}, u32[]{:S(2)}, u32[]{:S(2)}) collective-permute-start(bf16[256,2048]{1,0:T(8,128)(2,1)S(1)} %collective-permute-done.refs_1_), channel_id=1, source_target_pairs={{8,0},{9,1},{10,2},{11,3},{12,4},{13,5},{14,6},{15,7},{16,8},{17,9... | collective-permute-start | bytes 3145736 | tf_op jit(solution)/shard_map/ppermute | solution.py:33
  86.5 21.8 %pairs.5 = f32[8,6,2,128]{3,2,1,0:T(2,128)S(1)} custom-call(s32[8,16]{1,0:T(8,128)S(1)} %shift-left_reduce_fusion.flag_ref, f32[8,16,16,128]{3,2,1,0:T(8,128)S(1)} %copy-done.1, bf16[2,4,4,64,2048]{4,3,2,1,0:T(8,128)(2,1)} %bitcast.37, bf16[256,2048]{1,0:T(8,128)(2,1)} %collective-permute-done.2.refs_0_, bf16[256,2048]{1,0:T(8,128)(2,1)} %collective-permute-done.3.refs_1_, ...), custom_call_target="tpu_custom_call" | custom-call | flops 2000000000 | bytes 1048576 | tf_op jit(solution)/shard_map/pairs/pallas_call | solution.py:179
  108.4 3.7 %collective-permute-start.13 = (bf16[256,2048]{1,0:T(8,128)(2,1)S(1)}, bf16[256,2048]{1,0:T(8,128)(2,1)S(1)}, u32[]{:S(2)}, u32[]{:S(2)}) collective-permute-start(bf16[256,2048]{1,0:T(8,128)(2,1)S(1)} %collective-permute-done.12.refs_3_), channel_id=1, source_target_pairs={{8,0},{9,1},{10,2},{11,3},{12,4},{13,5},{14,6},{15,7},{16,8},{17,9... | collective-permute-start | bytes 3145736 | tf_op jit(solution)/shard_map/ppermute | solution.py:33
  112.1 14.3 %pairs.6 = f32[8,4,2,128]{3,2,1,0:T(2,128)S(1)} custom-call(s32[8,16]{1,0:T(8,128)S(1)} %shift-left_reduce_fusion.flag_ref, f32[8,16,16,128]{3,2,1,0:T(8,128)S(1)} %copy-done.1, bf16[2,4,4,64,2048]{4,3,2,1,0:T(8,128)(2,1)} %bitcast.38, bf16[256,2048]{1,0:T(8,128)(2,1)S(1)} %collective-permute-done.9.refs_0_, ...), custom_call_target="tpu_custom_call" | custom-call | flops 2000000000 | bytes 1048576 | tf_op jit(solution)/shard_map/pairs/pallas_call | solution.py:179
  126.4 2.0 %collective-permute-done.15.refs_2_ = bf16[256,2048]{1,0:T(8,128)(2,1)S(1)} collective-permute-done((bf16[256,2048]{1,0:T(8,128)(2,1)}, bf16[256,2048]{1,0:T(8,128)(2,1)S(1)}, u32[]{:S(2)}, u32[]{:S(2)}) %collective-permute-start.15) | collective-permute-done | bytes 1048608 | tf_op jit(solution)/shard_map/ppermute | solution.py:33
  128.4 11.6 %pairs.7 = f32[8,3,2,128]{3,2,1,0:T(2,128)S(1)} custom-call(s32[8,16]{1,0:T(8,128)S(1)} %shift-left_reduce_fusion.flag_ref, f32[8,16,16,128]{3,2,1,0:T(8,128)S(1)} %copy-done.1, bf16[2,4,4,64,2048]{4,3,2,1,0:T(8,128)(2,1)} %bitcast.39, bf16[256,2048]{1,0:T(8,128)(2,1)S(1)} %collective-permute-done.13.refs_0_, ...), custom_call_target="tpu_custom_call" | custom-call | flops 2000000000 | bytes 1048576 | tf_op jit(solution)/shard_map/pairs/pallas_call | solution.py:179
  142.1 16.3 %all_to_all.10 = f32[8,32,128]{2,1,0:T(8,128)S(1)} all-to-all(f32[8,32,128]{2,1,0:T(8,128)S(1)} %reshape.73), channel_id=1, replica_groups=mesh['z'=4,'y'=4,'c'=2,'x'=4] {'c','x'}, dimensions={0} | all-to-all | bytes 262144 | tf_op jit(solution)/shard_map/all_to_all | solution.py:256
  (46 shorter events, 6.9 us)
Async XLA Ops:
  6.5 59.0 %all-gather.3.cloned.1.call-start = ((), (), s32[]{:S(2)}) async-start(), calls=%async_computation.2 | async-start | bytes 9437184 | tf_op jit(solution)/shard_map/all_gather | solution.py:213
  9.3 19.9 %all-to-all-start = ((bf16[4,64,2048]{2,1,0:T(8,128)(2,1)}), bf16[4,64,2048]{2,1,0:T(8,128)(2,1)S(1)}, u32[]{:S(2)}, u32[]{:S(2)}) async-start(bf16[4,64,2048]{2,1,0:T(8,128)(2,1)} %bitcast.42), calls=%async_computation | async-start | bytes 2097152 | tf_op jit(solution)/shard_map/all_to_all | solution.py:212
  29.3 24.6 %collective-permute-start = (bf16[256,2048]{1,0:T(8,128)(2,1)S(1)}, bf16[256,2048]{1,0:T(8,128)(2,1)S(1)}, u32[]{:S(2)}, u32[]{:S(2)}) collective-permute-start(bf16[256,2048]{1,0:T(8,128)(2,1)S(1)} %bitcast.31), channel_id=1, source_target_pairs={{8,0},{9,1},{10,2},{11,3},{12,4},{13,5},{14,6},{15,7},{16,8},{17,9... | collective-permute-start | bytes 3145736 | tf_op jit(solution)/shard_map/ppermute | solution.py:33
  32.2 21.7 %collective-permute-start.1 = (bf16[256,2048]{1,0:T(8,128)(2,1)S(1)}, bf16[256,2048]{1,0:T(8,128)(2,1)}, u32[]{:S(2)}, u32[]{:S(2)}) collective-permute-start(bf16[256,2048]{1,0:T(8,128)(2,1)S(1)} %bitcast.32), channel_id=1, source_target_pairs={{24,0},{25,1},{26,2},{27,3},{28,4},{29,5},{30,6},{31,7},{0,8},{1,9... | collective-permute-start | bytes 3145736 | tf_op jit(solution)/shard_map/ppermute | solution.py:33
  32.2 22.2 %collective-permute-start.2 = (bf16[256,2048]{1,0:T(8,128)(2,1)S(1)}, bf16[256,2048]{1,0:T(8,128)(2,1)}, u32[]{:S(2)}, u32[]{:S(2)}) collective-permute-start(bf16[256,2048]{1,0:T(8,128)(2,1)S(1)} %bitcast.33), channel_id=1, source_target_pairs={{32,0},{33,1},{34,2},{35,3},{36,4},{37,5},{38,6},{39,7},{40,8},{41... | collective-permute-start | bytes 3145736 | tf_op jit(solution)/shard_map/ppermute | solution.py:33
  37.1 20.6 %collective-permute-start.3 = (bf16[256,2048]{1,0:T(8,128)(2,1)S(1)}, bf16[256,2048]{1,0:T(8,128)(2,1)}, u32[]{:S(2)}, u32[]{:S(2)}) collective-permute-start(bf16[256,2048]{1,0:T(8,128)(2,1)S(1)} %bitcast.34), channel_id=1, source_target_pairs={{96,0},{97,1},{98,2},{99,3},{100,4},{101,5},{102,6},{103,7},{104,8... | collective-permute-start | bytes 3145736 | tf_op jit(solution)/shard_map/ppermute | solution.py:33
  37.2 6.8 %collective-permute-start.4 = (s32[4,16,128]{2,1,0:T(8,128)S(1)}, s32[4,16,128]{2,1,0:T(8,128)S(1)}, u32[]{:S(2)}, u32[]{:S(2)}) collective-permute-start(s32[4,16,128]{2,1,0:T(8,128)S(1)} %bitcast.51), channel_id=1, source_target_pairs={{4,0},{5,1},{6,2},{7,3},{0,4},{1,5},{2,6},{3,7},{12,8},{13,9},{14,... | collective-permute-start | bytes 98312 | tf_op jit(solution)/shard_map/ppermute | solution.py:33
  50.2 36.3 %copy-start.1 = (f32[8,16,16,128]{3,2,1,0:T(8,128)S(1)}, f32[8,16,16,128]{3,2,1,0:T(8,128)}, u32[]{:S(2)}) copy-start(f32[8,16,16,128]{3,2,1,0:T(8,128)} %station_counts.1.times_ref) | copy-start | bytes 3145732
  57.7 22.3 %collective-permute-start.5 = (bf16[256,2048]{1,0:T(8,128)(2,1)}, bf16[256,2048]{1,0:T(8,128)(2,1)}, u32[]{:S(2)}, u32[]{:S(2)}) collective-permute-start(bf16[256,2048]{1,0:T(8,128)(2,1)} %collective-permute-done.2.refs_0_), channel_id=1, source_target_pairs={{8,0},{9,1},{10,2},{11,3},{12,4},{13,5},{14,6},{15,7},{16,8},{17,9... | collective-permute-start | bytes 3145736 | tf_op jit(solution)/shard_map/ppermute | solution.py:33
  60.1 19.9 %collective-permute-start.6 = (bf16[256,2048]{1,0:T(8,128)(2,1)}, bf16[256,2048]{1,0:T(8,128)(2,1)}, u32[]{:S(2)}, u32[]{:S(2)}) collective-permute-start(bf16[256,2048]{1,0:T(8,128)(2,1)} %collective-permute-done.3.refs_1_), channel_id=1, source_target_pairs={{24,0},{25,1},{26,2},{27,3},{28,4},{29,5},{30,6},{31,7},{0,8},{1,9... | collective-permute-start | bytes 3145736 | tf_op jit(solution)/shard_map/ppermute | solution.py:33
  60.1 19.9 %collective-permute-start.7 = (bf16[256,2048]{1,0:T(8,128)(2,1)}, bf16[256,2048]{1,0:T(8,128)(2,1)}, u32[]{:S(2)}, u32[]{:S(2)}) collective-permute-start(bf16[256,2048]{1,0:T(8,128)(2,1)} %collective-permute-done.1.refs_2_), channel_id=1, source_target_pairs={{32,0},{33,1},{34,2},{35,3},{36,4},{37,5},{38,6},{39,7},{40,8},{41... | collective-permute-start | bytes 3145736 | tf_op jit(solution)/shard_map/ppermute | solution.py:33
  60.4 19.7 %collective-permute-start.8 = (bf16[256,2048]{1,0:T(8,128)(2,1)S(1)}, bf16[256,2048]{1,0:T(8,128)(2,1)}, u32[]{:S(2)}, u32[]{:S(2)}) collective-permute-start(bf16[256,2048]{1,0:T(8,128)(2,1)S(1)} %collective-permute-done.refs_1_), channel_id=1, source_target_pairs={{96,0},{97,1},{98,2},{99,3},{100,4},{101,5},{102,6},{103,7},{104,8... | collective-permute-start | bytes 3145736 | tf_op jit(solution)/shard_map/ppermute | solution.py:33
  65.6 1.2 copy-start
  80.0 28.2 %collective-permute-start.10 = (bf16[256,2048]{1,0:T(8,128)(2,1)}, bf16[256,2048]{1,0:T(8,128)(2,1)S(1)}, u32[]{:S(2)}, u32[]{:S(2)}) collective-permute-start(bf16[256,2048]{1,0:T(8,128)(2,1)} %collective-permute-done.6.refs_3_), channel_id=1, source_target_pairs={{24,0},{25,1},{26,2},{27,3},{28,4},{29,5},{30,6},{31,7},{0,8},{1,9... | collective-permute-start | bytes 3145736 | tf_op jit(solution)/shard_map/ppermute | solution.py:33
  80.5 27.9 %collective-permute-start.11 = (bf16[256,2048]{1,0:T(8,128)(2,1)}, bf16[256,2048]{1,0:T(8,128)(2,1)S(1)}, u32[]{:S(2)}, u32[]{:S(2)}) collective-permute-start(bf16[256,2048]{1,0:T(8,128)(2,1)} %collective-permute-done.2.refs_0_), channel_id=1, source_target_pairs={{32,0},{33,1},{34,2},{35,3},{36,4},{37,5},{38,6},{39,7},{40,8},{41... | collective-permute-start | bytes 3145736 | tf_op jit(solution)/shard_map/ppermute | solution.py:33
  83.9 24.5 %collective-permute-start.12 = (bf16[256,2048]{1,0:T(8,128)(2,1)}, bf16[256,2048]{1,0:T(8,128)(2,1)S(1)}, u32[]{:S(2)}, u32[]{:S(2)}) collective-permute-start(bf16[256,2048]{1,0:T(8,128)(2,1)} %collective-permute-done.8.refs_5_), channel_id=1, source_target_pairs={{96,0},{97,1},{98,2},{99,3},{100,4},{101,5},{102,6},{103,7},{104,8... | collective-permute-start | bytes 3145736 | tf_op jit(solution)/shard_map/ppermute | solution.py:33
  83.9 24.5 %collective-permute-start.9 = (bf16[256,2048]{1,0:T(8,128)(2,1)S(1)}, bf16[256,2048]{1,0:T(8,128)(2,1)S(1)}, u32[]{:S(2)}, u32[]{:S(2)}) collective-permute-start(bf16[256,2048]{1,0:T(8,128)(2,1)S(1)} %collective-permute-done.refs_1_), channel_id=1, source_target_pairs={{8,0},{9,1},{10,2},{11,3},{12,4},{13,5},{14,6},{15,7},{16,8},{17,9... | collective-permute-start | bytes 3145736 | tf_op jit(solution)/shard_map/ppermute | solution.py:33
  86.5 39.9 %collective-permute-start.14 = (bf16[256,2048]{1,0:T(8,128)(2,1)}, bf16[256,2048]{1,0:T(8,128)(2,1)S(1)}, u32[]{:S(2)}, u32[]{:S(2)}) collective-permute-start(bf16[256,2048]{1,0:T(8,128)(2,1)} %collective-permute-done.7.refs_4_), channel_id=1, source_target_pairs={{24,0},{25,1},{26,2},{27,3},{28,4},{29,5},{30,6},{31,7},{0,8},{1,9... | collective-permute-start | bytes 3145736 | tf_op jit(solution)/shard_map/ppermute | solution.py:33
  108.3 20.1 %collective-permute-start.15 = (bf16[256,2048]{1,0:T(8,128)(2,1)}, bf16[256,2048]{1,0:T(8,128)(2,1)S(1)}, u32[]{:S(2)}, u32[]{:S(2)}) collective-permute-start(bf16[256,2048]{1,0:T(8,128)(2,1)} %collective-permute-done.6.refs_3_), channel_id=1, source_target_pairs={{96,0},{97,1},{98,2},{99,3},{100,4},{101,5},{102,6},{103,7},{104,8... | collective-permute-start | bytes 3145736 | tf_op jit(solution)/shard_map/ppermute | solution.py:33
  108.4 20.0 %collective-permute-start.13 = (bf16[256,2048]{1,0:T(8,128)(2,1)S(1)}, bf16[256,2048]{1,0:T(8,128)(2,1)S(1)}, u32[]{:S(2)}, u32[]{:S(2)}) collective-permute-start(bf16[256,2048]{1,0:T(8,128)(2,1)S(1)} %collective-permute-done.12.refs_3_), channel_id=1, source_target_pairs={{8,0},{9,1},{10,2},{11,3},{12,4},{13,5},{14,6},{15,7},{16,8},{17,9... | collective-permute-start | bytes 3145736 | tf_op jit(solution)/shard_map/ppermute | solution.py:33
Sparse Core Ops, SparseCore 0:
  9.5 56.0 all-gather.2

commit v10 on v9

--- a/solution.py
+++ b/solution.py
@@ -243,9 +243,9 @@
     flags, made_row = meet(0, (flags, made_row))
 
     travel(1)
-    blocks += meet(1, [made_of(0, 3)])
+    blocks += meet(1, [made_of(0, 4)])
     travel(2)
-    blocks += meet(2, [made_of(3, 6)])
+    blocks += meet(2, [made_of(4, 5)])
     travel(3)
     blocks += meet(3, [made_of(9, 4)])
     blocks.append(made_of(13, 3))

time: 168 us -> 170 us (1.012)
  waiting for transfers between devices: 23.8 us -> 32.8 us
  blocking collectives: 16.3 us -> 11.5 us
  starting transfers between devices: 32.2 us -> 29.8 us
    ppermute x16, waiting for transfers between devices: 5.8 us -> 14.8 us  [from_offset(): return lax.ppermute(value, AXES, pairs)]
    all_to_all x1, blocking collectives: 16.3 us -> 11.5 us  [body(): made = lax.all_to_all(made, ('c', 'x'), 0, 0, tiled=True)]
    ppermute x16, starting transfers between devices: 27.3 us -> 24.9 us  [from_offset(): return lax.ppermute(value, AXES, pairs)]
  transfers between devices with their start and end apart: 18 -> 18, of which waited for: 5 -> 9; matrix products, arithmetic and copies ran while one was open for 4% -> 4% of each run, Pallas kernels for 32% -> 31%
where the time goes in v10:
time: 170 us; the launch traced here: 168 us
  Pallas kernels  65.2 us (38%)
  waiting for transfers between devices  32.8 us (19%)
  starting transfers between devices  29.8 us (18%)
  between operations  13.6 us (8%)
  blocking collectives  11.5 us (7%)
  local copies, waits for them, and re-layouts  9.96 us (6%)
  other arithmetic  5.45 us (3%)
    pallas_call x4, Pallas kernels, predict(): pl.pallas_call(functools.partial(pair_kernel, first_s, count_s), in_specs...  60.2 us
    ppermute x16, starting transfers between devices, from_offset(): return lax.ppermute(value, AXES, pairs)  24.9 us
    ppermute x16, waiting for transfers between devices, from_offset(): return lax.ppermute(value, AXES, pairs)  14.8 us
    all_to_all x1, waiting for transfers between devices, body(): lax.all_to_all(native, 'x', 0, 0, tiled=True)  14 us
    all_to_all x1, blocking collectives, body(): made = lax.all_to_all(made, ('c', 'x'), 0, 0, tiled=True)  11.5 us
    pallas_call x1, Pallas kernels, station_counts(): pl.pallas_call(count_kernel, in_specs=[on_chip], out_specs=on_chip, out_s...  4.94 us
    all_to_all x1, starting transfers between devices, body(): lax.all_to_all(native, 'x', 0, 0, tiled=True)  4.87 us
    unnamed x6, local copies, waits for them, and re-layouts  4.02 us
  transfers between devices with their start and end apart: 18, of which 9 were waited for; matrix products, arithmetic and copies ran while one was open for 4% of the time, Pallas kernels for 31%

profile of v10, /device:TPU:1, one launch (start us, length us, event | category | flops | bytes accessed | tf_op | source)
XLA Modules:
  0.0 168.3 jit_solution(18316219361926292200)
XLA Ops:
  6.5 2.8 %copy.21 = bf16[64,4,2048]{2,0,1:T(8,128)(2,1)} copy(bf16[64,4,2048]{2,1,0:T(4,128)(2,1)} %param.5) | data formatting | bytes 2097152 | tf_op args[0]
  9.3 4.9 %all-to-all-start = ((bf16[4,64,2048]{2,1,0:T(8,128)(2,1)}), bf16[4,64,2048]{2,1,0:T(8,128)(2,1)S(1)}, u32[]{:S(2)}, u32[]{:S(2)}) async-start(bf16[4,64,2048]{2,1,0:T(8,128)(2,1)} %bitcast.42), calls=%async_computation | async-start | bytes 2097152 | tf_op jit(solution)/shard_map/all_to_all | solution.py:212
  15.3 14.0 %all-to-all-done = bf16[4,64,2048]{2,1,0:T(8,128)(2,1)S(1)} async-done(((bf16[4,64,2048]{2,1,0:T(8,128)(2,1)}), bf16[4,64,2048]{2,1,0:T(8,128)(2,1)S(1)}, u32[]{:S(2)}, u32[]{:S(2)}) %all-to-all-start) | async-done | bytes 1048608 | tf_op jit(solution)/shard_map/all_to_all | solution.py:212
  29.3 3.0 %collective-permute-start = (bf16[256,2048]{1,0:T(8,128)(2,1)S(1)}, bf16[256,2048]{1,0:T(8,128)(2,1)S(1)}, u32[]{:S(2)}, u32[]{:S(2)}) collective-permute-start(bf16[256,2048]{1,0:T(8,128)(2,1)S(1)} %bitcast.31), channel_id=1, source_target_pairs={{8,0},{9,1},{10,2},{11,3},{12,4},{13,5},{14,6},{15,7},{16,8},{17,9... | collective-permute-start | bytes 3145736 | tf_op jit(solution)/shard_map/ppermute | solution.py:33
  32.2 4.8 %collective-permute-start.2 = (bf16[256,2048]{1,0:T(8,128)(2,1)S(1)}, bf16[256,2048]{1,0:T(8,128)(2,1)}, u32[]{:S(2)}, u32[]{:S(2)}) collective-permute-start(bf16[256,2048]{1,0:T(8,128)(2,1)S(1)} %bitcast.33), channel_id=1, source_target_pairs={{32,0},{33,1},{34,2},{35,3},{36,4},{37,5},{38,6},{39,7},{40,8},{41... | collective-permute-start | bytes 3145736 | tf_op jit(solution)/shard_map/ppermute | solution.py:33
  37.2 5.4 %collective-permute-start.4 = (s32[4,16,128]{2,1,0:T(8,128)S(1)}, s32[4,16,128]{2,1,0:T(8,128)S(1)}, u32[]{:S(2)}, u32[]{:S(2)}) collective-permute-start(s32[4,16,128]{2,1,0:T(8,128)S(1)} %bitcast.51), channel_id=1, source_target_pairs={{4,0},{5,1},{6,2},{7,3},{0,4},{1,5},{2,6},{3,7},{12,8},{13,9},{14,... | collective-permute-start | bytes 98312 | tf_op jit(solution)/shard_map/ppermute | solution.py:33
  44.0 1.2 gather_fusion
  45.3 4.9 %station_counts.1.times_ref = f32[8,16,16,128]{3,2,1,0:T(8,128)} custom-call(s32[8,16,128]{2,1,0:T(8,128)} %bitcast.50), custom_call_target="tpu_custom_call" | custom-call | flops 1000000000 | bytes 1048576 | tf_op jit(solution)/shard_map/station_counts/pallas_call | solution.py:67
  50.2 3.6 %convert_reduce_fusion = s32[8,16,16]{2,1,0:T(8,128)S(1)} fusion(f32[8,16,16,128]{3,2,1,0:T(8,128)} %station_counts.1.times_ref), kind=kLoop, calls=%fused_computation.5 | loop fusion | flops 1570816 | bytes 1056768 | tf_op jit(solution)/shard_map/reduce_max | solution.py:240
  54.5 3.2 %collective-permute-done.3.refs_0_ = bf16[256,2048]{1,0:T(8,128)(2,1)} collective-permute-done((bf16[256,2048]{1,0:T(8,128)(2,1)S(1)}, bf16[256,2048]{1,0:T(8,128)(2,1)}, u32[]{:S(2)}, u32[]{:S(2)}) %collective-permute-start.3) | collective-permute-done | bytes 1048608 | tf_op jit(solution)/shard_map/ppermute | solution.py:33
  57.7 2.4 %collective-permute-start.5 = (bf16[256,2048]{1,0:T(8,128)(2,1)}, bf16[256,2048]{1,0:T(8,128)(2,1)}, u32[]{:S(2)}, u32[]{:S(2)}) collective-permute-start(bf16[256,2048]{1,0:T(8,128)(2,1)} %collective-permute-done.2.refs_3_), channel_id=1, source_target_pairs={{8,0},{9,1},{10,2},{11,3},{12,4},{13,5},{14,6},{15,7},{16,8},{17,9... | collective-permute-start | bytes 3145736 | tf_op jit(solution)/shard_map/ppermute | solution.py:33
  60.4 1.2 collective-permute-start.8
  61.6 4.0 %all-gather.3.cloned.1.call-done = bf16[32,64,2048]{2,1,0:T(8,128)(2,1)} async-done(((bf16[4,64,2048]{2,1,0:T(8,128)(2,1)}), bf16[32,64,2048]{2,1,0:T(8,128)(2,1)}) %all-gather.3.cloned.1.call-update) | async-done | bytes 8388624 | tf_op jit(solution)/shard_map/all_gather | solution.py:213
  65.6 1.2 copy-done
  66.8 15.3 %pairs.4 = f32[8,4,2,128]{3,2,1,0:T(2,128)S(1)} custom-call(s32[8,16]{1,0:T(8,128)S(1)} %shift-left_reduce_fusion.flag_ref, f32[8,16,16,128]{3,2,1,0:T(8,128)S(1)} %copy-done, bf16[2,4,4,64,2048]{4,3,2,1,0:T(8,128)(2,1)} %bitcast.36, bf16[256,2048]{1,0:T(8,128)(2,1)S(1)} %bitcast.35, bf16[256,2048]{1,0:T(8,128)(2,1)S(1)} %collective-permute-done.refs_1_, ...), custom_call_target="tpu_custom_call" | custom-call | flops 2000000000 | bytes 1048576 | tf_op jit(solution)/shard_map/pairs/pallas_call | solution.py:179
  82.6 4.2 %collective-permute-start.11 = (bf16[256,2048]{1,0:T(8,128)(2,1)}, bf16[256,2048]{1,0:T(8,128)(2,1)S(1)}, u32[]{:S(2)}, u32[]{:S(2)}) collective-permute-start(bf16[256,2048]{1,0:T(8,128)(2,1)} %collective-permute-done.2.refs_3_), channel_id=1, source_target_pairs={{32,0},{33,1},{34,2},{35,3},{36,4},{37,5},{38,6},{39,7},{40,8},{41... | collective-permute-start | bytes 3145736 | tf_op jit(solution)/shard_map/ppermute | solution.py:33
  86.8 2.0 %collective-permute-start.9 = (bf16[256,2048]{1,0:T(8,128)(2,1)S(1)}, bf16[256,2048]{1,0:T(8,128)(2,1)S(1)}, u32[]{:S(2)}, u32[]{:S(2)}) collective-permute-start(bf16[256,2048]{1,0:T(8,128)(2,1)S(1)} %collective-permute-done.refs_1_), channel_id=1, source_target_pairs={{8,0},{9,1},{10,2},{11,3},{12,4},{13,5},{14,6},{15,7},{16,8},{17,9... | collective-permute-start | bytes 3145736 | tf_op jit(solution)/shard_map/ppermute | solution.py:33
  88.7 18.7 %pairs.5 = f32[8,5,2,128]{3,2,1,0:T(2,128)S(1)} custom-call(s32[8,16]{1,0:T(8,128)S(1)} %shift-left_reduce_fusion.flag_ref, f32[8,16,16,128]{3,2,1,0:T(8,128)S(1)} %copy-done.1, bf16[2,4,4,64,2048]{4,3,2,1,0:T(8,128)(2,1)} %bitcast.37, bf16[256,2048]{1,0:T(8,128)(2,1)} %collective-permute-done.3.refs_0_, bf16[256,2048]{1,0:T(8,128)(2,1)} %collective-permute-done.5.refs_1_, ...), custom_call_target="tpu_custom_call" | custom-call | flops 2000000000 | bytes 1048576 | tf_op jit(solution)/shard_map/pairs/pallas_call | solution.py:179
  108.5 3.0 %collective-permute-done.12.refs_3_ = bf16[256,2048]{1,0:T(8,128)(2,1)S(1)} collective-permute-done((bf16[256,2048]{1,0:T(8,128)(2,1)}, bf16[256,2048]{1,0:T(8,128)(2,1)S(1)}, u32[]{:S(2)}, u32[]{:S(2)}) %collective-permute-start.12) | collective-permute-done | bytes 1048608 | tf_op jit(solution)/shard_map/ppermute | solution.py:33
  112.6 13.4 %pairs.6 = f32[8,4,2,128]{3,2,1,0:T(2,128)S(1)} custom-call(s32[8,16]{1,0:T(8,128)S(1)} %shift-left_reduce_fusion.flag_ref, f32[8,16,16,128]{3,2,1,0:T(8,128)S(1)} %copy-done.1, bf16[2,4,4,64,2048]{4,3,2,1,0:T(8,128)(2,1)} %bitcast.38, bf16[256,2048]{1,0:T(8,128)(2,1)S(1)} %collective-permute-done.9.refs_0_, ...), custom_call_target="tpu_custom_call" | custom-call | flops 2000000000 | bytes 1048576 | tf_op jit(solution)/shard_map/pairs/pallas_call | solution.py:179
  126.6 3.2 %collective-permute-done.15.refs_2_ = bf16[256,2048]{1,0:T(8,128)(2,1)S(1)} collective-permute-done((bf16[256,2048]{1,0:T(8,128)(2,1)}, bf16[256,2048]{1,0:T(8,128)(2,1)S(1)}, u32[]{:S(2)}, u32[]{:S(2)}) %collective-permute-start.15) | collective-permute-done | bytes 1048608 | tf_op jit(solution)/shard_map/ppermute | solution.py:33
  129.8 3.4 %collective-permute-done.13.refs_0_ = bf16[256,2048]{1,0:T(8,128)(2,1)S(1)} collective-permute-done((bf16[256,2048]{1,0:T(8,128)(2,1)S(1)}, bf16[256,2048]{1,0:T(8,128)(2,1)S(1)}, u32[]{:S(2)}, u32[]{:S(2)}) %collective-permute-start.13) | collective-permute-done | bytes 1048608 | tf_op jit(solution)/shard_map/ppermute | solution.py:33
  133.2 12.8 %pairs.7 = f32[8,3,2,128]{3,2,1,0:T(2,128)S(1)} custom-call(s32[8,16]{1,0:T(8,128)S(1)} %shift-left_reduce_fusion.flag_ref, f32[8,16,16,128]{3,2,1,0:T(8,128)S(1)} %copy-done.1, bf16[2,4,4,64,2048]{4,3,2,1,0:T(8,128)(2,1)} %bitcast.39, bf16[256,2048]{1,0:T(8,128)(2,1)S(1)} %collective-permute-done.13.refs_0_, ...), custom_call_target="tpu_custom_call" | custom-call | flops 2000000000 | bytes 1048576 | tf_op jit(solution)/shard_map/pairs/pallas_call | solution.py:179
  148.1 11.5 %all_to_all.10 = f32[8,32,128]{2,1,0:T(8,128)S(1)} all-to-all(f32[8,32,128]{2,1,0:T(8,128)S(1)} %reshape.73), channel_id=1, replica_groups=mesh['z'=4,'y'=4,'c'=2,'x'=4] {'c','x'}, dimensions={0} | all-to-all | bytes 262144 | tf_op jit(solution)/shard_map/all_to_all | solution.py:256
  (46 shorter events, 10.6 us)
Async XLA Ops:
  6.5 59.0 %all-gather.3.cloned.1.call-start = ((), (), s32[]{:S(2)}) async-start(), calls=%async_computation.2 | async-start | bytes 9437184 | tf_op jit(solution)/shard_map/all_gather | solution.py:213
  9.3 19.9 %all-to-all-start = ((bf16[4,64,2048]{2,1,0:T(8,128)(2,1)}), bf16[4,64,2048]{2,1,0:T(8,128)(2,1)S(1)}, u32[]{:S(2)}, u32[]{:S(2)}) async-start(bf16[4,64,2048]{2,1,0:T(8,128)(2,1)} %bitcast.42), calls=%async_computation | async-start | bytes 2097152 | tf_op jit(solution)/shard_map/all_to_all | solution.py:212
  29.3 24.6 %collective-permute-start = (bf16[256,2048]{1,0:T(8,128)(2,1)S(1)}, bf16[256,2048]{1,0:T(8,128)(2,1)S(1)}, u32[]{:S(2)}, u32[]{:S(2)}) collective-permute-start(bf16[256,2048]{1,0:T(8,128)(2,1)S(1)} %bitcast.31), channel_id=1, source_target_pairs={{8,0},{9,1},{10,2},{11,3},{12,4},{13,5},{14,6},{15,7},{16,8},{17,9... | collective-permute-start | bytes 3145736 | tf_op jit(solution)/shard_map/ppermute | solution.py:33
  32.2 21.7 %collective-permute-start.1 = (bf16[256,2048]{1,0:T(8,128)(2,1)S(1)}, bf16[256,2048]{1,0:T(8,128)(2,1)}, u32[]{:S(2)}, u32[]{:S(2)}) collective-permute-start(bf16[256,2048]{1,0:T(8,128)(2,1)S(1)} %bitcast.32), channel_id=1, source_target_pairs={{24,0},{25,1},{26,2},{27,3},{28,4},{29,5},{30,6},{31,7},{0,8},{1,9... | collective-permute-start | bytes 3145736 | tf_op jit(solution)/shard_map/ppermute | solution.py:33
  32.2 22.2 %collective-permute-start.2 = (bf16[256,2048]{1,0:T(8,128)(2,1)S(1)}, bf16[256,2048]{1,0:T(8,128)(2,1)}, u32[]{:S(2)}, u32[]{:S(2)}) collective-permute-start(bf16[256,2048]{1,0:T(8,128)(2,1)S(1)} %bitcast.33), channel_id=1, source_target_pairs={{32,0},{33,1},{34,2},{35,3},{36,4},{37,5},{38,6},{39,7},{40,8},{41... | collective-permute-start | bytes 3145736 | tf_op jit(solution)/shard_map/ppermute | solution.py:33
  37.1 20.6 %collective-permute-start.3 = (bf16[256,2048]{1,0:T(8,128)(2,1)S(1)}, bf16[256,2048]{1,0:T(8,128)(2,1)}, u32[]{:S(2)}, u32[]{:S(2)}) collective-permute-start(bf16[256,2048]{1,0:T(8,128)(2,1)S(1)} %bitcast.34), channel_id=1, source_target_pairs={{96,0},{97,1},{98,2},{99,3},{100,4},{101,5},{102,6},{103,7},{104,8... | collective-permute-start | bytes 3145736 | tf_op jit(solution)/shard_map/ppermute | solution.py:33
  37.2 6.8 %collective-permute-start.4 = (s32[4,16,128]{2,1,0:T(8,128)S(1)}, s32[4,16,128]{2,1,0:T(8,128)S(1)}, u32[]{:S(2)}, u32[]{:S(2)}) collective-permute-start(s32[4,16,128]{2,1,0:T(8,128)S(1)} %bitcast.51), channel_id=1, source_target_pairs={{4,0},{5,1},{6,2},{7,3},{0,4},{1,5},{2,6},{3,7},{12,8},{13,9},{14,... | collective-permute-start | bytes 98312 | tf_op jit(solution)/shard_map/ppermute | solution.py:33
  50.2 38.5 %copy-start.1 = (f32[8,16,16,128]{3,2,1,0:T(8,128)S(1)}, f32[8,16,16,128]{3,2,1,0:T(8,128)}, u32[]{:S(2)}) copy-start(f32[8,16,16,128]{3,2,1,0:T(8,128)} %station_counts.1.times_ref) | copy-start | bytes 3145732
  57.7 24.4 %collective-permute-start.5 = (bf16[256,2048]{1,0:T(8,128)(2,1)}, bf16[256,2048]{1,0:T(8,128)(2,1)}, u32[]{:S(2)}, u32[]{:S(2)}) collective-permute-start(bf16[256,2048]{1,0:T(8,128)(2,1)} %collective-permute-done.2.refs_3_), channel_id=1, source_target_pairs={{8,0},{9,1},{10,2},{11,3},{12,4},{13,5},{14,6},{15,7},{16,8},{17,9... | collective-permute-start | bytes 3145736 | tf_op jit(solution)/shard_map/ppermute | solution.py:33
  60.1 22.0 %collective-permute-start.6 = (bf16[256,2048]{1,0:T(8,128)(2,1)}, bf16[256,2048]{1,0:T(8,128)(2,1)}, u32[]{:S(2)}, u32[]{:S(2)}) collective-permute-start(bf16[256,2048]{1,0:T(8,128)(2,1)} %collective-permute-done.3.refs_0_), channel_id=1, source_target_pairs={{24,0},{25,1},{26,2},{27,3},{28,4},{29,5},{30,6},{31,7},{0,8},{1,9... | collective-permute-start | bytes 3145736 | tf_op jit(solution)/shard_map/ppermute | solution.py:33
  60.1 22.0 %collective-permute-start.7 = (bf16[256,2048]{1,0:T(8,128)(2,1)}, bf16[256,2048]{1,0:T(8,128)(2,1)}, u32[]{:S(2)}, u32[]{:S(2)}) collective-permute-start(bf16[256,2048]{1,0:T(8,128)(2,1)} %collective-permute-done.1.refs_2_), channel_id=1, source_target_pairs={{32,0},{33,1},{34,2},{35,3},{36,4},{37,5},{38,6},{39,7},{40,8},{41... | collective-permute-start | bytes 3145736 | tf_op jit(solution)/shard_map/ppermute | solution.py:33
  60.4 21.7 %collective-permute-start.8 = (bf16[256,2048]{1,0:T(8,128)(2,1)S(1)}, bf16[256,2048]{1,0:T(8,128)(2,1)}, u32[]{:S(2)}, u32[]{:S(2)}) collective-permute-start(bf16[256,2048]{1,0:T(8,128)(2,1)S(1)} %collective-permute-done.refs_1_), channel_id=1, source_target_pairs={{96,0},{97,1},{98,2},{99,3},{100,4},{101,5},{102,6},{103,7},{104,8... | collective-permute-start | bytes 3145736 | tf_op jit(solution)/shard_map/ppermute | solution.py:33
  65.6 1.2 copy-start
  82.1 25.3 %collective-permute-start.10 = (bf16[256,2048]{1,0:T(8,128)(2,1)}, bf16[256,2048]{1,0:T(8,128)(2,1)S(1)}, u32[]{:S(2)}, u32[]{:S(2)}) collective-permute-start(bf16[256,2048]{1,0:T(8,128)(2,1)} %collective-permute-done.6.refs_2_), channel_id=1, source_target_pairs={{24,0},{25,1},{26,2},{27,3},{28,4},{29,5},{30,6},{31,7},{0,8},{1,9... | collective-permute-start | bytes 3145736 | tf_op jit(solution)/shard_map/ppermute | solution.py:33
  82.6 26.0 %collective-permute-start.11 = (bf16[256,2048]{1,0:T(8,128)(2,1)}, bf16[256,2048]{1,0:T(8,128)(2,1)S(1)}, u32[]{:S(2)}, u32[]{:S(2)}) collective-permute-start(bf16[256,2048]{1,0:T(8,128)(2,1)} %collective-permute-done.2.refs_3_), channel_id=1, source_target_pairs={{32,0},{33,1},{34,2},{35,3},{36,4},{37,5},{38,6},{39,7},{40,8},{41... | collective-permute-start | bytes 3145736 | tf_op jit(solution)/shard_map/ppermute | solution.py:33
  86.8 24.8 %collective-permute-start.12 = (bf16[256,2048]{1,0:T(8,128)(2,1)}, bf16[256,2048]{1,0:T(8,128)(2,1)S(1)}, u32[]{:S(2)}, u32[]{:S(2)}) collective-permute-start(bf16[256,2048]{1,0:T(8,128)(2,1)} %collective-permute-done.8.refs_4_), channel_id=1, source_target_pairs={{96,0},{97,1},{98,2},{99,3},{100,4},{101,5},{102,6},{103,7},{104,8... | collective-permute-start | bytes 3145736 | tf_op jit(solution)/shard_map/ppermute | solution.py:33
  86.8 24.8 %collective-permute-start.9 = (bf16[256,2048]{1,0:T(8,128)(2,1)S(1)}, bf16[256,2048]{1,0:T(8,128)(2,1)S(1)}, u32[]{:S(2)}, u32[]{:S(2)}) collective-permute-start(bf16[256,2048]{1,0:T(8,128)(2,1)S(1)} %collective-permute-done.refs_1_), channel_id=1, source_target_pairs={{8,0},{9,1},{10,2},{11,3},{12,4},{13,5},{14,6},{15,7},{16,8},{17,9... | collective-permute-start | bytes 3145736 | tf_op jit(solution)/shard_map/ppermute | solution.py:33
  88.7 37.9 %collective-permute-start.14 = (bf16[256,2048]{1,0:T(8,128)(2,1)}, bf16[256,2048]{1,0:T(8,128)(2,1)S(1)}, u32[]{:S(2)}, u32[]{:S(2)}) collective-permute-start(bf16[256,2048]{1,0:T(8,128)(2,1)} %collective-permute-done.7.refs_3_), channel_id=1, source_target_pairs={{24,0},{25,1},{26,2},{27,3},{28,4},{29,5},{30,6},{31,7},{0,8},{1,9... | collective-permute-start | bytes 3145736 | tf_op jit(solution)/shard_map/ppermute | solution.py:33
  107.5 22.3 %collective-permute-start.15 = (bf16[256,2048]{1,0:T(8,128)(2,1)}, bf16[256,2048]{1,0:T(8,128)(2,1)S(1)}, u32[]{:S(2)}, u32[]{:S(2)}) collective-permute-start(bf16[256,2048]{1,0:T(8,128)(2,1)} %collective-permute-done.6.refs_2_), channel_id=1, source_target_pairs={{96,0},{97,1},{98,2},{99,3},{100,4},{101,5},{102,6},{103,7},{104,8... | collective-permute-start | bytes 3145736 | tf_op jit(solution)/shard_map/ppermute | solution.py:33
  111.6 21.6 %collective-permute-start.13 = (bf16[256,2048]{1,0:T(8,128)(2,1)S(1)}, bf16[256,2048]{1,0:T(8,128)(2,1)S(1)}, u32[]{:S(2)}, u32[]{:S(2)}) collective-permute-start(bf16[256,2048]{1,0:T(8,128)(2,1)S(1)} %collective-permute-done.12.refs_3_), channel_id=1, source_target_pairs={{8,0},{9,1},{10,2},{11,3},{12,4},{13,5},{14,6},{15,7},{16,8},{17,9... | collective-permute-start | bytes 3145736 | tf_op jit(solution)/shard_map/ppermute | solution.py:33
Sparse Core Ops, SparseCore 0:
  9.5 56.0 all-gather.2
